TPU v7x, 512 devices: a whole 4x8x8 slice. The times are simulated.
512 devices in a mesh: row: 16 (over x, y_hi), col: 32 (over z, y_lo, core).
Axes of the slice: x: 4, y: 8 (y_hi: 4, y_lo: 2; y = y_hi * 2 + y_lo), z: 8, core: 2. Of those that a mesh axis runs over, the one named last changes fastest.
Arguments:
- centers: float32 [3, 65536], P(None, 'row'), may hold values from -896 to 1920
- normals: float32 [3, 65536], P(None, 'row'), may hold values from -1 to 1, as said below
- areas: float32 [65536], P('row'), may hold values from 3 to 63
- onset: float32 [3, 32], replicated, may hold values from -1 to 1, as said below
- start: float32 [32, 65536], P(None, ('row', 'col')), may hold values from -3 to 3
Outputs:
- strengths: float32 [32, 65536], P(None, ('row', 'col'))
- pressure: float32 [32, 65536], P(None, ('row', 'col'))
Inputs may be any that keep to these rules, and one draw needn't show every extreme that they name: `normals`: each column has unit length. `onset`: each column has unit length.
All inputs are finite; a program needn't handle non-finite values.
Results may differ from a plain program's by a relative error of at most 0.0003.
Values may be sent and summed in bfloat16 or wider, within the bound.
No kernel may reach another device: no remote copies, remote signals or barrier semaphores. Data moves between devices by JAX's collectives and lax.ppermute only.
A program may use at most 64 MiB of HBM per device.

v0:
```python
import math

import jax
import jax.numpy as jnp
from jax import lax
from jax.sharding import PartitionSpec as P

PB = 32
SWEEPS = 2


INV_FOUR_PI = 1.0 / (4.0 * math.pi)
CAP = 0.4
OMEGA = 1.5
EPS = 1e-06


def from_root(block, axis, owner):
    block = jnp.where(lax.axis_index(axis) == owner, block, jnp.zeros_like(block))
    return lax.psum(block, axis)


def padded_2(block, sides, width):
    for axis, dim in sides:
        count = lax.axis_size(axis)
        forward = [(i, i + 1) for i in range(count - 1)]
        backward = [(target, source) for source, target in forward]
        low = lax.ppermute(
            lax.slice_in_dim(block, block.shape[dim] - width, None, axis=dim), axis, forward
        )
        high = lax.ppermute(lax.slice_in_dim(block, 0, width, axis=dim), axis, backward)
        block = jnp.concatenate([low, block, high], axis=dim)
    return block


def tile_block(source_geometry, target_centers, index):
    piece = lax.dynamic_slice_in_dim(source_geometry, index * 256, 256, 1)
    delta_x = target_centers[0][None, :] - piece[0][:, None]
    delta_y = target_centers[1][None, :] - piece[1][:, None]
    delta_z = target_centers[2][None, :] - piece[2][:, None]
    dist_sq = delta_x * delta_x + delta_y * delta_y + delta_z * delta_z + piece[6][:, None]
    inverse = lax.rsqrt(dist_sq)
    facing = piece[3][:, None] * delta_x + piece[4][:, None] * delta_y + piece[5][:, None] * delta_z
    value = (piece[6] * INV_FOUR_PI)[:, None] * facing * (inverse * inverse * inverse)
    return value.astype(jnp.bfloat16)


def make_product(source_geometry, target_centers, count):
    blocks = source_geometry.shape[1] // 256
    targets = target_centers.shape[1]
    stored = lax.map(
        lambda index: tile_block(source_geometry, target_centers, index),
        jnp.arange(blocks, dtype=jnp.int32),
    )

    def influence_product(moved):

        def add_block(index, acc):
            tile = stored[index]
            part = lax.dynamic_slice_in_dim(moved, index * 256, 256, 1)
            return acc + jnp.dot(part, tile, preferred_element_type=jnp.float32)

        return lax.fori_loop(0, blocks, add_block, jnp.zeros((count, targets), jnp.float32))

    return influence_product


def column_strengths(rowblock, root, offset, width):
    piece = lax.dynamic_slice_in_dim(rowblock, offset, width, 1)
    return from_root(piece, "row", root)


def surface_pressure(strengths, own_centers, onset, flat, all_lines):
    count = strengths.shape[0]
    lines = strengths.shape[1] // PB
    stacked = jnp.concatenate([strengths, own_centers], axis=0).reshape(count + 3, lines, PB)
    padded = padded_2(stacked, ((("row", "col"), 1),), 1)
    middle = padded[:, 1:-1]
    global_line = flat * lines + jnp.arange(lines, dtype=jnp.int32)
    at_first = (global_line == 0)[None, :, None]
    at_last = (global_line == all_lines - 1)[None, :, None]
    upper = jnp.where(at_last, middle, padded[:, 2:])
    lower = jnp.where(at_first, middle, padded[:, :-2])
    diff_a = upper - lower
    diff_b = jnp.roll(middle, -1, axis=2) - jnp.roll(middle, 1, axis=2)
    span_a = jnp.sqrt(jnp.sum(diff_a[count:] * diff_a[count:], axis=0))
    span_b = jnp.sqrt(jnp.sum(diff_b[count:] * diff_b[count:], axis=0))
    onset_a = jnp.sum(onset[:, :, None, None] * diff_a[count:][:, None], axis=0) / span_a
    onset_b = jnp.sum(onset[:, :, None, None] * diff_b[count:][:, None], axis=0) / span_b
    speed_a = onset_a - diff_a[:count] / span_a
    speed_b = onset_b - diff_b[:count] / span_b
    pressure = 1.0 - speed_a * speed_a - speed_b * speed_b
    return pressure.reshape(count, lines * PB)


def per_device(centers, normals, areas, onset, start):
    row_count = lax.axis_size("row")
    col_count = lax.axis_size("col")
    row_index = lax.axis_index("row")
    col_index = lax.axis_index("col")
    rows_here = centers.shape[1]
    own = start.shape[1]
    count = start.shape[0]
    own_first = col_index * own
    geometry = jnp.concatenate([centers, normals, areas[None, :]], axis=0)
    right_rows = -jnp.sum(onset[:, :, None] * normals[:, None, :], axis=0)
    own_areas = lax.dynamic_slice_in_dim(areas, own_first, own, 0)
    own_right = lax.dynamic_slice_in_dim(right_rows, own_first, own, 1)
    own_centers = lax.dynamic_slice_in_dim(centers, own_first, own, 1)
    width = rows_here * row_count // col_count
    root = col_index * width // rows_here
    offset = col_index * width % rows_here
    col_geometry = from_root(lax.dynamic_slice_in_dim(geometry, offset, width, 1), "row", root)
    influence_product = make_product(col_geometry, centers, count)
    state = start
    for sweep in range(SWEEPS):
        rowblock = lax.all_gather(state.astype(jnp.bfloat16), "col", axis=1, tiled=True)
        moved = column_strengths(rowblock, root, offset, width)
        product = lax.psum_scatter(influence_product(moved), "col", scatter_dimension=1, tiled=True)
        residual = own_right - 0.5 * state - product
        sums, total = lax.psum(
            (jnp.sum(own_areas[None, :] * residual * residual, axis=1), jnp.sum(own_areas)),
            ("row", "col"),
        )
        scale = jnp.minimum(1.0, CAP * jnp.sqrt(total) * lax.rsqrt(sums + EPS))
        state = state + OMEGA * scale[:, None] * residual
    flat = row_index * col_count + col_index
    all_lines = row_count * col_count * (own // PB)
    pressure = surface_pressure(state, own_centers, onset, flat, all_lines)
    return (state, pressure)


def solution(mesh):
    return jax.shard_map(
        per_device,
        mesh=mesh,
        in_specs=(P(None, "row"), P(None, "row"), P("row"), P(), P(None, ("row", "col"))),
        out_specs=(P(None, ("row", "col")), P(None, ("row", "col"))),
        check_vma=False,
    )
```

profile of v0, /device:TPU:6, one launch (start us, length us, event | category | flops | bytes accessed | tf_op | source)
XLA Modules:
  0.0 901.6 jit_solution(7518159152988218290)
XLA Ops:
  8.0 41.4 %all_gather.6 = bf16[32,4096]{1,0:T(8,128)(2,1)S(1)} all-gather(bf16[32,128]{1,0:T(8,128)(2,1)S(1)} %convert_element_type.16), channel_id=1, replica_groups=mesh['row'=16,'col'=32] {'col'}, dimensions={1}, use_global_device_ids=true | all-gather | bytes 270336 | tf_op jit(solution)/shard_map/all_gather | solution.py:117
  51.0 75.6 %psum.47 = f32[7,2048]{1,0:T(8,128)S(1)} all-reduce(f32[7,2048]{1,0:T(8,128)S(1)} %fusion.23), channel_id=1, replica_groups=mesh['row'=16,'col'=32] {'row'}, use_global_device_ids=true, to_apply=%region_3.4 | all-reduce | flops 14336 | bytes 114688 | tf_op jit(solution)/shard_map/psum | solution.py:20
  126.6 52.7 %while.38 = (s32[]{:T(128)}, bf16[8,256,4096]{2,1,0:T(8,128)(2,1)}, s32[8]{0:T(128)S(1)}, f32[7,2048]{1,0:T(8,128)S(1)}, f32[3,4096]{1,0:T(4,128)}, /*index=5*/s...) while((s32[]{:T(128)}, bf16[8,256,4096]{2,1,0:T(8,128)(2,1)}, ...), condition=%wide.region_5.6_spmd, body=%wide.region_4.5_spmd.sunk | while | flops 19923212 | bytes 2269995 | solution.py:51
  128.9 4.3 fusion.52
  135.6 4.2 fusion.52
  142.2 4.3 fusion.52
  148.8 4.2 fusion.52
  155.3 4.2 fusion.52
  161.9 4.2 fusion.52
  168.5 4.2 fusion.52
  175.0 4.2 fusion.52
  179.3 32.2 %all-reduce.4.cloned.1.call-done = bf16[32,2048]{1,0:T(8,128)(2,1)} async-done(((bf16[32,2048]{1,0:T(8,128)(2,1)}), bf16[32,2048]{1,0:T(8,128)(2,1)}) %all-reduce.4.cloned.1.call-update) | async-done | bytes 131088 | tf_op jit(solution)/shard_map/psum | solution.py:20
  211.5 17.0 %while.39 = (s32[]{:T(128)}, f32[32,4096]{1,0:T(8,128)S(1)}, bf16[32,2048]{1,0:T(8,128)(2,1)}, bf16[8,256,4096]{2,1,0:T(8,128)(2,1)}, s32[]{:T(128)}, /*index=5*/s32[]{:T(128)}, s32[]{:T(128)}, s32[]{:T(128)}) while((s32[]{:T(128)}, f32[32,4096]{1,0:T(8,128)S(1)}, bf16[32,2048]{1,0:T(8,128)(2,1)}, bf16[8,256,4096]{2,1,0:T(8,128)(2,1)}, ...), condition=%wide.region_8.9_spmd.clone, body=%wide.region_7.8_spmd.clone.sunk | while | flops 67371016 | bytes 3162769 | solution.py:63
  211.5 2.1 convolution_add_fusion.4
  213.7 2.1 convolution_add_fusion.4
  217.9 2.1 convolution_add_fusion.4
  220.1 2.1 convolution_add_fusion.4
  222.2 2.1 convolution_add_fusion.4
  226.4 2.1 convolution_add_fusion.4
  231.0 119.2 %reduce-scatter.3.cloned.1.call-done = f32[32,128]{1,0:T(8,128)} async-done(((f32[32,4096]{1,0:T(8,128)}), f32[32,128]{1,0:T(8,128)}) %reduce-scatter.3.cloned.1.call-update) | async-done | bytes 16400 | tf_op jit(solution)/shard_map/reduce_scatter | solution.py:119
  351.0 95.2 %all-reduce = (f32[32]{0:T(128)S(1)}, f32[]{:T(128)}) all-reduce(f32[32]{0:T(128)S(1)} %fusion.32, f32[]{:T(128)} %get-tuple-element.254), channel_id=1, replica_groups=mesh['row'=16,'col'=32] {'row','col'}, use_global_device_ids=true, to_apply=%region_11.12 | all-reduce | flops 33 | bytes 264 | tf_op jit(solution)/shard_map/psum | solution.py:121
  447.7 33.2 %all_gather.7 = bf16[32,4096]{1,0:T(8,128)(2,1)S(1)} all-gather(bf16[32,128]{1,0:T(8,128)(2,1)S(1)} %get-tuple-element.252), channel_id=1, replica_groups=mesh['row'=16,'col'=32] {'col'}, dimensions={1}, use_global_device_ids=true | all-gather | bytes 270336 | tf_op jit(solution)/shard_map/all_gather | solution.py:117
  481.7 163.6 %all-reduce.6.cloned.1.call-done = bf16[32,2048]{1,0:T(8,128)(2,1)} async-done(((bf16[32,2048]{1,0:T(8,128)(2,1)}), bf16[32,2048]{1,0:T(8,128)(2,1)}) %all-reduce.6.cloned.1.call-update) | async-done | bytes 131088 | tf_op jit(solution)/shard_map/psum | solution.py:20
  645.3 17.0 %while.40 = (s32[]{:T(128)}, f32[32,4096]{1,0:T(8,128)S(1)}, bf16[32,2048]{1,0:T(8,128)(2,1)}, bf16[8,256,4096]{2,1,0:T(8,128)(2,1)}, s32[]{:T(128)}, /*index=5*/s32[]{:T(128)}, s32[]{:T(128)}, s32[]{:T(128)}) while((s32[]{:T(128)}, f32[32,4096]{1,0:T(8,128)S(1)}, bf16[32,2048]{1,0:T(8,128)(2,1)}, ...), condition=%wide.region_14.15_spmd.clone, body=%wide.region_13.14_spmd.clone.sunk | while | flops 67371016 | bytes 3162769 | solution.py:63
  647.4 2.1 convolution_add_fusion.5
  653.8 2.1 convolution_add_fusion.5
  658.0 2.1 convolution_add_fusion.5
  660.1 2.1 convolution_add_fusion.5
  663.8 120.0 %reduce-scatter.5.cloned.1.call-done = f32[32,128]{1,0:T(8,128)} async-done(((f32[32,4096]{1,0:T(8,128)}), f32[32,128]{1,0:T(8,128)}) %reduce-scatter.5.cloned.1.call-update) | async-done | bytes 16400 | tf_op jit(solution)/shard_map/reduce_scatter | solution.py:119
  784.6 95.5 %psum.50 = f32[32]{0:T(128)S(1)} all-reduce(f32[32]{0:T(128)S(1)} %fusion.33), channel_id=1, replica_groups=mesh['row'=16,'col'=32] {'row','col'}, use_global_device_ids=true, to_apply=%region_17.18 | all-reduce | flops 32 | bytes 256 | tf_op jit(solution)/shard_map/psum | solution.py:121
  881.3 3.4 collective-permute-start
  886.7 7.3 collective-permute-done.1
  (95 shorter events, 39.7 us)
Async XLA Ops:
  7.2 204.4 %all-reduce.4.cloned.1.call-start = ((), (), s32[]{:S(2)}) async-start(), calls=%async_computation.2 | async-start | bytes 262144 | tf_op jit(solution)/shard_map/psum | solution.py:20
  50.1 300.0 %reduce-scatter.3.cloned.1.call-start = ((), (), s32[]{:S(2)}) async-start(), calls=%async_computation.3 | async-start | bytes 540672 | tf_op jit(solution)/shard_map/reduce_scatter | solution.py:119
  211.5 19.3 %copy-start.2 = (f32[3,4096]{1,0:T(4,128)S(1)}, f32[3,4096]{1,0:T(4,128)}, u32[]{:S(2)}) copy-start(f32[3,4096]{1,0:T(4,128)} %param.12) | copy-start | bytes 147460
  211.5 19.3 %copy-start.5 = (f32[3,32]{1,0:T(4,128)S(1)}, f32[3,32]{1,0:T(4,128)}, u32[]{:S(2)}) copy-start(f32[3,32]{1,0:T(4,128)} %param.14) | copy-start | bytes 1156
  211.5 138.6 %copy-start.3 = (f32[32,128]{1,0:T(8,128)S(1)}, f32[32,128]{1,0:T(8,128)}, u32[]{:S(2)}) copy-start(f32[32,128]{1,0:T(8,128)} %param.15) | copy-start | bytes 49156
  228.5 0.8 copy-start
  229.4 415.9 %all-reduce.6.cloned.1.call-start = ((), (), s32[]{:S(2)}) async-start(), calls=%async_computation.4 | async-start | bytes 262144 | tf_op jit(solution)/shard_map/psum | solution.py:20
  481.7 302.1 %reduce-scatter.5.cloned.1.call-start = ((), (), s32[]{:S(2)}) async-start(), calls=%async_computation.5 | async-start | bytes 540672 | tf_op jit(solution)/shard_map/reduce_scatter | solution.py:119
  662.3 0.8 copy-start.1
  880.9 14.1 %copy-start.4 = (f32[32,128]{1,0:T(8,128)}, f32[32,128]{1,0:T(8,128)S(1)}, u32[]{:S(2)}) copy-start(f32[32,128]{1,0:T(8,128)S(1)} %multiply_add_fusion) | copy-start | bytes 49156
  881.3 5.4 collective-permute-start
  884.6 9.3 %collective-permute-start.1 = (f32[35,1,32]{2,0,1:T(8,128)S(1)}, f32[35,1,32]{2,0,1:T(8,128)S(1)}, u32[]{:S(2)}, u32[]{:S(2)}) collective-permute-start(f32[35,1,32]{2,0,1:T(8,128)S(1)} %get-tuple-element.269), channel_id=1, source_target_pairs={{0,1},{1,2},{2,3},{3,4},{4,5},{5,6},{6,7},{7,8},{8,9},{9,10},{10,1... | collective-permute-start | bytes 13448 | tf_op jit(solution)/shard_map/ppermute | solution.py:28
Sparse Core Ops, SparseCore 0:
  50.2 161.2 all-reduce.3
  229.5 120.6 reduce-scatter.2
  481.8 163.4 all-reduce.5
  663.2 120.5 reduce-scatter.4
where the time goes:
time: 905 us; the launch traced here: 902 us
  waiting for transfers between devices  442 us (49%)
  blocking collectives  341 us (38%)
  other arithmetic  42.2 us (5%)
  matrix products  33.5 us (4%)
  local copies, waits for them, and re-layouts  16.7 us (2%)
  between operations  14.7 us (2%)
    reduce_scatter x2, waiting for transfers between devices, per_device(): lax.psum_scatter(influence_product(moved), 'col', scatter_dimension=1, ti...  239 us
    psum x2, waiting for transfers between devices, from_root(): return lax.psum(block, axis)  196 us
    psum x2, blocking collectives, per_device(): lax.psum((jnp.sum(own_areas[None, :] * residual * residual, axis=1), jnp....  191 us
    psum x1, blocking collectives, from_root(): return lax.psum(block, axis)  75.6 us
    all_gather x2, blocking collectives, per_device(): lax.all_gather(state.astype(jnp.bfloat16), 'col', axis=1, tiled=True)  74.7 us
    dynamic_update_slice x8, other arithmetic, make_product(): lax.map(lambda index: tile_block(source_geometry, target_centers, index),...  33.9 us
    dot_general x16, matrix products, add_block(): return acc + jnp.dot(part, tile, preferred_element_type=jnp.float32)  33.5 us
  transfers between devices with their start and end apart: 6, of which 5 were waited for; matrix products, arithmetic and copies ran while one was open for 6% of the time, Pallas kernels for 0%

commit v1 on v0

v1 whole, which is shorter than its diff:
```python
import math

import jax
import jax.numpy as jnp
from jax import lax
from jax.experimental import pallas as pl
from jax.experimental.pallas import tpu as pltpu
from jax.sharding import PartitionSpec as P

PB = 32
SWEEPS = 2


INV_FOUR_PI = 1.0 / (4.0 * math.pi)
CAP = 0.4
OMEGA = 1.5
EPS = 1e-06
LANES = 128
STEP = 256


def spread(block, axis, count):
    copies = jnp.broadcast_to(block[None], (count,) + block.shape)
    return lax.all_to_all(copies, axis, 0, 0, tiled=True)


def build_kernel(source_ref, target_ref, moved_ref, tile_ref, product_ref, wide_ref):
    step = pl.program_id(0)
    targets = target_ref.shape[1]

    for row in range(7):
        column = source_ref[:, row : row + 1]
        wide_ref[row] = jnp.broadcast_to(column, (STEP, LANES))

    def rows(index, carry):
        at = pl.ds(pl.multiple_of(index * 16, 16), 16)
        src_x, src_y, src_z = wide_ref[0, at, :], wide_ref[1, at, :], wide_ref[2, at, :]
        nor_x, nor_y, nor_z = wide_ref[3, at, :], wide_ref[4, at, :], wide_ref[5, at, :]
        area = wide_ref[6, at, :]
        for lane in range(0, targets, LANES):
            here = slice(lane, lane + LANES)
            delta_x = target_ref[0:1, here] - src_x
            delta_y = target_ref[1:2, here] - src_y
            delta_z = target_ref[2:3, here] - src_z
            dist_sq = delta_x * delta_x + delta_y * delta_y + delta_z * delta_z + area
            inverse = lax.rsqrt(dist_sq)
            facing = nor_x * delta_x + nor_y * delta_y + nor_z * delta_z
            value = facing * (inverse * inverse * inverse)
            tile_ref[at, here] = value.astype(jnp.bfloat16)
        return carry

    lax.fori_loop(0, STEP // 16, rows, 0)

    part = jnp.concatenate([moved_ref[i] for i in range(STEP // LANES)], axis=1)
    product = jnp.dot(part, tile_ref[...], preferred_element_type=jnp.float32)

    @pl.when(step == 0)
    def _():
        for chunk in range(targets // LANES):
            product_ref[chunk] = product[:, chunk * LANES : (chunk + 1) * LANES]

    @pl.when(step > 0)
    def _():
        for chunk in range(targets // LANES):
            product_ref[chunk] += product[:, chunk * LANES : (chunk + 1) * LANES]


def build(sources, targets, moved):
    count = sources.shape[0]
    width = targets.shape[1]
    blocks, onsets, _ = moved.shape
    return pl.pallas_call(
        build_kernel,
        grid=(count // STEP,),
        in_specs=[
            pl.BlockSpec((STEP, 8), lambda i: (i, 0)),
            pl.BlockSpec((8, width), lambda i: (0, 0)),
            pl.BlockSpec((STEP // LANES, onsets, LANES), lambda i: (i, 0, 0)),
        ],
        out_specs=[
            pl.BlockSpec((STEP, width), lambda i: (i, 0)),
            pl.BlockSpec((width // LANES, onsets, LANES), lambda i: (0, 0, 0)),
        ],
        out_shape=[
            jax.ShapeDtypeStruct((count, width), jnp.bfloat16),
            jax.ShapeDtypeStruct((width // LANES, onsets, LANES), jnp.float32),
        ],
        scratch_shapes=[pltpu.VMEM((7, STEP, LANES), jnp.float32)],
        compiler_params=pltpu.CompilerParams(vmem_limit_bytes=40 << 20),
        name="build",
    )(sources, targets, moved)


def apply_kernel(moved_ref, tile_ref, product_ref):
    step = pl.program_id(0)
    targets = tile_ref.shape[1]
    blocks = tile_ref.shape[0] // LANES
    part = jnp.concatenate([moved_ref[i] for i in range(blocks)], axis=1)
    product = jnp.dot(part, tile_ref[...], preferred_element_type=jnp.float32)

    @pl.when(step == 0)
    def _():
        for chunk in range(targets // LANES):
            product_ref[chunk] = product[:, chunk * LANES : (chunk + 1) * LANES]

    @pl.when(step > 0)
    def _():
        for chunk in range(targets // LANES):
            product_ref[chunk] += product[:, chunk * LANES : (chunk + 1) * LANES]


def apply(tile, moved, depth=512):
    count, width = tile.shape
    blocks, onsets, _ = moved.shape
    return pl.pallas_call(
        apply_kernel,
        grid=(count // depth,),
        in_specs=[
            pl.BlockSpec((depth // LANES, onsets, LANES), lambda i: (i, 0, 0)),
            pl.BlockSpec((depth, width), lambda i: (i, 0)),
        ],
        out_specs=pl.BlockSpec((width // LANES, onsets, LANES), lambda i: (0, 0, 0)),
        out_shape=jax.ShapeDtypeStruct((width // LANES, onsets, LANES), jnp.float32),
        compiler_params=pltpu.CompilerParams(vmem_limit_bytes=40 << 20),
        name="apply",
    )(moved, tile)


def in_three(value):
    high = lax.reduce_precision(value, 8, 7)
    rest = value - high
    middle = lax.reduce_precision(rest, 8, 7)
    return high, middle, rest - middle


def per_device(centers, normals, areas, onset, start):
    row_count = lax.axis_size("row")
    col_count = lax.axis_size("col")
    row_index = lax.axis_index("row")
    col_index = lax.axis_index("col")
    own = start.shape[1]
    count = start.shape[0]
    own_first = col_index * own
    own_areas = lax.dynamic_slice_in_dim(areas, own_first, own, 0)
    own_normals = lax.dynamic_slice_in_dim(normals, own_first, own, 1)
    own_centers = lax.dynamic_slice_in_dim(centers, own_first, own, 1)

    block_area = jnp.broadcast_to(jnp.sum(areas), (1, own))
    note = jnp.concatenate([own_centers, block_area, jnp.zeros((4, own), jnp.float32)], axis=0)
    notes = spread(note, "row", row_count)
    targets = jnp.transpose(notes, (1, 0, 2)).reshape(8, row_count * own)
    total = jnp.sum(notes[:, 3, 0])
    moved = spread(start.astype(jnp.bfloat16), "col", col_count)

    sources = jnp.concatenate(
        [centers, normals * (areas * INV_FOUR_PI)[None, :], areas[None, :], areas[None, :]], axis=0
    ).T
    tile, partial = build(sources, targets, moved)

    product = jnp.sum(lax.all_to_all(partial, "row", 0, 0, tiled=True), axis=0)
    right = -jnp.sum(onset[:, :, None] * own_normals[:, None, :], axis=0)
    residual = right - 0.5 * start - product
    part = jnp.sum(own_areas[None, :] * residual * residual, axis=1)
    high, middle, low = in_three(part)
    line = jnp.concatenate([high, middle, low, jnp.zeros_like(low)])[None, :]
    line = jnp.concatenate([line, jnp.zeros((15, own), jnp.float32)], axis=0)
    sent = jnp.concatenate([residual, line], axis=0).astype(jnp.bfloat16)
    gathered = spread(sent, "col", col_count)
    parts = jnp.sum(gathered[:, count, :].astype(jnp.float32), axis=0)
    block_sum = parts[:count] + (parts[count : 2 * count] + parts[2 * count : 3 * count])
    partial = apply(tile, gathered[:, :count, :])
    extra = jnp.broadcast_to(jnp.pad(block_sum, (0, own - count))[None, None], (row_count, 8, own))
    swapped = jnp.sum(
        lax.all_to_all(jnp.concatenate([partial, extra], axis=1), "row", 0, 0, tiled=True), axis=0
    )
    change = swapped[:count]
    sums = swapped[count, :count]
    weight = OMEGA * jnp.minimum(1.0, CAP * jnp.sqrt(total) * lax.rsqrt(sums + EPS))[:, None]
    state = start + weight * residual
    product = product + weight * change
    residual = right - 0.5 * state - product

    flat = row_index * col_count + col_index
    devices = row_count * col_count
    edges = jnp.concatenate([state, residual, own_centers], axis=0)
    forward = [(i, i + 1) for i in range(devices - 1)]
    backward = [(i + 1, i) for i in range(devices - 1)]
    before = lax.ppermute(edges[:, own - PB :], ("row", "col"), forward)
    after = lax.ppermute(edges[:, :PB], ("row", "col"), backward)

    part = jnp.sum(own_areas[None, :] * residual * residual, axis=1)
    part = jnp.broadcast_to(jnp.pad(part, (0, own - count))[None], (8, own))
    part = jnp.sum(spread(part, "col", col_count), axis=0)
    sums = jnp.sum(spread(part, "row", row_count), axis=0)[0, :count]
    weight = OMEGA * jnp.minimum(1.0, CAP * jnp.sqrt(total) * lax.rsqrt(sums + EPS))[:, None]

    def finish(edge):
        return jnp.concatenate(
            [edge[:count] + weight * edge[count : 2 * count], edge[2 * count :]], axis=0
        )

    fields = finish(edges)
    state = fields[:count]
    before = jnp.where(flat == 0, fields[:, :PB], finish(before))
    after = jnp.where(flat == devices - 1, fields[:, own - PB :], finish(after))
    padded = jnp.concatenate([before, fields, after], axis=1)
    diff_a = padded[:, 2 * PB :] - padded[:, : own]
    lane = lax.broadcasted_iota(jnp.int32, fields.shape, 1) % PB
    following = jnp.where(lane == PB - 1, jnp.roll(fields, PB - 1, 1), jnp.roll(fields, -1, 1))
    preceding = jnp.where(lane == 0, jnp.roll(fields, 1 - PB, 1), jnp.roll(fields, 1, 1))
    diff_b = following - preceding
    speeds = []
    for diff in (diff_a, diff_b):
        step = diff[count:]
        span = jnp.sqrt(jnp.sum(step * step, axis=0))
        along = jnp.sum(onset[:, :, None] * step[:, None, :], axis=0)
        speeds.append(along / span - diff[:count] / span)
    pressure = 1.0 - speeds[0] * speeds[0] - speeds[1] * speeds[1]
    return (state, pressure)


def solution(mesh):
    return jax.shard_map(
        per_device,
        mesh=mesh,
        in_specs=(P(None, "row"), P(None, "row"), P("row"), P(), P(None, ("row", "col"))),
        out_specs=(P(None, ("row", "col")), P(None, ("row", "col"))),
        check_vma=False,
    )
```

time: 905 us -> 183 us (0.20)
  waiting for transfers between devices: 442 us -> 54.2 us
  blocking collectives: 341 us -> 18.4 us
  Pallas kernels: 0 us -> 44.1 us
  starting transfers between devices: 5.46 us -> 48.5 us
  matrix products: 33.5 us -> 0 us
  other arithmetic: 42.2 us -> 9.01 us
  between operations: 14.7 us -> 1.55 us
  local copies, waits for them, and re-layouts: 16.7 us -> 6.43 us
    psum x3 -> x0, blocking collectives: 266 us -> none  [the longest x2 191 us: per_device(): lax.psum((jnp.sum(own_areas[None, :] * residual * residual, axis=1), jnp....]
    reduce_scatter x2 -> x0, waiting for transfers between devices: 239 us -> none  [per_device(): lax.psum_scatter(influence_product(moved), 'col', scatter_dimension=1, ti...]
    psum x2 -> x0, waiting for transfers between devices: 196 us -> none  [from_root(): return lax.psum(block, axis)]
    all_gather x2 -> x0, blocking collectives: 74.7 us -> none  [per_device(): lax.all_gather(state.astype(jnp.bfloat16), 'col', axis=1, tiled=True)]
    all_to_all x0 -> x6, waiting for transfers between devices: none -> 46.6 us  [the longest x4 26.7 us: spread(): return lax.all_to_all(copies, axis, 0, 0, tiled=True)]
    pallas_call x0 -> x2, Pallas kernels: none -> 44.1 us  [the longest x1 34.6 us: build(): pl.pallas_call(build_kernel, grid=(count // STEP,), in_specs=[pl.BlockSpe...]
    all_to_all x0 -> x6, starting transfers between devices: none -> 42 us  [the longest x4 30.5 us: spread(): return lax.all_to_all(copies, axis, 0, 0, tiled=True)]
    dynamic_update_slice x8 -> x0, other arithmetic: 33.9 us -> none  [make_product(): lax.map(lambda index: tile_block(source_geometry, target_centers, index),...]
  transfers between devices with their start and end apart: 6 -> 8, of which waited for: 5 -> 6; matrix products, arithmetic and copies ran while one was open for 6% -> 3% of each run, Pallas kernels for 0% -> 0%
where the time goes in v1:
time: 183 us; the launch traced here: 182 us
  waiting for transfers between devices  54.2 us (30%)
  starting transfers between devices  48.5 us (27%)
  Pallas kernels  44.1 us (24%)
  blocking collectives  18.4 us (10%)
  other arithmetic  9.01 us (5%)
  local copies, waits for them, and re-layouts  6.43 us (4%)
    pallas_call x1, Pallas kernels, build(): pl.pallas_call(build_kernel, grid=(count // STEP,), in_specs=[pl.BlockSpe...  34.6 us
    all_to_all x4, starting transfers between devices, spread(): return lax.all_to_all(copies, axis, 0, 0, tiled=True)  30.5 us
    all_to_all x4, waiting for transfers between devices, spread(): return lax.all_to_all(copies, axis, 0, 0, tiled=True)  26.7 us
    all_to_all x1, blocking collectives, spread(): return lax.all_to_all(copies, axis, 0, 0, tiled=True)  18.4 us
    all_to_all x1, waiting for transfers between devices, per_device(): lax.all_to_all(jnp.concatenate([partial, extra], axis=1), 'row', 0, 0, ti...  11 us
    pallas_call x1, Pallas kernels, apply(): pl.pallas_call(apply_kernel, grid=(count // depth,), in_specs=[pl.BlockSp...  9.47 us
    all_to_all x1, waiting for transfers between devices, per_device(): product = jnp.sum(lax.all_to_all(partial, 'row', 0, 0, tiled=True), axis=0)  8.98 us
    ppermute x1, waiting for transfers between devices, per_device(): before = lax.ppermute(edges[:, own - PB:], ('row', 'col'), forward)  7.53 us
  transfers between devices with their start and end apart: 8, of which 6 were waited for; matrix products, arithmetic and copies ran while one was open for 3% of the time, Pallas kernels for 0%

profile of v1, /device:TPU:6, one launch (start us, length us, event | category | flops | bytes accessed | tf_op | source)
XLA Modules:
  0.0 182.1 jit_solution(12943854011065976275)
XLA Ops:
  0.7 1.3 fusion.38
  2.0 0.7 pad.46.clone
  2.8 0.7 constant_dynamic-slice_fusion.1
  4.2 10.1 %all-to-all-start = ((f32[16,8,128]{2,1,0:T(8,128)}), f32[16,8,128]{2,1,0:T(8,128)S(1)}, u32[]{:S(2)}, u32[]{:S(2)}) async-start(f32[16,8,128]{2,1,0:T(8,128)} %broadcast_in_dim.22), calls=%async_computation | async-start | bytes 131072 | tf_op jit(solution)/shard_map/all_to_all | solution.py:24
  14.2 0.7 convert_element_type.15
  14.9 7.3 %all-to-all-done = f32[16,8,128]{2,1,0:T(8,128)S(1)} async-done(((f32[16,8,128]{2,1,0:T(8,128)}), f32[16,8,128]{2,1,0:T(8,128)S(1)}, u32[]{:S(2)}, u32[]{:S(2)}) %all-to-all-start) | async-done | bytes 65568 | tf_op jit(solution)/shard_map/all_to_all | solution.py:24
  22.3 0.7 broadcast_in_dim.24
  23.0 10.8 %all-to-all-start.1 = ((bf16[32,32,128]{2,1,0:T(8,128)(2,1)}), bf16[32,32,128]{2,1,0:T(8,128)(2,1)S(1)}, u32[]{:S(2)}, u32[]{:S(2)}) async-start(bf16[32,32,128]{2,1,0:T(8,128)(2,1)} %broadcast_in_dim.24), calls=%async_computation.1 | async-start | bytes 524288 | tf_op jit(solution)/shard_map/all_to_all | solution.py:24
  33.8 0.9 broadcast_multiply_fusion
  34.7 0.9 pad_maximum_fusion.1
  36.3 9.8 %all-to-all-done.1.moved_ref = bf16[32,32,128]{2,1,0:T(8,128)(2,1)S(1)} async-done(((bf16[32,32,128]{2,1,0:T(8,128)(2,1)}), bf16[32,32,128]{2,1,0:T(8,128)(2,1)S(1)}, u32[]{:S(2)}, u32[]{:S(2)}) %all-to-all-start.1) | async-done | bytes 262176 | tf_op jit(solution)/shard_map/all_to_all | solution.py:24
  46.1 34.6 %build.1 = (bf16[4096,2048]{1,0:T(8,128)(2,1)}, f32[16,32,128]{2,1,0:T(8,128)}) custom-call(f32[4096,8]{1,0:T(8,128)S(1)} %bitcast.12, f32[8,2048]{1,0:T(8,128)S(1)} %bitcast.13, bf16[32,32,128]{2,1,0:T(8,128)(2,1)S(1)} %all-to-all-done.1.moved_ref), custom_call_target="tpu_custom_call" | custom-call | tf_op jit(solution)/shard_map/build/pallas_call | solution.py:72
  80.7 5.7 %all-to-all-start.2 = ((f32[16,32,128]{2,1,0:T(8,128)}), f32[16,32,128]{2,1,0:T(8,128)S(1)}, u32[]{:S(2)}, u32[]{:S(2)}) async-start(f32[16,32,128]{2,1,0:T(8,128)} %get-tuple-element.4), calls=%async_computation.2 | async-start | bytes 524288 | tf_op jit(solution)/shard_map/all_to_all | solution.py:160
  86.3 0.8 dynamic_slice.11
  87.2 0.7 constant_dynamic-slice_fusion
  87.9 0.8 multiply_reduce_fusion.2
  88.6 9.0 %all-to-all-done.2 = f32[16,32,128]{2,1,0:T(8,128)S(1)} async-done(((f32[16,32,128]{2,1,0:T(8,128)}), f32[16,32,128]{2,1,0:T(8,128)S(1)}, u32[]{:S(2)}, u32[]{:S(2)}) %all-to-all-start.2) | async-done | bytes 262176 | tf_op jit(solution)/shard_map/all_to_all | solution.py:160
  97.6 0.7 fusion.36
  98.7 18.4 %all_to_all.35 = bf16[32,48,128]{2,1,0:T(8,128)(2,1)S(1)} all-to-all(bf16[32,48,128]{2,1,0:T(8,128)(2,1)S(1)} %broadcast_in_dim.27), channel_id=1, replica_groups=mesh['row'=16,'col'=32] {'col'}, dimensions={0} | all-to-all | bytes 786432 | tf_op jit(solution)/shard_map/all_to_all | solution.py:24
  117.3 9.5 %apply.1 = f32[16,32,128]{2,1,0:T(8,128)S(1)} custom-call(bf16[32,32,128]{2,1,0:T(8,128)(2,1)S(1)} %slice.143.moved_ref, bf16[4096,2048]{1,0:T(8,128)(2,1)} %get-tuple-element.5.tile_ref), custom_call_target="tpu_custom_call" | custom-call | tf_op jit(solution)/shard_map/apply/pallas_call | solution.py:115
  126.8 0.7 pad_maximum_fusion
  127.5 5.8 %all-to-all-start.4 = ((f32[16,40,128]{2,1,0:T(8,128)}), f32[16,40,128]{2,1,0:T(8,128)S(1)}, u32[]{:S(2)}, u32[]{:S(2)}) async-start(f32[16,40,128]{2,1,0:T(8,128)} %pad_maximum_fusion), calls=%async_computation.4 | async-start | bytes 655360 | tf_op jit(solution)/shard_map/all_to_all | solution.py:174
  134.6 11.0 %all-to-all-done.4 = f32[16,40,128]{2,1,0:T(8,128)S(1)} async-done(((f32[16,40,128]{2,1,0:T(8,128)}), f32[16,40,128]{2,1,0:T(8,128)S(1)}, u32[]{:S(2)}, u32[]{:S(2)}) %all-to-all-start.4) | async-done | bytes 327712 | tf_op jit(solution)/shard_map/all_to_all | solution.py:174
  145.9 0.7 broadcast_in_dim_broadcast_in_dim_broadcast_in_dim.2
  146.5 3.9 %all-to-all-start.5 = ((f32[32,8,128]{2,1,0:T(8,128)}), f32[32,8,128]{2,1,0:T(8,128)S(1)}, u32[]{:S(2)}, u32[]{:S(2)}) async-start(f32[32,8,128]{2,1,0:T(8,128)} %broadcast_in_dim_broadcast_in_dim_broadcast_in_dim.2), calls=%async_computation.5 | async-start | bytes 262144 | tf_op jit(solution)/shard_map/all_to_all | solution.py:24
  150.4 9.5 %all-to-all-done.5 = f32[32,8,128]{2,1,0:T(8,128)S(1)} async-done(((f32[32,8,128]{2,1,0:T(8,128)}), f32[32,8,128]{2,1,0:T(8,128)S(1)}, u32[]{:S(2)}, u32[]{:S(2)}) %all-to-all-start.5) | async-done | bytes 131104 | tf_op jit(solution)/shard_map/all_to_all | solution.py:24
  160.0 0.6 broadcast_in_dim.29
  160.6 5.8 %all-to-all-start.6 = ((f32[16,8,128]{2,1,0:T(8,128)}), f32[16,8,128]{2,1,0:T(8,128)S(1)}, u32[]{:S(2)}, u32[]{:S(2)}) async-start(f32[16,8,128]{2,1,0:T(8,128)} %broadcast_in_dim.29), calls=%async_computation.6 | async-start | bytes 131072 | tf_op jit(solution)/shard_map/all_to_all | solution.py:24
  166.4 4.6 %collective-permute-start = (f32[67,32]{1,0:T(8,128)S(1)}, f32[67,32]{1,0:T(8,128)S(1)}, u32[]{:S(2)}, u32[]{:S(2)}) collective-permute-start(f32[67,32]{1,0:T(8,128)S(1)} %get-tuple-element.16), channel_id=1, source_target_pairs={{1,0},{2,1},{3,2},{4,3},{5,4},{6,5},{7,6},{8,7},{9,8},{10,9},{11,1... | collective-permute-start | bytes 25736 | tf_op jit(solution)/shard_map/ppermute | solution.py:189
  171.0 1.9 %collective-permute-start.1 = (f32[67,32]{1,0:T(8,128)S(1)}, f32[67,32]{1,0:T(8,128)S(1)}, u32[]{:S(2)}, u32[]{:S(2)}) collective-permute-start(f32[67,32]{1,0:T(8,128)S(1)} %get-tuple-element.15), channel_id=1, source_target_pairs={{0,1},{1,2},{2,3},{3,4},{4,5},{5,6},{6,7},{7,8},{8,9},{9,10},{10,1... | collective-permute-start | bytes 25736 | tf_op jit(solution)/shard_map/ppermute | solution.py:188
  173.0 7.5 %collective-permute-done.1 = f32[67,32]{1,0:T(8,128)S(1)} collective-permute-done((f32[67,32]{1,0:T(8,128)S(1)}, f32[67,32]{1,0:T(8,128)S(1)}, u32[]{:S(2)}, u32[]{:S(2)}) %collective-permute-start.1) | collective-permute-done | bytes 8608 | tf_op jit(solution)/shard_map/ppermute | solution.py:188
  181.4 0.7 fusion.18
  (54 shorter events, 3.8 us)
Async XLA Ops:
  0.6 145.0 %copy-start.1 = (f32[32,128]{1,0:T(8,128)S(1)}, f32[32,128]{1,0:T(8,128)}, u32[]{:S(2)}) copy-start(f32[32,128]{1,0:T(8,128)} %param.9) | copy-start | bytes 49156
  0.6 180.7 %copy-start.2 = (f32[3,32]{1,0:T(4,128)S(1)}, f32[3,32]{1,0:T(4,128)}, u32[]{:S(2)}) copy-start(f32[3,32]{1,0:T(4,128)} %param.8) | copy-start | bytes 1156
  4.2 18.1 %all-to-all-start = ((f32[16,8,128]{2,1,0:T(8,128)}), f32[16,8,128]{2,1,0:T(8,128)S(1)}, u32[]{:S(2)}, u32[]{:S(2)}) async-start(f32[16,8,128]{2,1,0:T(8,128)} %broadcast_in_dim.22), calls=%async_computation | async-start | bytes 131072 | tf_op jit(solution)/shard_map/all_to_all | solution.py:24
  23.0 23.1 %all-to-all-start.1 = ((bf16[32,32,128]{2,1,0:T(8,128)(2,1)}), bf16[32,32,128]{2,1,0:T(8,128)(2,1)S(1)}, u32[]{:S(2)}, u32[]{:S(2)}) async-start(bf16[32,32,128]{2,1,0:T(8,128)(2,1)} %broadcast_in_dim.24), calls=%async_computation.1 | async-start | bytes 524288 | tf_op jit(solution)/shard_map/all_to_all | solution.py:24
  80.7 16.9 %all-to-all-start.2 = ((f32[16,32,128]{2,1,0:T(8,128)}), f32[16,32,128]{2,1,0:T(8,128)S(1)}, u32[]{:S(2)}, u32[]{:S(2)}) async-start(f32[16,32,128]{2,1,0:T(8,128)} %get-tuple-element.4), calls=%async_computation.2 | async-start | bytes 524288 | tf_op jit(solution)/shard_map/all_to_all | solution.py:160
  127.5 18.1 %all-to-all-start.4 = ((f32[16,40,128]{2,1,0:T(8,128)}), f32[16,40,128]{2,1,0:T(8,128)S(1)}, u32[]{:S(2)}, u32[]{:S(2)}) async-start(f32[16,40,128]{2,1,0:T(8,128)} %pad_maximum_fusion), calls=%async_computation.4 | async-start | bytes 655360 | tf_op jit(solution)/shard_map/all_to_all | solution.py:174
  146.5 13.4 %all-to-all-start.5 = ((f32[32,8,128]{2,1,0:T(8,128)}), f32[32,8,128]{2,1,0:T(8,128)S(1)}, u32[]{:S(2)}, u32[]{:S(2)}) async-start(f32[32,8,128]{2,1,0:T(8,128)} %broadcast_in_dim_broadcast_in_dim_broadcast_in_dim.2), calls=%async_computation.5 | async-start | bytes 262144 | tf_op jit(solution)/shard_map/all_to_all | solution.py:24
  160.6 19.9 %all-to-all-start.6 = ((f32[16,8,128]{2,1,0:T(8,128)}), f32[16,8,128]{2,1,0:T(8,128)S(1)}, u32[]{:S(2)}, u32[]{:S(2)}) async-start(f32[16,8,128]{2,1,0:T(8,128)} %broadcast_in_dim.29), calls=%async_computation.6 | async-start | bytes 131072 | tf_op jit(solution)/shard_map/all_to_all | solution.py:24
  166.4 6.5 %collective-permute-start = (f32[67,32]{1,0:T(8,128)S(1)}, f32[67,32]{1,0:T(8,128)S(1)}, u32[]{:S(2)}, u32[]{:S(2)}) collective-permute-start(f32[67,32]{1,0:T(8,128)S(1)} %get-tuple-element.16), channel_id=1, source_target_pairs={{1,0},{2,1},{3,2},{4,3},{5,4},{6,5},{7,6},{8,7},{9,8},{10,9},{11,1... | collective-permute-start | bytes 25736 | tf_op jit(solution)/shard_map/ppermute | solution.py:189
  171.0 9.5 %collective-permute-start.1 = (f32[67,32]{1,0:T(8,128)S(1)}, f32[67,32]{1,0:T(8,128)S(1)}, u32[]{:S(2)}, u32[]{:S(2)}) collective-permute-start(f32[67,32]{1,0:T(8,128)S(1)} %get-tuple-element.15), channel_id=1, source_target_pairs={{0,1},{1,2},{2,3},{3,4},{4,5},{5,6},{6,7},{7,8},{8,9},{9,10},{10,1... | collective-permute-start | bytes 25736 | tf_op jit(solution)/shard_map/ppermute | solution.py:188
  180.6 1.5 copy-start

commit v2 on v1

v2 whole, which is shorter than its diff:
```python
import math

import jax
import jax.numpy as jnp
from jax import lax
from jax.experimental import pallas as pl
from jax.experimental.pallas import tpu as pltpu
from jax.sharding import PartitionSpec as P

PB = 32
SWEEPS = 2


INV_FOUR_PI = 1.0 / (4.0 * math.pi)
CAP = 0.4
OMEGA = 1.5
EPS = 1e-06
LANES = 128
STEP = 256
BLOCK = 512
VMEM_BYTES = 58 << 20


def spread(block, axis, count):
    copies = jnp.broadcast_to(block[None], (count,) + block.shape)
    return lax.all_to_all(copies, axis, 0, 0, tiled=True)


def fill(source_ref, wide_ref, tile_refs, first):
    targets = wide_ref.shape[2]
    for half in range(0, 32, 16):
        at = pl.ds(pl.multiple_of(first + half, 16), 16)
        params = [
            jnp.broadcast_to(source_ref[at, row : row + 1], (16, LANES)) for row in range(7)
        ]
        src_x, src_y, src_z, nor_x, nor_y, nor_z, area = params
        for lane in range(0, targets, LANES):
            here = slice(lane, lane + LANES)
            delta_x = wide_ref[0, :, here] - src_x
            delta_y = wide_ref[1, :, here] - src_y
            delta_z = wide_ref[2, :, here] - src_z
            dist_sq = delta_x * delta_x + delta_y * delta_y + delta_z * delta_z + area
            inverse = lax.rsqrt(dist_sq)
            facing = nor_x * delta_x + nor_y * delta_y + nor_z * delta_z
            value = (facing * (inverse * inverse * inverse)).astype(jnp.bfloat16)
            for tile_ref in tile_refs:
                tile_ref[at, here] = value


def widen(target_ref, wide_ref):
    for row in range(3):
        wide_ref[row] = jnp.broadcast_to(target_ref[row : row + 1, :], wide_ref.shape[1:])


def build_kernel(source_ref, target_ref, tile_ref, wide_ref):
    @pl.when(pl.program_id(0) == 0)
    def _():
        widen(target_ref, wide_ref)

    def rows(index, carry):
        fill(source_ref, wide_ref, [tile_ref], index * 32)
        return carry

    lax.fori_loop(0, BLOCK // 32, rows, 0)


def finish_kernel(
    source_ref, target_ref, moved_ref, old_ref, tile_ref, product_ref, wide_ref, kept_ref
):
    step = pl.program_id(0)
    blocks = pl.num_programs(0) - 1
    columns = tile_ref.shape[1] // STEP
    now = step % 2
    before = 1 - now

    @pl.when(step == 0)
    def _():
        widen(target_ref, wide_ref)
        product_ref[...] = jnp.zeros_like(product_ref)

    def part_of(block):
        return jnp.concatenate([moved_ref[2 * block], moved_ref[2 * block + 1]], axis=1)

    def dot(block, value):
        return jnp.dot(part_of(block), value, preferred_element_type=jnp.float32)

    def place(index):
        down, column = index // columns, index % columns
        rows = pl.ds(pl.multiple_of(down * STEP, STEP), STEP)
        lanes = pl.ds(pl.multiple_of(column * STEP, STEP), STEP)
        return down, column, rows, lanes

    def add_to(column, value):
        product_ref[2 * column] += value[:, :LANES]
        product_ref[2 * column + 1] += value[:, LANES:]

    deep = BLOCK // STEP
    offset = blocks * deep

    @pl.when(step == 0)
    def _():
        def each(index, carry):
            down, column, rows, lanes = place(index)
            fill(source_ref, wide_ref, [tile_ref, kept_ref.at[now]], index * 32)
            add_to(column, dot(down, old_ref[rows, lanes]))
            return carry

        lax.fori_loop(0, BLOCK // 32, each, 0)

    @pl.when((step > 0) & (step < blocks))
    def _():
        def each(index, carry):
            down, column, rows, lanes = place(index)
            fill(source_ref, wide_ref, [tile_ref, kept_ref.at[now]], index * 32)
            value = dot(step * deep + down, old_ref[rows, lanes])
            value += dot(offset + (step - 1) * deep + down, kept_ref[before, rows, lanes])
            add_to(column, value)
            return carry

        lax.fori_loop(0, BLOCK // 32, each, 0)

    @pl.when(step == blocks)
    def _():
        def each(index, carry):
            down, column, rows, lanes = place(index)
            add_to(column, dot(offset + (step - 1) * deep + down, kept_ref[before, rows, lanes]))
            return carry

        lax.fori_loop(0, deep * columns, each, 0)


def build(sources, targets, count):
    width = targets.shape[1]
    return pl.pallas_call(
        build_kernel,
        grid=(count // BLOCK,),
        in_specs=[
            pl.BlockSpec((BLOCK, 8), lambda i: (i, 0)),
            pl.BlockSpec((8, width), lambda i: (0, 0)),
        ],
        out_specs=pl.BlockSpec((BLOCK, width), lambda i: (i, 0)),
        out_shape=pltpu.HBM((count, width), jnp.bfloat16),
        scratch_shapes=[pltpu.VMEM((3, 16, width), jnp.float32)],
        compiler_params=pltpu.CompilerParams(vmem_limit_bytes=VMEM_BYTES),
        cost_estimate=pl.CostEstimate(
            flops=count * width * 18, bytes_accessed=count * width * 2, transcendentals=count * width
        ),
        name="build",
    )(sources, targets)


def finish_build(sources, targets, moved, old):
    count, width = old.shape
    blocks = count // BLOCK
    onsets = moved.shape[1]
    return pl.pallas_call(
        finish_kernel,
        grid=(blocks + 1,),
        in_specs=[
            pl.BlockSpec((BLOCK, 8), lambda i: (blocks + jnp.minimum(i, blocks - 1), 0)),
            pl.BlockSpec((8, width), lambda i: (0, 0)),
            pl.BlockSpec(moved.shape, lambda i: (0, 0, 0)),
            pl.BlockSpec((BLOCK, width), lambda i: (jnp.minimum(i, blocks - 1), 0)),
        ],
        out_specs=[
            pl.BlockSpec((BLOCK, width), lambda i: (jnp.minimum(i, blocks - 1), 0)),
            pl.BlockSpec((width // LANES, onsets, LANES), lambda i: (0, 0, 0)),
        ],
        out_shape=[
            pltpu.HBM((count, width), jnp.bfloat16),
            jax.ShapeDtypeStruct((width // LANES, onsets, LANES), jnp.float32),
        ],
        scratch_shapes=[
            pltpu.VMEM((3, 16, width), jnp.float32),
            pltpu.VMEM((2, BLOCK, width), jnp.bfloat16),
        ],
        compiler_params=pltpu.CompilerParams(vmem_limit_bytes=VMEM_BYTES),
        name="finish",
    )(sources, targets, moved, old)


def apply_kernel(early_ref, late_ref, old_ref, tile_ref, product_ref):
    step = pl.program_id(0)

    def wide(ref):
        return jnp.concatenate([ref[i] for i in range(ref.shape[0])], axis=1)

    early, late = wide(early_ref), wide(late_ref)
    for column in range(tile_ref.shape[1] // STEP):
        lanes = slice(column * STEP, (column + 1) * STEP)
        value = jnp.dot(early, old_ref[:, lanes], preferred_element_type=jnp.float32)
        value += jnp.dot(late, tile_ref[:, lanes], preferred_element_type=jnp.float32)

        @pl.when(step == 0)
        def _():
            product_ref[2 * column] = value[:, :LANES]
            product_ref[2 * column + 1] = value[:, LANES:]

        @pl.when(step > 0)
        def _():
            product_ref[2 * column] += value[:, :LANES]
            product_ref[2 * column + 1] += value[:, LANES:]


def apply(moved, old, tile, depth=256):
    count, width = tile.shape
    onsets = moved.shape[1]
    steps = count // depth
    return pl.pallas_call(
        apply_kernel,
        grid=(steps,),
        in_specs=[
            pl.BlockSpec((depth // LANES, onsets, LANES), lambda i: (i, 0, 0)),
            pl.BlockSpec((depth // LANES, onsets, LANES), lambda i: (steps + i, 0, 0)),
            pl.BlockSpec((depth, width), lambda i: (i, 0)),
            pl.BlockSpec((depth, width), lambda i: (i, 0)),
        ],
        out_specs=pl.BlockSpec((width // LANES, onsets, LANES), lambda i: (0, 0, 0)),
        out_shape=jax.ShapeDtypeStruct((width // LANES, onsets, LANES), jnp.float32),
        compiler_params=pltpu.CompilerParams(vmem_limit_bytes=VMEM_BYTES),
        name="apply",
    )(moved, moved, old, tile)


def per_device(centers, normals, areas, onset, start):
    row_count = lax.axis_size("row")
    col_count = lax.axis_size("col")
    row_index = lax.axis_index("row")
    col_index = lax.axis_index("col")
    own = start.shape[1]
    count = start.shape[0]
    own_first = col_index * own
    own_areas = lax.dynamic_slice_in_dim(areas, own_first, own, 0)
    own_normals = lax.dynamic_slice_in_dim(normals, own_first, own, 1)
    own_centers = lax.dynamic_slice_in_dim(centers, own_first, own, 1)

    note = jnp.concatenate([own_centers, jnp.zeros((5, own), jnp.float32)], axis=0)
    notes = spread(note, "row", row_count)
    targets = jnp.transpose(notes, (1, 0, 2)).reshape(8, row_count * own)
    shown = lax.optimization_barrier((start, notes))[0]
    moved = spread(shown.astype(jnp.bfloat16), "col", col_count)

    sources = jnp.concatenate(
        [centers, normals * (areas * INV_FOUR_PI)[None, :], areas[None, :], areas[None, :]], axis=0
    ).T
    old = build(sources, targets, sources.shape[0] // 2)
    tile, partial = finish_build(sources, targets, moved, old)

    product = jnp.sum(lax.all_to_all(partial, "row", 0, 0, tiled=True), axis=0)
    right = -jnp.sum(onset[:, :, None] * own_normals[:, None, :], axis=0)
    residual = right - 0.5 * start - product
    gathered = spread(residual.astype(jnp.bfloat16), "col", col_count)
    partial = apply(gathered, old, tile)
    change = jnp.sum(lax.all_to_all(partial, "row", 0, 0, tiled=True), axis=0)

    flat = row_index * col_count + col_index
    devices = row_count * col_count
    edges = jnp.concatenate([start, residual, change, own_centers], axis=0)
    forward = [(i, i + 1) for i in range(devices - 1)]
    backward = [(i + 1, i) for i in range(devices - 1)]
    before = lax.ppermute(edges[:, own - PB :], ("row", "col"), forward)
    after = lax.ppermute(edges[:, :PB], ("row", "col"), backward)

    weighted = own_areas[None, :] * residual
    part = jnp.concatenate(
        [
            jnp.sum(weighted * residual, axis=1),
            jnp.sum(weighted * change, axis=1),
            jnp.sum(own_areas[None, :] * change * change, axis=1),
            jnp.broadcast_to(jnp.sum(own_areas), (count,)),
        ]
    )
    part = jnp.broadcast_to(part[None], (8, 4 * count))
    part = jnp.sum(spread(part, "col", col_count), axis=0)
    part = jnp.sum(spread(part, "row", row_count), axis=0)[0]
    both = part[:count]
    mixed = part[count : 2 * count]
    changed = part[2 * count : 3 * count]
    reach = CAP * jnp.sqrt(part[3 * count])

    def damp(sums):
        return OMEGA * jnp.minimum(1.0, reach * lax.rsqrt(sums + EPS))

    one = damp(both)
    keep = 1.0 - 0.5 * one
    sums = keep * keep * both - 2.0 * keep * one * mixed + one * one * changed
    two = damp(jnp.maximum(sums, 0.0))
    on_residual = (one + two * keep)[:, None]
    on_change = (two * one)[:, None]

    def finish(edge):
        strengths = edge[:count] + on_residual * edge[count : 2 * count]
        strengths = strengths - on_change * edge[2 * count : 3 * count]
        return jnp.concatenate([strengths, edge[3 * count :]], axis=0)

    fields = finish(edges)
    state = fields[:count]
    before = jnp.where(flat == 0, fields[:, :PB], finish(before))
    after = jnp.where(flat == devices - 1, fields[:, own - PB :], finish(after))
    padded = jnp.concatenate([before, fields, after], axis=1)
    diff_a = padded[:, 2 * PB :] - padded[:, :own]
    lane = lax.broadcasted_iota(jnp.int32, fields.shape, 1) % PB
    following = jnp.where(lane == PB - 1, jnp.roll(fields, PB - 1, 1), jnp.roll(fields, -1, 1))
    preceding = jnp.where(lane == 0, jnp.roll(fields, 1 - PB, 1), jnp.roll(fields, 1, 1))
    diff_b = following - preceding
    speeds = []
    for diff in (diff_a, diff_b):
        step = diff[count:]
        span = jnp.sqrt(jnp.sum(step * step, axis=0))
        along = jnp.sum(onset[:, :, None] * step[:, None, :], axis=0)
        speeds.append(along / span - diff[:count] / span)
    pressure = 1.0 - speeds[0] * speeds[0] - speeds[1] * speeds[1]
    return (state, pressure)


def solution(mesh):
    return jax.shard_map(
        per_device,
        mesh=mesh,
        in_specs=(P(None, "row"), P(None, "row"), P("row"), P(), P(None, ("row", "col"))),
        out_specs=(P(None, ("row", "col")), P(None, ("row", "col"))),
        check_vma=False,
    )
```

time: 183 us -> 195 us (1.066)
  Pallas kernels: 44.1 us -> 63.8 us
  waiting for transfers between devices: 54.2 us -> 46 us
  other arithmetic: 9.01 us -> 6.66 us
    pallas_call x2 -> x3, Pallas kernels: 44.1 us -> 63.8 us  [the longest x1 30.2 us: finish_build(): pl.pallas_call(finish_kernel, grid=(blocks + 1,), in_specs=[pl.BlockSpec(...]
    all_to_all x4, waiting for transfers between devices: 26.7 us -> 16.9 us  [spread(): return lax.all_to_all(copies, axis, 0, 0, tiled=True)]
    all_to_all x1, waiting for transfers between devices: 8.98 us -> 11.6 us  [per_device(): product = jnp.sum(lax.all_to_all(partial, 'row', 0, 0, tiled=True), axis=0)]
  transfers between devices with their start and end apart: 8 -> 8, of which waited for: 6 -> 5; matrix products, arithmetic and copies ran while one was open for 3% -> 3% of each run, Pallas kernels for 0% -> 10%
where the time goes in v2:
time: 195 us; the launch traced here: 194 us
  Pallas kernels  63.8 us (33%)
  starting transfers between devices  48.4 us (25%)
  waiting for transfers between devices  46 us (24%)
  blocking collectives  19.5 us (10%)
  local copies, waits for them, and re-layouts  8.08 us (4%)
  other arithmetic  6.66 us (3%)
    all_to_all x4, starting transfers between devices, spread(): return lax.all_to_all(copies, axis, 0, 0, tiled=True)  30.5 us
    pallas_call x1, Pallas kernels, finish_build(): pl.pallas_call(finish_kernel, grid=(blocks + 1,), in_specs=[pl.BlockSpec(...  30.2 us
    all_to_all x1, blocking collectives, spread(): return lax.all_to_all(copies, axis, 0, 0, tiled=True)  19.5 us
    pallas_call x1, Pallas kernels, build(): pl.pallas_call(build_kernel, grid=(count // BLOCK,), in_specs=[pl.BlockSp...  18.8 us
    all_to_all x4, waiting for transfers between devices, spread(): return lax.all_to_all(copies, axis, 0, 0, tiled=True)  16.9 us
    pallas_call x1, Pallas kernels, apply(): pl.pallas_call(apply_kernel, grid=(steps,), in_specs=[pl.BlockSpec((depth...  14.7 us
    all_to_all x1, waiting for transfers between devices, per_device(): product = jnp.sum(lax.all_to_all(partial, 'row', 0, 0, tiled=True), axis=0)  11.6 us
    all_to_all x1, waiting for transfers between devices, per_device(): change = jnp.sum(lax.all_to_all(partial, 'row', 0, 0, tiled=True), axis=0)  9.93 us
  transfers between devices with their start and end apart: 8, of which 5 were waited for; matrix products, arithmetic and copies ran while one was open for 3% of the time, Pallas kernels for 10%

profile of v2, /device:TPU:6, one launch (start us, length us, event | category | flops | bytes accessed | tf_op | source)
XLA Modules:
  0.0 194.0 jit_solution(16712074726608776332)
XLA Ops:
  0.6 0.7 constant_dynamic-slice_fusion
  1.3 0.6 broadcast_in_dim.13
  2.0 10.1 %all-to-all-start = ((f32[16,8,128]{2,1,0:T(8,128)}), f32[16,8,128]{2,1,0:T(8,128)S(1)}, u32[]{:S(2)}, u32[]{:S(2)}) async-start(f32[16,8,128]{2,1,0:T(8,128)} %broadcast_in_dim.13), calls=%async_computation | async-start | bytes 131072 | tf_op jit(solution)/shard_map/all_to_all | solution.py:26
  12.0 0.7 broadcast_multiply_fusion.1
  12.7 7.3 %all-to-all-done = f32[16,8,128]{2,1,0:T(8,128)S(1)} async-done(((f32[16,8,128]{2,1,0:T(8,128)}), f32[16,8,128]{2,1,0:T(8,128)S(1)}, u32[]{:S(2)}, u32[]{:S(2)}) %all-to-all-start) | async-done | bytes 65568 | tf_op jit(solution)/shard_map/all_to_all | solution.py:26
  20.1 0.7 convert_element_type.6
  20.8 0.7 broadcast_in_dim.14
  21.5 10.8 %all-to-all-start.1 = ((bf16[32,32,128]{2,1,0:T(8,128)(2,1)}), bf16[32,32,128]{2,1,0:T(8,128)(2,1)S(1)}, u32[]{:S(2)}, u32[]{:S(2)}) async-start(bf16[32,32,128]{2,1,0:T(8,128)(2,1)} %broadcast_in_dim.14), calls=%async_computation.1 | async-start | bytes 524288 | tf_op jit(solution)/shard_map/all_to_all | solution.py:26
  32.4 0.9 broadcast_multiply_fusion
  33.2 0.9 pad_maximum_fusion
  34.2 2.0 %copy.16 = f32[8,4096]{0,1:T(8,128)} copy(f32[8,4096]{1,0:T(8,128)S(1)} %pad_maximum_fusion) | data formatting | bytes 262144 | tf_op jit(solution)/shard_map/concatenate | solution.py:243
  36.2 18.8 %build.1.old_ref = bf16[2048,2048]{1,0:T(8,128)(2,1)} custom-call(f32[4096,8]{1,0:T(8,128)} %bitcast.44, f32[8,2048]{1,0:T(8,128)} %bitcast.46), custom_call_target="tpu_custom_call" | custom-call | flops 75497472 | bytes 8388608 | tf_op jit(solution)/shard_map/build/pallas_call | solution.py:134
  55.0 0.7 copy-done.1
  55.7 30.2 %finish.1 = (bf16[2048,2048]{1,0:T(8,128)(2,1)}, f32[16,32,128]{2,1,0:T(8,128)}) custom-call(f32[4096,8]{1,0:T(8,128)} %bitcast.45, f32[8,2048]{1,0:T(8,128)} %bitcast.47, bf16[32,32,128]{2,1,0:T(8,128)(2,1)} %copy-done.1, bf16[2048,2048]{1,0:T(8,128)(2,1)} %build.1.old_ref), custom_call_target="tpu_custom_call" | custom-call | tf_op jit(solution)/shard_map/finish/pallas_call | solution.py:156
  85.9 5.7 %all-to-all-start.2 = ((f32[16,32,128]{2,1,0:T(8,128)}), f32[16,32,128]{2,1,0:T(8,128)S(1)}, u32[]{:S(2)}, u32[]{:S(2)}) async-start(f32[16,32,128]{2,1,0:T(8,128)} %get-tuple-element.6), calls=%async_computation.2 | async-start | bytes 524288 | tf_op jit(solution)/shard_map/all_to_all | solution.py:249
  91.6 0.7 constant_dynamic-slice_fusion.1
  92.3 11.6 %all-to-all-done.2 = f32[16,32,128]{2,1,0:T(8,128)S(1)} async-done(((f32[16,32,128]{2,1,0:T(8,128)}), f32[16,32,128]{2,1,0:T(8,128)S(1)}, u32[]{:S(2)}, u32[]{:S(2)}) %all-to-all-start.2) | async-done | bytes 262176 | tf_op jit(solution)/shard_map/all_to_all | solution.py:249
  104.0 19.5 %all_to_all.35.early_ref.late_ref = bf16[32,32,128]{2,1,0:T(8,128)(2,1)} all-to-all(bf16[32,32,128]{2,1,0:T(8,128)(2,1)S(1)} %broadcast_in_dim.15), channel_id=1, replica_groups=mesh['row'=16,'col'=32] {'col'}, dimensions={0} | all-to-all | bytes 524288 | tf_op jit(solution)/shard_map/all_to_all | solution.py:26
  123.5 14.7 %apply.1 = f32[16,32,128]{2,1,0:T(8,128)} custom-call(bf16[32,32,128]{2,1,0:T(8,128)(2,1)} %all_to_all.35.early_ref.late_ref, bf16[32,32,128]{2,1,0:T(8,128)(2,1)} %all_to_all.35.early_ref.late_ref, bf16[2048,2048]{1,0:T(8,128)(2,1)} %build.1.old_ref, bf16[2048,2048]{1,0:T(8,128)(2,1)} %get-tuple-element.7.tile_ref), custom_call_target="tpu_custom_call" | custom-call | tf_op jit(solution)/shard_map/apply/pallas_call | solution.py:209
  138.2 5.8 %all-to-all-start.4 = ((f32[16,32,128]{2,1,0:T(8,128)}), f32[16,32,128]{2,1,0:T(8,128)S(1)}, u32[]{:S(2)}, u32[]{:S(2)}) async-start(f32[16,32,128]{2,1,0:T(8,128)} %apply.1), calls=%async_computation.4 | async-start | bytes 524288 | tf_op jit(solution)/shard_map/all_to_all | solution.py:254
  144.0 1.4 fusion.36
  145.4 9.9 %all-to-all-done.4 = f32[16,32,128]{2,1,0:T(8,128)S(1)} async-done(((f32[16,32,128]{2,1,0:T(8,128)}), f32[16,32,128]{2,1,0:T(8,128)S(1)}, u32[]{:S(2)}, u32[]{:S(2)}) %all-to-all-start.4) | async-done | bytes 262176 | tf_op jit(solution)/shard_map/all_to_all | solution.py:254
  155.5 0.7 broadcast_in_dim.16
  156.2 0.7 broadcast_in_dim_broadcast_in_dim_broadcast_in_dim.2
  156.9 3.9 %all-to-all-start.5 = ((f32[32,8,128]{2,1,0:T(8,128)}), f32[32,8,128]{2,1,0:T(8,128)S(1)}, u32[]{:S(2)}, u32[]{:S(2)}) async-start(f32[32,8,128]{2,1,0:T(8,128)} %broadcast_in_dim_broadcast_in_dim_broadcast_in_dim.2), calls=%async_computation.5 | async-start | bytes 262144 | tf_op jit(solution)/shard_map/all_to_all | solution.py:26
  160.7 9.5 %all-to-all-done.5 = f32[32,8,128]{2,1,0:T(8,128)S(1)} async-done(((f32[32,8,128]{2,1,0:T(8,128)}), f32[32,8,128]{2,1,0:T(8,128)S(1)}, u32[]{:S(2)}, u32[]{:S(2)}) %all-to-all-start.5) | async-done | bytes 131104 | tf_op jit(solution)/shard_map/all_to_all | solution.py:26
  170.3 0.6 broadcast_in_dim.17
  170.9 5.8 %all-to-all-start.6 = ((f32[16,8,128]{2,1,0:T(8,128)}), f32[16,8,128]{2,1,0:T(8,128)S(1)}, u32[]{:S(2)}, u32[]{:S(2)}) async-start(f32[16,8,128]{2,1,0:T(8,128)} %broadcast_in_dim.17), calls=%async_computation.6 | async-start | bytes 131072 | tf_op jit(solution)/shard_map/all_to_all | solution.py:26
  176.8 4.6 %collective-permute-start = (f32[99,32]{1,0:T(8,128)S(1)}, f32[99,32]{1,0:T(8,128)S(1)}, u32[]{:S(2)}, u32[]{:S(2)}) collective-permute-start(f32[99,32]{1,0:T(8,128)S(1)} %get-tuple-element.22), channel_id=1, source_target_pairs={{1,0},{2,1},{3,2},{4,3},{5,4},{6,5},{7,6},{8,7},{9,8},{10,9},{11,1... | collective-permute-start | bytes 38024 | tf_op jit(solution)/shard_map/ppermute | solution.py:262
  181.3 1.9 collective-permute-start.1
  183.3 7.7 %collective-permute-done.1 = f32[99,32]{1,0:T(8,128)S(1)} collective-permute-done((f32[99,32]{1,0:T(8,128)S(1)}, f32[99,32]{1,0:T(8,128)S(1)}, u32[]{:S(2)}, u32[]{:S(2)}) %collective-permute-start.1) | collective-permute-done | bytes 12704 | tf_op jit(solution)/shard_map/ppermute | solution.py:261
  193.3 0.7 fusion.19
  (44 shorter events, 2.1 us)
Async XLA Ops:
  2.0 18.1 %all-to-all-start = ((f32[16,8,128]{2,1,0:T(8,128)}), f32[16,8,128]{2,1,0:T(8,128)S(1)}, u32[]{:S(2)}, u32[]{:S(2)}) async-start(f32[16,8,128]{2,1,0:T(8,128)} %broadcast_in_dim.13), calls=%async_computation | async-start | bytes 131072 | tf_op jit(solution)/shard_map/all_to_all | solution.py:26
  20.1 16.1 %copy-start.2 = (f32[16,8,128]{2,1,0:T(8,128)}, f32[16,8,128]{2,1,0:T(8,128)S(1)}, u32[]{:S(2)}) copy-start(f32[16,8,128]{2,1,0:T(8,128)S(1)} %all-to-all-done) | copy-start | bytes 196612
  21.5 33.5 %all-to-all-start.1 = ((bf16[32,32,128]{2,1,0:T(8,128)(2,1)}), bf16[32,32,128]{2,1,0:T(8,128)(2,1)S(1)}, u32[]{:S(2)}, u32[]{:S(2)}) async-start(bf16[32,32,128]{2,1,0:T(8,128)(2,1)} %broadcast_in_dim.14), calls=%async_computation.1 | async-start | bytes 524288 | tf_op jit(solution)/shard_map/all_to_all | solution.py:26
  36.1 56.1 %copy-start.4 = (f32[3,32]{1,0:T(4,128)S(1)}, f32[3,32]{1,0:T(4,128)}, u32[]{:S(2)}) copy-start(f32[3,32]{1,0:T(4,128)} %param.8) | copy-start | bytes 1156
  55.0 48.9 %copy-start.3 = (f32[32,128]{1,0:T(8,128)S(1)}, f32[32,128]{1,0:T(8,128)}, u32[]{:S(2)}) copy-start(f32[32,128]{1,0:T(8,128)} %param.9) | copy-start | bytes 49156
  55.0 0.7 copy-start.1
  85.9 18.0 %all-to-all-start.2 = ((f32[16,32,128]{2,1,0:T(8,128)}), f32[16,32,128]{2,1,0:T(8,128)S(1)}, u32[]{:S(2)}, u32[]{:S(2)}) async-start(f32[16,32,128]{2,1,0:T(8,128)} %get-tuple-element.6), calls=%async_computation.2 | async-start | bytes 524288 | tf_op jit(solution)/shard_map/all_to_all | solution.py:249
  138.2 17.1 %all-to-all-start.4 = ((f32[16,32,128]{2,1,0:T(8,128)}), f32[16,32,128]{2,1,0:T(8,128)S(1)}, u32[]{:S(2)}, u32[]{:S(2)}) async-start(f32[16,32,128]{2,1,0:T(8,128)} %apply.1), calls=%async_computation.4 | async-start | bytes 524288 | tf_op jit(solution)/shard_map/all_to_all | solution.py:254
  156.9 13.4 %all-to-all-start.5 = ((f32[32,8,128]{2,1,0:T(8,128)}), f32[32,8,128]{2,1,0:T(8,128)S(1)}, u32[]{:S(2)}, u32[]{:S(2)}) async-start(f32[32,8,128]{2,1,0:T(8,128)} %broadcast_in_dim_broadcast_in_dim_broadcast_in_dim.2), calls=%async_computation.5 | async-start | bytes 262144 | tf_op jit(solution)/shard_map/all_to_all | solution.py:26
  170.9 20.1 %all-to-all-start.6 = ((f32[16,8,128]{2,1,0:T(8,128)}), f32[16,8,128]{2,1,0:T(8,128)S(1)}, u32[]{:S(2)}, u32[]{:S(2)}) async-start(f32[16,8,128]{2,1,0:T(8,128)} %broadcast_in_dim.17), calls=%async_computation.6 | async-start | bytes 131072 | tf_op jit(solution)/shard_map/all_to_all | solution.py:26
  176.8 6.5 %collective-permute-start = (f32[99,32]{1,0:T(8,128)S(1)}, f32[99,32]{1,0:T(8,128)S(1)}, u32[]{:S(2)}, u32[]{:S(2)}) collective-permute-start(f32[99,32]{1,0:T(8,128)S(1)} %get-tuple-element.22), channel_id=1, source_target_pairs={{1,0},{2,1},{3,2},{4,3},{5,4},{6,5},{7,6},{8,7},{9,8},{10,9},{11,1... | collective-permute-start | bytes 38024 | tf_op jit(solution)/shard_map/ppermute | solution.py:262
  181.3 9.7 %collective-permute-start.1 = (f32[99,32]{1,0:T(8,128)S(1)}, f32[99,32]{1,0:T(8,128)S(1)}, u32[]{:S(2)}, u32[]{:S(2)}) collective-permute-start(f32[99,32]{1,0:T(8,128)S(1)} %get-tuple-element.21), channel_id=1, source_target_pairs={{0,1},{1,2},{2,3},{3,4},{4,5},{5,6},{6,7},{7,8},{8,9},{9,10},{10,1... | collective-permute-start | bytes 38024 | tf_op jit(solution)/shard_map/ppermute | solution.py:261
  192.5 1.5 copy-start

commit v3 on v2

v3 whole, which is shorter than its diff:
```python
import math

import jax
import jax.numpy as jnp
from jax import lax
from jax.experimental import pallas as pl
from jax.experimental.pallas import tpu as pltpu
from jax.sharding import PartitionSpec as P

PB = 32
SWEEPS = 2


INV_FOUR_PI = 1.0 / (4.0 * math.pi)
CAP = 0.4
OMEGA = 1.5
EPS = 1e-06
LANES = 128
STEP = 256
BLOCK = 512
VMEM_BYTES = 58 << 20


def spread(block, axis, count):
    copies = jnp.broadcast_to(block[None], (count,) + block.shape)
    return lax.all_to_all(copies, axis, 0, 0, tiled=True)


def three(value):
    high = value.astype(jnp.bfloat16).astype(jnp.float32)
    rest = value - high
    middle = rest.astype(jnp.bfloat16).astype(jnp.float32)
    return high, middle, rest - middle


def factor_kernel(place_ref, normal_ref, factor_ref):
    place = place_ref[...]
    scaled = normal_ref[...] * (place[3:4, :] * INV_FOUR_PI)
    level = -jnp.sum(scaled * place, axis=0, keepdims=True)
    at_level = lax.broadcasted_iota(jnp.int32, place.shape, 0) == 3
    high, middle, low = three(jnp.where(at_level, level, scaled))
    bare = jnp.where(at_level, 0.0, high)
    bare_middle = jnp.where(at_level, 0.0, middle)
    none = jnp.zeros_like(high)
    rows = [high, bare, middle, bare, bare_middle, low, none, none]
    rows += list(three(place)) + [none] * 5
    factor_ref[...] = jnp.concatenate(rows, axis=0).T.astype(jnp.bfloat16)


def source_factors(place, normal):
    count = place.shape[1]
    return pl.pallas_call(
        factor_kernel,
        grid=(count // BLOCK,),
        in_specs=[pl.BlockSpec((8, BLOCK), lambda i: (0, i))] * 2,
        out_specs=pl.BlockSpec((BLOCK, LANES), lambda i: (i, 0)),
        out_shape=jax.ShapeDtypeStruct((count, LANES), jnp.bfloat16),
        cost_estimate=pl.CostEstimate(
            flops=count * 400, bytes_accessed=count * 320, transcendentals=0
        ),
        name="factors",
    )(place, normal)


def target_factors(targets):
    high = targets.astype(jnp.bfloat16).astype(jnp.float32)
    rest = targets - high
    middle = rest.astype(jnp.bfloat16).astype(jnp.float32)
    low = rest - middle
    rows = [high, middle, high, low, middle, high]
    return jnp.concatenate(rows, axis=0).astype(jnp.bfloat16)


def fill(factor_ref, target_ref, wide_ref, pair_ref, column, stores):
    facing = jnp.dot(
        factor_ref[:, :48],
        pair_ref[:, column : column + STEP],
        preferred_element_type=jnp.float32,
    )
    for lane in range(0, STEP, LANES):
        here = slice(column + lane, column + lane + LANES)
        x, y, z = (target_ref[d : d + 1, here] for d in range(3))
        for row in range(0, BLOCK, 16):
            at = slice(row, row + 16)
            delta_x = x - wide_ref[0, at, :]
            delta_y = y - wide_ref[1, at, :]
            delta_z = z - wide_ref[2, at, :]
            dist_sq = delta_x * delta_x + delta_y * delta_y + delta_z * delta_z + wide_ref[3, at, :]
            inverse = lax.rsqrt(dist_sq)
            value = facing[row : row + 16, lane : lane + LANES] * (inverse * inverse * inverse)
            value = value.astype(jnp.bfloat16)
            for store in stores:
                store[at, here] = value


def prepare(target_ref, pair_ref, spread_ref):
    pair_ref[...] = target_factors(target_ref[...])
    which = lax.broadcasted_iota(jnp.int32, spread_ref.shape, 0)
    lane = lax.broadcasted_iota(jnp.int32, spread_ref.shape, 1)
    chosen = which % 8 == lane // LANES
    spread_ref[...] = jnp.where(chosen, 1.0, 0.0).astype(jnp.bfloat16)


def spread_params(factor_ref, spread_ref, wide_ref):
    wide = jnp.dot(factor_ref[:, 64:96], spread_ref[...], preferred_element_type=jnp.float32)
    for row in range(4):
        wide_ref[row] = wide[:, row * LANES : (row + 1) * LANES]


def build_kernel(factor_ref, target_ref, tile_ref, wide_ref, pair_ref, spread_ref):
    @pl.when(pl.program_id(0) == 0)
    def _():
        prepare(target_ref, pair_ref, spread_ref)

    spread_params(factor_ref, spread_ref, wide_ref)
    for column in range(0, tile_ref.shape[1], STEP):
        fill(factor_ref, target_ref, wide_ref, pair_ref, column, [tile_ref])


def finish_kernel(
    factor_ref,
    target_ref,
    moved_ref,
    old_ref,
    tile_ref,
    product_ref,
    wide_ref,
    pair_ref,
    spread_ref,
    even_ref,
    odd_ref,
):
    step = pl.program_id(0)
    blocks = pl.num_programs(0) - 1
    width = tile_ref.shape[1]
    deep = BLOCK // LANES

    @pl.when(step == 0)
    def _():
        prepare(target_ref, pair_ref, spread_ref)
        product_ref[...] = jnp.zeros_like(product_ref)

    def dot(block, ref, column):
        part = jnp.concatenate([moved_ref[deep * block + i] for i in range(deep)], axis=1)
        return jnp.dot(
            part, ref[:, column : column + STEP], preferred_element_type=jnp.float32
        )

    def add_to(column, value):
        for lane in range(0, STEP, LANES):
            product_ref[(column + lane) // LANES] += value[:, lane : lane + LANES]

    def whole(now_ref, before_ref):
        spread_params(factor_ref, spread_ref, wide_ref)
        for column in range(0, width, STEP):
            value = dot(step, old_ref, column)
            if before_ref is not None:
                value += dot(blocks + step - 1, before_ref, column)
            fill(
                factor_ref, target_ref, wide_ref, pair_ref, column, [tile_ref, now_ref]
            )
            add_to(column, value)

    @pl.when(step == 0)
    def _():
        whole(even_ref, None)

    @pl.when((step > 0) & (step < blocks) & (step % 2 == 0))
    def _():
        whole(even_ref, odd_ref)

    @pl.when((step < blocks) & (step % 2 == 1))
    def _():
        whole(odd_ref, even_ref)

    @pl.when((step == blocks) & (step % 2 == 0))
    def _():
        for column in range(0, width, STEP):
            add_to(column, dot(blocks + step - 1, odd_ref, column))

    @pl.when((step == blocks) & (step % 2 == 1))
    def _():
        for column in range(0, width, STEP):
            add_to(column, dot(blocks + step - 1, even_ref, column))


def build(factors, targets):
    count = factors.shape[0]
    width = targets.shape[1]
    return pl.pallas_call(
        build_kernel,
        grid=(count // BLOCK // 2,),
        in_specs=[
            pl.BlockSpec((BLOCK, LANES), lambda i: (i, 0)),
            pl.BlockSpec((8, width), lambda i: (0, 0)),
        ],
        out_specs=pl.BlockSpec((BLOCK, width), lambda i: (i, 0)),
        out_shape=pltpu.HBM((count, width), jnp.bfloat16),
        scratch_shapes=[
            pltpu.VMEM((4, BLOCK, LANES), jnp.float32),
            pltpu.VMEM((48, width), jnp.bfloat16),
            pltpu.VMEM((32, 4 * LANES), jnp.bfloat16),
        ],
        compiler_params=pltpu.CompilerParams(vmem_limit_bytes=VMEM_BYTES),
        cost_estimate=pl.CostEstimate(
            flops=count * width * 50, bytes_accessed=count * width, transcendentals=count * width // 2
        ),
        name="build",
    )(factors, targets)


def finish_build(factors, targets, moved, tile):
    count, width = tile.shape
    blocks = count // BLOCK // 2
    onsets = moved.shape[1]
    return pl.pallas_call(
        finish_kernel,
        grid=(blocks + 1,),
        in_specs=[
            pl.BlockSpec((BLOCK, LANES), lambda i: (blocks + jnp.minimum(i, blocks - 1), 0)),
            pl.BlockSpec((8, width), lambda i: (0, 0)),
            pl.BlockSpec(moved.shape, lambda i: (0, 0, 0)),
            pl.BlockSpec((BLOCK, width), lambda i: (jnp.minimum(i, blocks - 1), 0)),
        ],
        out_specs=[
            pl.BlockSpec((BLOCK, width), lambda i: (blocks + jnp.minimum(i, blocks - 1), 0)),
            pl.BlockSpec((width // LANES, onsets, LANES), lambda i: (0, 0, 0)),
        ],
        out_shape=[
            pltpu.HBM((count, width), jnp.bfloat16),
            jax.ShapeDtypeStruct((width // LANES, onsets, LANES), jnp.float32),
        ],
        scratch_shapes=[
            pltpu.VMEM((4, BLOCK, LANES), jnp.float32),
            pltpu.VMEM((48, width), jnp.bfloat16),
            pltpu.VMEM((32, 4 * LANES), jnp.bfloat16),
            pltpu.VMEM((BLOCK, width), jnp.bfloat16),
            pltpu.VMEM((BLOCK, width), jnp.bfloat16),
        ],
        input_output_aliases={3: 0},
        compiler_params=pltpu.CompilerParams(vmem_limit_bytes=VMEM_BYTES),
        name="finish",
    )(factors, targets, moved, tile)


def apply_kernel(moved_ref, tile_ref, product_ref):
    step = pl.program_id(0)
    chunks = range(tile_ref.shape[1] // LANES)
    part = jnp.concatenate([moved_ref[i] for i in range(moved_ref.shape[0])], axis=1)
    product = jnp.dot(part, tile_ref[...], preferred_element_type=jnp.float32)

    @pl.when(step == 0)
    def _():
        for chunk in chunks:
            product_ref[chunk] = product[:, chunk * LANES : (chunk + 1) * LANES]

    @pl.when(step > 0)
    def _():
        for chunk in chunks:
            product_ref[chunk] += product[:, chunk * LANES : (chunk + 1) * LANES]


def apply(moved, tile, depth=1024):
    count, width = tile.shape
    onsets = moved.shape[1]
    return pl.pallas_call(
        apply_kernel,
        grid=(count // depth,),
        in_specs=[
            pl.BlockSpec((depth // LANES, onsets, LANES), lambda i: (i, 0, 0)),
            pl.BlockSpec((depth, width), lambda i: (i, 0)),
        ],
        out_specs=pl.BlockSpec((width // LANES, onsets, LANES), lambda i: (0, 0, 0)),
        out_shape=jax.ShapeDtypeStruct((width // LANES, onsets, LANES), jnp.float32),
        compiler_params=pltpu.CompilerParams(vmem_limit_bytes=VMEM_BYTES),
        name="apply",
    )(moved, tile)


def per_device(centers, normals, areas, onset, start):
    row_count = lax.axis_size("row")
    col_count = lax.axis_size("col")
    row_index = lax.axis_index("row")
    col_index = lax.axis_index("col")
    own = start.shape[1]
    count = start.shape[0]
    own_first = col_index * own
    own_areas = lax.dynamic_slice_in_dim(areas, own_first, own, 0)
    own_normals = lax.dynamic_slice_in_dim(normals, own_first, own, 1)
    own_centers = lax.dynamic_slice_in_dim(centers, own_first, own, 1)

    mark = jnp.concatenate([jnp.ones((1, own)), jnp.zeros((4, own))], axis=0)
    note = jnp.concatenate([own_centers, mark.astype(jnp.float32)], axis=0)
    notes = spread(note, "row", row_count)
    shown = jnp.broadcast_to(start.astype(jnp.bfloat16)[None], (col_count, count, own))
    place = jnp.concatenate([centers, areas[None, :], jnp.zeros((4, areas.shape[0]))], axis=0)
    factors = source_factors(place, jnp.pad(normals, ((0, 5), (0, 0))))
    notes, shown, factors = lax.optimization_barrier((notes, shown, factors))
    targets = jnp.transpose(notes, (1, 0, 2)).reshape(8, row_count * own)
    moved = lax.all_to_all(shown, "col", 0, 0, tiled=True)

    tile = build(factors, targets)
    tile, partial = finish_build(factors, targets, moved, tile)

    product = jnp.sum(lax.all_to_all(partial, "row", 0, 0, tiled=True), axis=0)
    right = -jnp.sum(onset[:, :, None] * own_normals[:, None, :], axis=0)
    residual = right - 0.5 * start - product
    gathered = spread(residual.astype(jnp.bfloat16), "col", col_count)
    partial = apply(gathered, tile)
    change = jnp.sum(lax.all_to_all(partial, "row", 0, 0, tiled=True), axis=0)

    flat = row_index * col_count + col_index
    devices = row_count * col_count
    edges = jnp.concatenate([start, residual, change, own_centers], axis=0)
    forward = [(i, i + 1) for i in range(devices - 1)]
    backward = [(i + 1, i) for i in range(devices - 1)]
    before = lax.ppermute(edges[:, own - PB :], ("row", "col"), forward)
    after = lax.ppermute(edges[:, :PB], ("row", "col"), backward)

    weighted = own_areas[None, :] * residual
    part = jnp.concatenate(
        [
            jnp.sum(weighted * residual, axis=1),
            jnp.sum(weighted * change, axis=1),
            jnp.sum(own_areas[None, :] * change * change, axis=1),
            jnp.broadcast_to(jnp.sum(own_areas), (count,)),
        ]
    )
    part = jnp.broadcast_to(part[None, None], (col_count, 8, 4 * count))
    part = jnp.sum(lax.all_to_all(part, "col", 0, 0, tiled=True), axis=0)
    part = jnp.sum(spread(part, "row", row_count), axis=0)[0]
    both = part[:count]
    mixed = part[count : 2 * count]
    changed = part[2 * count : 3 * count]
    reach = CAP * jnp.sqrt(part[3 * count])

    def damp(sums):
        return OMEGA * jnp.minimum(1.0, reach * lax.rsqrt(sums + EPS))

    one = damp(both)
    keep = 1.0 - 0.5 * one
    sums = keep * keep * both - 2.0 * keep * one * mixed + one * one * changed
    two = damp(jnp.maximum(sums, 0.0))
    on_residual = (one + two * keep)[:, None]
    on_change = (two * one)[:, None]

    def finish(edge):
        strengths = edge[:count] + on_residual * edge[count : 2 * count]
        strengths = strengths - on_change * edge[2 * count : 3 * count]
        return jnp.concatenate([strengths, edge[3 * count :]], axis=0)

    fields = finish(edges)
    state = fields[:count]
    before = jnp.where(flat == 0, fields[:, :PB], finish(before))
    after = jnp.where(flat == devices - 1, fields[:, own - PB :], finish(after))
    padded = jnp.concatenate([before, fields, after], axis=1)
    diff_a = padded[:, 2 * PB :] - padded[:, :own]
    lane = lax.broadcasted_iota(jnp.int32, fields.shape, 1) % PB
    following = jnp.where(lane == PB - 1, jnp.roll(fields, PB - 1, 1), jnp.roll(fields, -1, 1))
    preceding = jnp.where(lane == 0, jnp.roll(fields, 1 - PB, 1), jnp.roll(fields, 1, 1))
    diff_b = following - preceding
    speeds = []
    for diff in (diff_a, diff_b):
        step = diff[count:]
        span = jnp.sqrt(jnp.sum(step * step, axis=0))
        along = jnp.sum(onset[:, :, None] * step[:, None, :], axis=0)
        speeds.append(along / span - diff[:count] / span)
    pressure = 1.0 - speeds[0] * speeds[0] - speeds[1] * speeds[1]
    return (state, pressure)


def solution(mesh):
    return jax.shard_map(
        per_device,
        mesh=mesh,
        in_specs=(P(None, "row"), P(None, "row"), P("row"), P(), P(None, ("row", "col"))),
        out_specs=(P(None, ("row", "col")), P(None, ("row", "col"))),
        check_vma=False,
    )
```

time: 195 us -> 164 us (0.84)
  Pallas kernels: 63.8 us -> 37.5 us
  waiting for transfers between devices: 46 us -> 38.6 us
  starting transfers between devices: 48.4 us -> 52.4 us
    all_to_all x4 -> x2, waiting for transfers between devices: 16.9 us -> 0.01 us  [spread(): return lax.all_to_all(copies, axis, 0, 0, tiled=True)]
    pallas_call x1, Pallas kernels: 30.2 us -> 13.5 us  [finish_build(): pl.pallas_call(finish_kernel, grid=(blocks + 1,), in_specs=[pl.BlockSpec(...]
    all_to_all x4 -> x2, starting transfers between devices: 30.5 us -> 15.8 us  [spread(): return lax.all_to_all(copies, axis, 0, 0, tiled=True)]
    all_to_all x0 -> x2, starting transfers between devices: none -> 14.7 us  [the longest x1 10.8 us: per_device(): moved = lax.all_to_all(shown, 'col', 0, 0, tiled=True)]
    all_to_all x0 -> x2, waiting for transfers between devices: none -> 10.9 us  [the longest x1 9.52 us: per_device(): part = jnp.sum(lax.all_to_all(part, 'col', 0, 0, tiled=True), axis=0)]
    pallas_call x2 -> x3, Pallas kernels: 33.6 us -> 24 us  [the longest x1 10.8 us: build(): pl.pallas_call(build_kernel, grid=(count // BLOCK // 2,), in_specs=[pl.Bl...]
    all_to_all x1, starting transfers between devices: 5.66 us -> 9.63 us  [per_device(): product = jnp.sum(lax.all_to_all(partial, 'row', 0, 0, tiled=True), axis=0)]
  transfers between devices with their start and end apart: 8 -> 8, of which waited for: 5 -> 5; matrix products, arithmetic and copies ran while one was open for 3% -> 4% of each run, Pallas kernels for 10% -> 10%
where the time goes in v3:
time: 164 us; the launch traced here: 163 us
  starting transfers between devices  52.4 us (32%)
  waiting for transfers between devices  38.6 us (24%)
  Pallas kernels  37.5 us (23%)
  blocking collectives  19.4 us (12%)
  local copies, waits for them, and re-layouts  7.79 us (5%)
  other arithmetic  5.78 us (4%)
    all_to_all x1, blocking collectives, spread(): return lax.all_to_all(copies, axis, 0, 0, tiled=True)  19.4 us
    all_to_all x2, starting transfers between devices, spread(): return lax.all_to_all(copies, axis, 0, 0, tiled=True)  15.8 us
    pallas_call x1, Pallas kernels, finish_build(): pl.pallas_call(finish_kernel, grid=(blocks + 1,), in_specs=[pl.BlockSpec(...  13.5 us
    pallas_call x1, Pallas kernels, build(): pl.pallas_call(build_kernel, grid=(count // BLOCK // 2,), in_specs=[pl.Bl...  10.8 us
    all_to_all x1, starting transfers between devices, per_device(): moved = lax.all_to_all(shown, 'col', 0, 0, tiled=True)  10.8 us
    all_to_all x1, waiting for transfers between devices, per_device(): product = jnp.sum(lax.all_to_all(partial, 'row', 0, 0, tiled=True), axis=0)  10.1 us
    all_to_all x1, waiting for transfers between devices, per_device(): change = jnp.sum(lax.all_to_all(partial, 'row', 0, 0, tiled=True), axis=0)  9.93 us
    all_to_all x1, starting transfers between devices, per_device(): product = jnp.sum(lax.all_to_all(partial, 'row', 0, 0, tiled=True), axis=0)  9.63 us
  transfers between devices with their start and end apart: 8, of which 5 were waited for; matrix products, arithmetic and copies ran while one was open for 4% of the time, Pallas kernels for 10%

profile of v3, /device:TPU:6, one launch (start us, length us, event | category | flops | bytes accessed | tf_op | source)
XLA Modules:
  0.0 163.0 jit_solution(15700029559112156707)
XLA Ops:
  0.8 0.7 constant_dynamic-slice_fusion
  1.6 0.6 broadcast_in_dim.22
  2.2 10.1 %all-to-all-start = ((f32[16,8,128]{2,1,0:T(8,128)}), f32[16,8,128]{2,1,0:T(8,128)S(1)}, u32[]{:S(2)}, u32[]{:S(2)}) async-start(f32[16,8,128]{2,1,0:T(8,128)} %broadcast_in_dim.22), calls=%async_computation | async-start | bytes 131072 | tf_op jit(solution)/shard_map/all_to_all | solution.py:26
  12.2 1.6 maximum_maximum_fusion.place_ref
  13.8 1.5 pad.4.normal_ref
  15.3 0.7 convert_element_type.8
  16.0 4.8 %factors.1.factor_ref = bf16[4096,128]{1,0:T(8,128)(2,1)} custom-call(f32[8,4096]{1,0:T(8,128)} %maximum_maximum_fusion.place_ref, f32[8,4096]{1,0:T(8,128)} %pad.4.normal_ref), custom_call_target="tpu_custom_call" | custom-call | flops 1638400 | bytes 1310720 | tf_op jit(solution)/shard_map/factors/pallas_call | solution.py:52
  20.9 0.8 broadcast_in_dim.23
  21.6 10.8 %all-to-all-start.1 = ((bf16[32,32,128]{2,1,0:T(8,128)(2,1)}), bf16[32,32,128]{2,1,0:T(8,128)(2,1)S(1)}, u32[]{:S(2)}, u32[]{:S(2)}) async-start(bf16[32,32,128]{2,1,0:T(8,128)(2,1)} %broadcast_in_dim.23), calls=%async_computation.1 | async-start | bytes 524288 | tf_op jit(solution)/shard_map/all_to_all | solution.py:300
  32.5 10.8 %build.1.old_ref = bf16[4096,2048]{1,0:T(8,128)(2,1)} custom-call(bf16[4096,128]{1,0:T(8,128)(2,1)} %factors.1.factor_ref, f32[8,2048]{1,0:T(8,128)} %bitcast.44), custom_call_target="tpu_custom_call" | custom-call | flops 419430400 | bytes 8388608 | tf_op jit(solution)/shard_map/build/pallas_call | solution.py:190
  43.3 1.4 all-to-all-done.1.moved_ref
  44.7 0.7 copy-done.1
  45.4 13.5 %finish.1 = (bf16[4096,2048]{1,0:T(8,128)(2,1)}, f32[16,32,128]{2,1,0:T(8,128)}) custom-call(bf16[4096,128]{1,0:T(8,128)(2,1)} %factors.1.factor_ref, f32[8,2048]{1,0:T(8,128)} %bitcast.45, bf16[32,32,128]{2,1,0:T(8,128)(2,1)} %copy-done.1, bf16[4096,2048]{1,0:T(8,128)(2,1)} %build.1.old_ref), custom_call_target="tpu_custom_call", output_to_operand_aliasing={{0}: (3, {})} | custom-call | tf_op jit(solution)/shard_map/finish/pallas_call | solution.py:216
  58.9 9.6 %all-to-all-start.2 = ((f32[16,32,128]{2,1,0:T(8,128)}), f32[16,32,128]{2,1,0:T(8,128)S(1)}, u32[]{:S(2)}, u32[]{:S(2)}) async-start(f32[16,32,128]{2,1,0:T(8,128)} %get-tuple-element.10), calls=%async_computation.2 | async-start | bytes 524288 | tf_op jit(solution)/shard_map/all_to_all | solution.py:305
  68.5 0.7 constant_dynamic-slice_fusion.1
  69.3 10.1 %all-to-all-done.2 = f32[16,32,128]{2,1,0:T(8,128)S(1)} async-done(((f32[16,32,128]{2,1,0:T(8,128)}), f32[16,32,128]{2,1,0:T(8,128)S(1)}, u32[]{:S(2)}, u32[]{:S(2)}) %all-to-all-start.2) | async-done | bytes 262176 | tf_op jit(solution)/shard_map/all_to_all | solution.py:305
  79.5 19.4 %all_to_all.35.moved_ref = bf16[32,32,128]{2,1,0:T(8,128)(2,1)} all-to-all(bf16[32,32,128]{2,1,0:T(8,128)(2,1)S(1)} %broadcast_in_dim.26), channel_id=1, replica_groups=mesh['row'=16,'col'=32] {'col'}, dimensions={0} | all-to-all | bytes 524288 | tf_op jit(solution)/shard_map/all_to_all | solution.py:26
  98.9 8.4 %apply.1 = f32[16,32,128]{2,1,0:T(8,128)} custom-call(bf16[32,32,128]{2,1,0:T(8,128)(2,1)} %all_to_all.35.moved_ref, bf16[4096,2048]{1,0:T(8,128)(2,1)} %get-tuple-element.11.tile_ref), custom_call_target="tpu_custom_call" | custom-call | tf_op jit(solution)/shard_map/apply/pallas_call | solution.py:266
  107.2 5.8 %all-to-all-start.4 = ((f32[16,32,128]{2,1,0:T(8,128)}), f32[16,32,128]{2,1,0:T(8,128)S(1)}, u32[]{:S(2)}, u32[]{:S(2)}) async-start(f32[16,32,128]{2,1,0:T(8,128)} %apply.1), calls=%async_computation.4 | async-start | bytes 524288 | tf_op jit(solution)/shard_map/all_to_all | solution.py:310
  113.0 1.4 fusion.36
  114.4 9.9 %all-to-all-done.4 = f32[16,32,128]{2,1,0:T(8,128)S(1)} async-done(((f32[16,32,128]{2,1,0:T(8,128)}), f32[16,32,128]{2,1,0:T(8,128)S(1)}, u32[]{:S(2)}, u32[]{:S(2)}) %all-to-all-start.4) | async-done | bytes 262176 | tf_op jit(solution)/shard_map/all_to_all | solution.py:310
  124.5 0.7 broadcast_in_dim.27
  125.2 0.7 broadcast_in_dim.28
  125.9 3.9 %all-to-all-start.5 = ((f32[32,8,128]{2,1,0:T(8,128)}), f32[32,8,128]{2,1,0:T(8,128)S(1)}, u32[]{:S(2)}, u32[]{:S(2)}) async-start(f32[32,8,128]{2,1,0:T(8,128)} %broadcast_in_dim.28), calls=%async_computation.5 | async-start | bytes 262144 | tf_op jit(solution)/shard_map/all_to_all | solution.py:330
  129.8 9.5 %all-to-all-done.5 = f32[32,8,128]{2,1,0:T(8,128)S(1)} async-done(((f32[32,8,128]{2,1,0:T(8,128)}), f32[32,8,128]{2,1,0:T(8,128)S(1)}, u32[]{:S(2)}, u32[]{:S(2)}) %all-to-all-start.5) | async-done | bytes 131104 | tf_op jit(solution)/shard_map/all_to_all | solution.py:330
  139.3 0.6 broadcast_in_dim.29
  139.9 5.8 %all-to-all-start.6 = ((f32[16,8,128]{2,1,0:T(8,128)}), f32[16,8,128]{2,1,0:T(8,128)S(1)}, u32[]{:S(2)}, u32[]{:S(2)}) async-start(f32[16,8,128]{2,1,0:T(8,128)} %broadcast_in_dim.29), calls=%async_computation.6 | async-start | bytes 131072 | tf_op jit(solution)/shard_map/all_to_all | solution.py:26
  145.8 4.6 %collective-permute-start = (f32[99,32]{1,0:T(8,128)S(1)}, f32[99,32]{1,0:T(8,128)S(1)}, u32[]{:S(2)}, u32[]{:S(2)}) collective-permute-start(f32[99,32]{1,0:T(8,128)S(1)} %get-tuple-element.26), channel_id=1, source_target_pairs={{1,0},{2,1},{3,2},{4,3},{5,4},{6,5},{7,6},{8,7},{9,8},{10,9},{11,1... | collective-permute-start | bytes 38024 | tf_op jit(solution)/shard_map/ppermute | solution.py:318
  150.4 1.9 %collective-permute-start.1 = (f32[99,32]{1,0:T(8,128)S(1)}, f32[99,32]{1,0:T(8,128)S(1)}, u32[]{:S(2)}, u32[]{:S(2)}) collective-permute-start(f32[99,32]{1,0:T(8,128)S(1)} %get-tuple-element.25), channel_id=1, source_target_pairs={{0,1},{1,2},{2,3},{3,4},{4,5},{5,6},{6,7},{7,8},{8,9},{9,10},{10,1... | collective-permute-start | bytes 38024 | tf_op jit(solution)/shard_map/ppermute | solution.py:317
  152.3 7.7 %collective-permute-done.1 = f32[99,32]{1,0:T(8,128)S(1)} collective-permute-done((f32[99,32]{1,0:T(8,128)S(1)}, f32[99,32]{1,0:T(8,128)S(1)}, u32[]{:S(2)}, u32[]{:S(2)}) %collective-permute-start.1) | collective-permute-done | bytes 12704 | tf_op jit(solution)/shard_map/ppermute | solution.py:317
  160.1 0.6 slice.115
  162.3 0.7 fusion.19
  (46 shorter events, 1.7 us)
Async XLA Ops:
  2.2 18.7 %all-to-all-start = ((f32[16,8,128]{2,1,0:T(8,128)}), f32[16,8,128]{2,1,0:T(8,128)S(1)}, u32[]{:S(2)}, u32[]{:S(2)}) async-start(f32[16,8,128]{2,1,0:T(8,128)} %broadcast_in_dim.22), calls=%async_computation | async-start | bytes 131072 | tf_op jit(solution)/shard_map/all_to_all | solution.py:26
  20.9 11.6 %copy-start.2 = (f32[16,8,128]{2,1,0:T(8,128)}, f32[16,8,128]{2,1,0:T(8,128)S(1)}, u32[]{:S(2)}) copy-start(f32[16,8,128]{2,1,0:T(8,128)S(1)} %all-to-all-done) | copy-start | bytes 196612
  21.6 23.0 %all-to-all-start.1 = ((bf16[32,32,128]{2,1,0:T(8,128)(2,1)}), bf16[32,32,128]{2,1,0:T(8,128)(2,1)S(1)}, u32[]{:S(2)}, u32[]{:S(2)}) async-start(bf16[32,32,128]{2,1,0:T(8,128)(2,1)} %broadcast_in_dim.23), calls=%async_computation.1 | async-start | bytes 524288 | tf_op jit(solution)/shard_map/all_to_all | solution.py:300
  32.5 36.7 %copy-start.4 = (f32[3,32]{1,0:T(4,128)S(1)}, f32[3,32]{1,0:T(4,128)}, u32[]{:S(2)}) copy-start(f32[3,32]{1,0:T(4,128)} %param.8) | copy-start | bytes 1156
  32.5 46.9 %copy-start.3 = (f32[32,128]{1,0:T(8,128)S(1)}, f32[32,128]{1,0:T(8,128)}, u32[]{:S(2)}) copy-start(f32[32,128]{1,0:T(8,128)} %param.9) | copy-start | bytes 49156
  44.7 0.7 copy-start.1
  58.9 20.5 %all-to-all-start.2 = ((f32[16,32,128]{2,1,0:T(8,128)}), f32[16,32,128]{2,1,0:T(8,128)S(1)}, u32[]{:S(2)}, u32[]{:S(2)}) async-start(f32[16,32,128]{2,1,0:T(8,128)} %get-tuple-element.10), calls=%async_computation.2 | async-start | bytes 524288 | tf_op jit(solution)/shard_map/all_to_all | solution.py:305
  107.2 17.1 %all-to-all-start.4 = ((f32[16,32,128]{2,1,0:T(8,128)}), f32[16,32,128]{2,1,0:T(8,128)S(1)}, u32[]{:S(2)}, u32[]{:S(2)}) async-start(f32[16,32,128]{2,1,0:T(8,128)} %apply.1), calls=%async_computation.4 | async-start | bytes 524288 | tf_op jit(solution)/shard_map/all_to_all | solution.py:310
  125.9 13.4 %all-to-all-start.5 = ((f32[32,8,128]{2,1,0:T(8,128)}), f32[32,8,128]{2,1,0:T(8,128)S(1)}, u32[]{:S(2)}, u32[]{:S(2)}) async-start(f32[32,8,128]{2,1,0:T(8,128)} %broadcast_in_dim.28), calls=%async_computation.5 | async-start | bytes 262144 | tf_op jit(solution)/shard_map/all_to_all | solution.py:330
  139.9 20.1 %all-to-all-start.6 = ((f32[16,8,128]{2,1,0:T(8,128)}), f32[16,8,128]{2,1,0:T(8,128)S(1)}, u32[]{:S(2)}, u32[]{:S(2)}) async-start(f32[16,8,128]{2,1,0:T(8,128)} %broadcast_in_dim.29), calls=%async_computation.6 | async-start | bytes 131072 | tf_op jit(solution)/shard_map/all_to_all | solution.py:26
  145.8 6.5 %collective-permute-start = (f32[99,32]{1,0:T(8,128)S(1)}, f32[99,32]{1,0:T(8,128)S(1)}, u32[]{:S(2)}, u32[]{:S(2)}) collective-permute-start(f32[99,32]{1,0:T(8,128)S(1)} %get-tuple-element.26), channel_id=1, source_target_pairs={{1,0},{2,1},{3,2},{4,3},{5,4},{6,5},{7,6},{8,7},{9,8},{10,9},{11,1... | collective-permute-start | bytes 38024 | tf_op jit(solution)/shard_map/ppermute | solution.py:318
  150.4 9.7 %collective-permute-start.1 = (f32[99,32]{1,0:T(8,128)S(1)}, f32[99,32]{1,0:T(8,128)S(1)}, u32[]{:S(2)}, u32[]{:S(2)}) collective-permute-start(f32[99,32]{1,0:T(8,128)S(1)} %get-tuple-element.25), channel_id=1, source_target_pairs={{0,1},{1,2},{2,3},{3,4},{4,5},{5,6},{6,7},{7,8},{8,9},{9,10},{10,1... | collective-permute-start | bytes 38024 | tf_op jit(solution)/shard_map/ppermute | solution.py:317
  161.5 1.5 copy-start

commit v4 on v3

--- a/solution.py
+++ b/solution.py
@@ -19,6 +19,8 @@
 STEP = 256
 BLOCK = 512
 VMEM_BYTES = 58 << 20
+FINISH_BYTES = 50 << 20
+SMALL_BYTES = 4 << 20
 
 
 def spread(block, axis, count):
@@ -33,12 +35,15 @@
     return high, middle, rest - middle
 
 
-def factor_kernel(place_ref, normal_ref, factor_ref):
-    place = place_ref[...]
-    scaled = normal_ref[...] * (place[3:4, :] * INV_FOUR_PI)
-    level = -jnp.sum(scaled * place, axis=0, keepdims=True)
-    at_level = lax.broadcasted_iota(jnp.int32, place.shape, 0) == 3
-    high, middle, low = three(jnp.where(at_level, level, scaled))
+def factor_kernel(center_ref, normal_ref, area_ref, factor_ref):
+    width = center_ref.shape[1]
+    blank = jnp.zeros((4, width), jnp.float32)
+    area = area_ref[...]
+    place = jnp.concatenate([center_ref[...], area, blank], axis=0)
+    scaled = normal_ref[...] * (area * INV_FOUR_PI)
+    level = -jnp.sum(scaled * center_ref[...], axis=0, keepdims=True)
+    high, middle, low = three(jnp.concatenate([scaled, level, blank], axis=0))
+    at_level = lax.broadcasted_iota(jnp.int32, high.shape, 0) == 3
     bare = jnp.where(at_level, 0.0, high)
     bare_middle = jnp.where(at_level, 0.0, middle)
     none = jnp.zeros_like(high)
@@ -47,19 +52,23 @@
     factor_ref[...] = jnp.concatenate(rows, axis=0).T.astype(jnp.bfloat16)
 
 
-def source_factors(place, normal):
-    count = place.shape[1]
+def source_factors(centers, normals, areas, block=1024):
+    count = centers.shape[1]
     return pl.pallas_call(
         factor_kernel,
-        grid=(count // BLOCK,),
-        in_specs=[pl.BlockSpec((8, BLOCK), lambda i: (0, i))] * 2,
-        out_specs=pl.BlockSpec((BLOCK, LANES), lambda i: (i, 0)),
+        grid=(count // block,),
+        in_specs=[
+            pl.BlockSpec((3, block), lambda i: (0, i)),
+            pl.BlockSpec((3, block), lambda i: (0, i)),
+            pl.BlockSpec((1, block), lambda i: (0, i)),
+        ],
+        out_specs=pl.BlockSpec((block, LANES), lambda i: (i, 0)),
         out_shape=jax.ShapeDtypeStruct((count, LANES), jnp.bfloat16),
         cost_estimate=pl.CostEstimate(
             flops=count * 400, bytes_accessed=count * 320, transcendentals=0
         ),
         name="factors",
-    )(place, normal)
+    )(centers, normals, areas[None, :])
 
 
 def target_factors(targets):
@@ -238,7 +247,7 @@
             pltpu.VMEM((BLOCK, width), jnp.bfloat16),
         ],
         input_output_aliases={3: 0},
-        compiler_params=pltpu.CompilerParams(vmem_limit_bytes=VMEM_BYTES),
+        compiler_params=pltpu.CompilerParams(vmem_limit_bytes=FINISH_BYTES),
         name="finish",
     )(factors, targets, moved, tile)
 
@@ -275,6 +284,148 @@
         compiler_params=pltpu.CompilerParams(vmem_limit_bytes=VMEM_BYTES),
         name="apply",
     )(moved, tile)
+
+
+def residual_kernel(part_ref, base_ref, residual_ref, sent_ref):
+    residual = base_ref[...] - jnp.sum(part_ref[...], axis=0)
+    residual_ref[...] = residual
+    sent = residual.astype(jnp.bfloat16)
+    for device in range(sent_ref.shape[0]):
+        sent_ref[device] = sent
+
+
+def residual_of(parts, base, devices):
+    return pl.pallas_call(
+        residual_kernel,
+        in_specs=[WHOLE] * 2,
+        out_specs=[WHOLE] * 2,
+        out_shape=[
+            jax.ShapeDtypeStruct(base.shape, jnp.float32),
+            jax.ShapeDtypeStruct((devices,) + base.shape, jnp.bfloat16),
+        ],
+        compiler_params=pltpu.CompilerParams(vmem_limit_bytes=SMALL_BYTES),
+        name="residual",
+    )(parts, base)
+
+
+def sums_kernel(part_ref, start_ref, residual_ref, center_ref, area_ref, field_ref, sent_ref):
+    change = jnp.sum(part_ref[...], axis=0)
+    residual = residual_ref[...]
+    count = residual.shape[0]
+    field_ref[:count] = start_ref[...]
+    field_ref[count : 2 * count] = residual
+    field_ref[2 * count : 3 * count] = change
+    field_ref[3 * count :] = center_ref[...]
+    area = jnp.broadcast_to(area_ref[...], residual.shape)
+    weighted = area * residual
+    terms = [weighted * residual, weighted * change, area * change * change, area]
+    total = jnp.sum(jnp.concatenate(terms, axis=0).T, axis=0, keepdims=True)
+    sent = jnp.broadcast_to(total, sent_ref.shape[1:])
+    for device in range(sent_ref.shape[0]):
+        sent_ref[device] = sent
+
+
+def sums_of(parts, start, residual, centers, areas, devices):
+    count, own = start.shape
+    return pl.pallas_call(
+        sums_kernel,
+        in_specs=[WHOLE] * 5,
+        out_specs=[WHOLE] * 2,
+        out_shape=[
+            jax.ShapeDtypeStruct((3 * count + 8, own), jnp.float32),
+            jax.ShapeDtypeStruct((devices, 8, 4 * count), jnp.float32),
+        ],
+        compiler_params=pltpu.CompilerParams(vmem_limit_bytes=SMALL_BYTES),
+        name="sums",
+    )(parts, start, residual, centers, areas)
+
+
+def regroup_kernel(part_ref, sent_ref):
+    sent = jnp.sum(part_ref[...], axis=0)
+    for device in range(sent_ref.shape[0]):
+        sent_ref[device] = sent
+
+
+def regroup(parts, devices):
+    return pl.pallas_call(
+        regroup_kernel,
+        in_specs=[WHOLE],
+        out_specs=WHOLE,
+        out_shape=jax.ShapeDtypeStruct((devices,) + parts.shape[1:], jnp.float32),
+        compiler_params=pltpu.CompilerParams(vmem_limit_bytes=SMALL_BYTES),
+        name="regroup",
+    )(parts)
+
+
+def last_kernel(
+    part_ref, field_ref, before_ref, after_ref, onset_ref, end_ref, state_ref, pressure_ref
+):
+    count, own = state_ref.shape
+    total = jnp.sum(part_ref[...], axis=0)[0:1, :]
+    total = jnp.broadcast_to(total, (4 * count, own)).T
+    both, mixed, changed, area = (total[i * count : (i + 1) * count] for i in range(4))
+    reach = CAP * jnp.sqrt(area)
+
+    def damp(sums):
+        return OMEGA * jnp.minimum(1.0, reach * lax.rsqrt(sums + EPS))
+
+    one = damp(both)
+    keep = 1.0 - 0.5 * one
+    sums = keep * keep * both - 2.0 * keep * one * mixed + one * one * changed
+    two = damp(jnp.maximum(sums, 0.0))
+    on_residual = one + two * keep
+    on_change = two * one
+
+    def strengths(ref):
+        value = ref[:count] + on_residual * ref[count : 2 * count]
+        return value - on_change * ref[2 * count : 3 * count]
+
+    state = strengths(field_ref)
+    state_ref[...] = state
+
+    def differences(middle, low, high):
+        lane = lax.broadcasted_iota(jnp.int32, middle.shape, 1)
+        is_first = jnp.broadcast_to(end_ref[0], middle.shape) == 1
+        is_last = jnp.broadcast_to(end_ref[1], middle.shape) == 1
+        low = jnp.where(is_first, middle, pltpu.roll(low, PB, 1))
+        high = jnp.where(is_last, middle, pltpu.roll(high, own - PB, 1))
+        lower = jnp.where(lane < PB, low, pltpu.roll(middle, PB, 1))
+        upper = jnp.where(lane >= own - PB, high, pltpu.roll(middle, own - PB, 1))
+        around = lane % PB
+        following = jnp.where(
+            around == PB - 1, pltpu.roll(middle, PB - 1, 1), pltpu.roll(middle, own - 1, 1)
+        )
+        preceding = jnp.where(
+            around == 0, pltpu.roll(middle, own - PB + 1, 1), pltpu.roll(middle, 1, 1)
+        )
+        return upper - lower, following - preceding
+
+    steps = differences(field_ref[3 * count :], before_ref[3 * count :], after_ref[3 * count :])
+    changes = differences(state, strengths(before_ref), strengths(after_ref))
+    pressure = jnp.ones_like(state)
+    for step, change in zip(steps, changes):
+        span = jnp.sqrt(jnp.sum(step * step, axis=0, keepdims=True))
+        along = onset_ref[:, 0:1] * step[0:1]
+        along += onset_ref[:, 1:2] * step[1:2]
+        along += onset_ref[:, 2:3] * step[2:3]
+        speed = along / span - change / span
+        pressure -= speed * speed
+    pressure_ref[...] = pressure
+
+
+def last(parts, fields, before, after, onset, ends, count):
+    own = fields.shape[1]
+    return pl.pallas_call(
+        last_kernel,
+        in_specs=[WHOLE] * 5 + [pl.BlockSpec(memory_space=pltpu.SMEM)],
+        out_specs=[WHOLE] * 2,
+        out_shape=[jax.ShapeDtypeStruct((count, own), jnp.float32)] * 2,
+        compiler_params=pltpu.CompilerParams(vmem_limit_bytes=SMALL_BYTES),
+        name="last",
+    )(parts, fields, before, after, onset, ends)
+
+
+WHOLE = pl.BlockSpec(memory_space=pltpu.VMEM)
 
 
 def per_device(centers, normals, areas, onset, start):
@@ -293,8 +444,7 @@
     note = jnp.concatenate([own_centers, mark.astype(jnp.float32)], axis=0)
     notes = spread(note, "row", row_count)
     shown = jnp.broadcast_to(start.astype(jnp.bfloat16)[None], (col_count, count, own))
-    place = jnp.concatenate([centers, areas[None, :], jnp.zeros((4, areas.shape[0]))], axis=0)
-    factors = source_factors(place, jnp.pad(normals, ((0, 5), (0, 0))))
+    factors = source_factors(centers, normals, areas)
     notes, shown, factors = lax.optimization_barrier((notes, shown, factors))
     targets = jnp.transpose(notes, (1, 0, 2)).reshape(8, row_count * own)
     moved = lax.all_to_all(shown, "col", 0, 0, tiled=True)
@@ -302,71 +452,27 @@
     tile = build(factors, targets)
     tile, partial = finish_build(factors, targets, moved, tile)
 
-    product = jnp.sum(lax.all_to_all(partial, "row", 0, 0, tiled=True), axis=0)
     right = -jnp.sum(onset[:, :, None] * own_normals[:, None, :], axis=0)
-    residual = right - 0.5 * start - product
-    gathered = spread(residual.astype(jnp.bfloat16), "col", col_count)
+    base = right - 0.5 * start
+    parts = lax.all_to_all(partial, "row", 0, 0, tiled=True)
+    residual, sent = residual_of(parts, base, col_count)
+    gathered = lax.all_to_all(sent, "col", 0, 0, tiled=True)
     partial = apply(gathered, tile)
-    change = jnp.sum(lax.all_to_all(partial, "row", 0, 0, tiled=True), axis=0)
+    parts = lax.all_to_all(partial, "row", 0, 0, tiled=True)
+    here = jnp.pad(own_centers, ((0, 5), (0, 0)))
+    fields, sent = sums_of(parts, start, residual, here, own_areas[None, :], col_count)
 
     flat = row_index * col_count + col_index
     devices = row_count * col_count
-    edges = jnp.concatenate([start, residual, change, own_centers], axis=0)
     forward = [(i, i + 1) for i in range(devices - 1)]
     backward = [(i + 1, i) for i in range(devices - 1)]
-    before = lax.ppermute(edges[:, own - PB :], ("row", "col"), forward)
-    after = lax.ppermute(edges[:, :PB], ("row", "col"), backward)
-
-    weighted = own_areas[None, :] * residual
-    part = jnp.concatenate(
-        [
-            jnp.sum(weighted * residual, axis=1),
-            jnp.sum(weighted * change, axis=1),
-            jnp.sum(own_areas[None, :] * change * change, axis=1),
-            jnp.broadcast_to(jnp.sum(own_areas), (count,)),
-        ]
-    )
-    part = jnp.broadcast_to(part[None, None], (col_count, 8, 4 * count))
-    part = jnp.sum(lax.all_to_all(part, "col", 0, 0, tiled=True), axis=0)
-    part = jnp.sum(spread(part, "row", row_count), axis=0)[0]
-    both = part[:count]
-    mixed = part[count : 2 * count]
-    changed = part[2 * count : 3 * count]
-    reach = CAP * jnp.sqrt(part[3 * count])
-
-    def damp(sums):
-        return OMEGA * jnp.minimum(1.0, reach * lax.rsqrt(sums + EPS))
-
-    one = damp(both)
-    keep = 1.0 - 0.5 * one
-    sums = keep * keep * both - 2.0 * keep * one * mixed + one * one * changed
-    two = damp(jnp.maximum(sums, 0.0))
-    on_residual = (one + two * keep)[:, None]
-    on_change = (two * one)[:, None]
-
-    def finish(edge):
-        strengths = edge[:count] + on_residual * edge[count : 2 * count]
-        strengths = strengths - on_change * edge[2 * count : 3 * count]
-        return jnp.concatenate([strengths, edge[3 * count :]], axis=0)
-
-    fields = finish(edges)
-    state = fields[:count]
-    before = jnp.where(flat == 0, fields[:, :PB], finish(before))
-    after = jnp.where(flat == devices - 1, fields[:, own - PB :], finish(after))
-    padded = jnp.concatenate([before, fields, after], axis=1)
-    diff_a = padded[:, 2 * PB :] - padded[:, :own]
-    lane = lax.broadcasted_iota(jnp.int32, fields.shape, 1) % PB
-    following = jnp.where(lane == PB - 1, jnp.roll(fields, PB - 1, 1), jnp.roll(fields, -1, 1))
-    preceding = jnp.where(lane == 0, jnp.roll(fields, 1 - PB, 1), jnp.roll(fields, 1, 1))
-    diff_b = following - preceding
-    speeds = []
-    for diff in (diff_a, diff_b):
-        step = diff[count:]
-        span = jnp.sqrt(jnp.sum(step * step, axis=0))
-        along = jnp.sum(onset[:, :, None] * step[:, None, :], axis=0)
-        speeds.append(along / span - diff[:count] / span)
-    pressure = 1.0 - speeds[0] * speeds[0] - speeds[1] * speeds[1]
-    return (state, pressure)
+    parts = lax.all_to_all(sent, "col", 0, 0, tiled=True)
+    before = lax.ppermute(fields, ("row", "col"), forward)
+    after = lax.ppermute(fields, ("row", "col"), backward)
+    parts, before, after = lax.optimization_barrier((parts, before, after))
+    parts = lax.all_to_all(regroup(parts, row_count), "row", 0, 0, tiled=True)
+    ends = jnp.stack([flat == 0, flat == devices - 1]).astype(jnp.int32)
+    return last(parts, fields, before, after, onset.T, ends, count)
 
 
 def solution(mesh):

time: 164 us -> 153 us (0.933)
  blocking collectives: 19.4 us -> 36.4 us
  waiting for transfers between devices: 38.6 us -> 24.7 us
  starting transfers between devices: 52.4 us -> 44.8 us
  other arithmetic: 5.78 us -> 1.8 us
  local copies, waits for them, and re-layouts: 7.79 us -> 3.93 us
    all_to_all x1 -> x2, blocking collectives: 19.4 us -> 36.4 us  [the longest x1 19.4 us: per_device(): gathered = lax.all_to_all(sent, 'col', 0, 0, tiled=True)]
    all_to_all x3, waiting for transfers between devices: 29.5 us -> 18.4 us  [the longest x1 10.5 us: per_device(): parts = lax.all_to_all(partial, 'row', 0, 0, tiled=True)]
    ppermute x2, waiting for transfers between devices: 7.7 us -> 1.76 us  [the longest x1 1.76 us: per_device(): after = lax.ppermute(fields, ('row', 'col'), backward)]
    all_to_all x2 -> x1, starting transfers between devices: 15.8 us -> 10.1 us  [spread(): return lax.all_to_all(copies, axis, 0, 0, tiled=True)]
    all_to_all x3, starting transfers between devices: 19.3 us -> 14.2 us  [the longest x1 5.77 us: per_device(): parts = lax.all_to_all(partial, 'row', 0, 0, tiled=True)]
    ppermute x2, starting transfers between devices: 6.48 us -> 9.78 us  [the longest x1 7.71 us: per_device(): after = lax.ppermute(fields, ('row', 'col'), backward)]
    all_to_all x2 -> x1, waiting for transfers between devices: 0.01 us -> 3.21 us  [spread(): return lax.all_to_all(copies, axis, 0, 0, tiled=True)]
    concatenate x8 -> x0, other arithmetic: 2.04 us -> none  [the longest x1 1.57 us: per_device(): jnp.concatenate([centers, areas[None, :], jnp.zeros((4, areas.shape[0]))]...]
  transfers between devices with their start and end apart: 8 -> 7, of which waited for: 5 -> 5; matrix products, arithmetic and copies ran while one was open for 4% -> 2% of each run, Pallas kernels for 10% -> 9%
where the time goes in v4:
time: 153 us; the launch traced here: 151 us
  starting transfers between devices  44.8 us (29%)
  Pallas kernels  38.7 us (25%)
  blocking collectives  36.4 us (24%)
  waiting for transfers between devices  24.7 us (16%)
  local copies, waits for them, and re-layouts  3.93 us (3%)
  other arithmetic  1.8 us (1%)
    all_to_all x1, blocking collectives, per_device(): gathered = lax.all_to_all(sent, 'col', 0, 0, tiled=True)  19.4 us
    all_to_all x1, blocking collectives, per_device(): parts = lax.all_to_all(partial, 'row', 0, 0, tiled=True)  17 us
    pallas_call x1, Pallas kernels, finish_build(): pl.pallas_call(finish_kernel, grid=(blocks + 1,), in_specs=[pl.BlockSpec(...  13.4 us
    all_to_all x1, starting transfers between devices, per_device(): moved = lax.all_to_all(shown, 'col', 0, 0, tiled=True)  10.8 us
    pallas_call x1, Pallas kernels, build(): pl.pallas_call(build_kernel, grid=(count // BLOCK // 2,), in_specs=[pl.Bl...  10.8 us
    all_to_all x1, waiting for transfers between devices, per_device(): parts = lax.all_to_all(partial, 'row', 0, 0, tiled=True)  10.5 us
    all_to_all x1, starting transfers between devices, spread(): return lax.all_to_all(copies, axis, 0, 0, tiled=True)  10.1 us
    pallas_call x1, Pallas kernels, apply(): pl.pallas_call(apply_kernel, grid=(count // depth,), in_specs=[pl.BlockSp...  8.37 us
  transfers between devices with their start and end apart: 7, of which 5 were waited for; matrix products, arithmetic and copies ran while one was open for 2% of the time, Pallas kernels for 9%

profile of v4, /device:TPU:6, one launch (start us, length us, event | category | flops | bytes accessed | tf_op | source)
XLA Modules:
  0.0 151.1 jit_solution(16002946731834858040)
XLA Ops:
  0.6 0.1 pad.9.clone
  0.8 0.7 constant_dynamic-slice_fusion
  1.5 0.1 fusion
  1.6 0.6 broadcast_in_dim.28
  2.2 10.1 %all-to-all-start = ((f32[16,8,128]{2,1,0:T(8,128)}), f32[16,8,128]{2,1,0:T(8,128)S(1)}, u32[]{:S(2)}, u32[]{:S(2)}) async-start(f32[16,8,128]{2,1,0:T(8,128)} %broadcast_in_dim.28), calls=%async_computation | async-start | bytes 131072 | tf_op jit(solution)/shard_map/all_to_all | solution.py:28
  12.2 3.2 %factors.1.factor_ref = bf16[4096,128]{1,0:T(8,128)(2,1)} custom-call(f32[3,4096]{1,0:T(4,128)} %center_ref.1, f32[3,4096]{1,0:T(4,128)} %normal_ref.1, f32[1,4096]{1,0:T(1,128)} %bitcast.13), custom_call_target="tpu_custom_call" | custom-call | flops 1638400 | bytes 1310720 | tf_op jit(solution)/shard_map/factors/pallas_call | solution.py:57
  15.4 0.8 multiply_reduce_fusion
  16.3 0.8 multiply_subtract_fusion
  17.1 3.2 %all-to-all-done = f32[16,8,128]{2,1,0:T(8,128)S(1)} async-done(((f32[16,8,128]{2,1,0:T(8,128)}), f32[16,8,128]{2,1,0:T(8,128)S(1)}, u32[]{:S(2)}, u32[]{:S(2)}) %all-to-all-start) | async-done | bytes 65568 | tf_op jit(solution)/shard_map/all_to_all | solution.py:28
  20.3 0.8 broadcast_in_dim.29
  21.1 10.8 %all-to-all-start.1 = ((bf16[32,32,128]{2,1,0:T(8,128)(2,1)}), bf16[32,32,128]{2,1,0:T(8,128)(2,1)S(1)}, u32[]{:S(2)}, u32[]{:S(2)}) async-start(bf16[32,32,128]{2,1,0:T(8,128)(2,1)} %broadcast_in_dim.29), calls=%async_computation.1 | async-start | bytes 524288 | tf_op jit(solution)/shard_map/all_to_all | solution.py:450
  31.9 10.8 %build.1.old_ref = bf16[4096,2048]{1,0:T(8,128)(2,1)} custom-call(bf16[4096,128]{1,0:T(8,128)(2,1)} %factors.1.factor_ref, f32[8,2048]{1,0:T(8,128)} %bitcast.10), custom_call_target="tpu_custom_call" | custom-call | flops 419430400 | bytes 8388608 | tf_op jit(solution)/shard_map/build/pallas_call | solution.py:199
  42.7 1.4 all-to-all-done.1.moved_ref
  44.1 0.8 copy-done.2
  45.0 13.4 %finish.1 = (bf16[4096,2048]{1,0:T(8,128)(2,1)}, f32[16,32,128]{2,1,0:T(8,128)S(1)}) custom-call(bf16[4096,128]{1,0:T(8,128)(2,1)S(1)} %copy-done, f32[8,2048]{1,0:T(8,128)S(1)} %bitcast.11, bf16[32,32,128]{2,1,0:T(8,128)(2,1)S(1)} %all-to-all-done.1.moved_ref, bf16[4096,2048]{1,0:T(8,128)(2,1)} %build.1.old_ref), custom_call_target="tpu_custom_call", output_to_operand_aliasing={{0}: (3, {})} | custom-call | tf_op jit(solution)/shard_map/finish/pallas_call | solution.py:225
  58.4 17.0 %all_to_all.35.part_ref = f32[16,32,128]{2,1,0:T(8,128)S(1)} all-to-all(f32[16,32,128]{2,1,0:T(8,128)S(1)} %get-tuple-element.17), channel_id=1, replica_groups=mesh['row'=16,'col'=32] {'row'}, dimensions={0} | all-to-all | bytes 524288 | tf_op jit(solution)/shard_map/all_to_all | solution.py:457
  75.4 19.4 %all_to_all.36.moved_ref = bf16[32,32,128]{2,1,0:T(8,128)(2,1)} all-to-all(bf16[32,32,128]{2,1,0:T(8,128)(2,1)S(1)} %get-tuple-element.18), channel_id=1, replica_groups=mesh['row'=16,'col'=32] {'col'}, dimensions={0} | all-to-all | bytes 524288 | tf_op jit(solution)/shard_map/all_to_all | solution.py:459
  94.9 8.4 %apply.1 = f32[16,32,128]{2,1,0:T(8,128)} custom-call(bf16[32,32,128]{2,1,0:T(8,128)(2,1)} %all_to_all.36.moved_ref, bf16[4096,2048]{1,0:T(8,128)(2,1)} %get-tuple-element.19.tile_ref), custom_call_target="tpu_custom_call" | custom-call | tf_op jit(solution)/shard_map/apply/pallas_call | solution.py:275
  103.2 5.8 %all-to-all-start.4 = ((f32[16,32,128]{2,1,0:T(8,128)}), f32[16,32,128]{2,1,0:T(8,128)S(1)}, u32[]{:S(2)}, u32[]{:S(2)}) async-start(f32[16,32,128]{2,1,0:T(8,128)} %apply.1), calls=%async_computation.4 | async-start | bytes 524288 | tf_op jit(solution)/shard_map/all_to_all | solution.py:461
  109.0 0.8 dynamic-slice_bitcast_fusion.area_ref
  109.8 10.5 %all-to-all-done.4.part_ref = f32[16,32,128]{2,1,0:T(8,128)S(1)} async-done(((f32[16,32,128]{2,1,0:T(8,128)}), f32[16,32,128]{2,1,0:T(8,128)S(1)}, u32[]{:S(2)}, u32[]{:S(2)}) %all-to-all-start.4) | async-done | bytes 262176 | tf_op jit(solution)/shard_map/all_to_all | solution.py:461
  120.3 0.8 sums.1
  121.1 3.9 %all-to-all-start.5 = ((f32[32,8,128]{2,1,0:T(8,128)}), f32[32,8,128]{2,1,0:T(8,128)S(1)}, u32[]{:S(2)}, u32[]{:S(2)}) async-start(f32[32,8,128]{2,1,0:T(8,128)} %get-tuple-element.21), calls=%async_computation.5 | async-start | bytes 262144 | tf_op jit(solution)/shard_map/all_to_all | solution.py:469
  124.9 2.1 %collective-permute-start = (f32[104,128]{1,0:T(8,128)S(1)}, f32[104,128]{1,0:T(8,128)S(1)}, u32[]{:S(2)}, u32[]{:S(2)}) collective-permute-start(f32[104,128]{1,0:T(8,128)S(1)} %get-tuple-element.22.field_ref), channel_id=1, source_target_pairs={{0,1},{1,2},{2,3},{3,4},{4,5},{5,6},{6,7},{7,8},{8,9},{9,10},{10,1... | collective-permute-start | bytes 159752 | tf_op jit(solution)/shard_map/ppermute | solution.py:470
  127.0 7.7 %collective-permute-start.1 = (f32[104,128]{1,0:T(8,128)S(1)}, f32[104,128]{1,0:T(8,128)S(1)}, u32[]{:S(2)}, u32[]{:S(2)}) collective-permute-start(f32[104,128]{1,0:T(8,128)S(1)} %get-tuple-element.22.field_ref), channel_id=1, source_target_pairs={{1,0},{2,1},{3,2},{4,3},{5,4},{6,5},{7,6},{8,7},{9,8},{10,9},{11,1... | collective-permute-start | bytes 159752 | tf_op jit(solution)/shard_map/ppermute | solution.py:471
  134.7 1.8 %collective-permute-done.1.after_ref = f32[104,128]{1,0:T(8,128)S(1)} collective-permute-done((f32[104,128]{1,0:T(8,128)S(1)}, f32[104,128]{1,0:T(8,128)S(1)}, u32[]{:S(2)}, u32[]{:S(2)}) %collective-permute-start.1) | collective-permute-done | bytes 53280 | tf_op jit(solution)/shard_map/ppermute | solution.py:471
  136.5 0.6 regroup.1
  137.1 4.5 %all-to-all-start.6 = ((f32[16,8,128]{2,1,0:T(8,128)}), f32[16,8,128]{2,1,0:T(8,128)S(1)}, u32[]{:S(2)}, u32[]{:S(2)}) async-start(f32[16,8,128]{2,1,0:T(8,128)} %regroup.1), calls=%async_computation.6 | async-start | bytes 131072 | tf_op jit(solution)/shard_map/all_to_all | solution.py:473
  141.7 0.1 copy.9
  141.8 0.1 add_convert_fusion.end_ref
  141.8 7.9 %all-to-all-done.6.part_ref = f32[16,8,128]{2,1,0:T(8,128)S(1)} async-done(((f32[16,8,128]{2,1,0:T(8,128)}), f32[16,8,128]{2,1,0:T(8,128)S(1)}, u32[]{:S(2)}, u32[]{:S(2)}) %all-to-all-start.6) | async-done | bytes 65568 | tf_op jit(solution)/shard_map/all_to_all | solution.py:473
  149.7 1.4 last.1
  (14 shorter events, 0.1 us)
Async XLA Ops:
  2.2 18.1 %all-to-all-start = ((f32[16,8,128]{2,1,0:T(8,128)}), f32[16,8,128]{2,1,0:T(8,128)S(1)}, u32[]{:S(2)}, u32[]{:S(2)}) async-start(f32[16,8,128]{2,1,0:T(8,128)} %broadcast_in_dim.28), calls=%async_computation | async-start | bytes 131072 | tf_op jit(solution)/shard_map/all_to_all | solution.py:28
  15.4 28.7 %copy-start = (bf16[4096,128]{1,0:T(8,128)(2,1)S(1)}, bf16[4096,128]{1,0:T(8,128)(2,1)}, u32[]{:S(2)}) copy-start(bf16[4096,128]{1,0:T(8,128)(2,1)} %factors.1.factor_ref) | copy-start | bytes 3145732
  20.3 11.6 %copy-start.1 = (f32[16,8,128]{2,1,0:T(8,128)}, f32[16,8,128]{2,1,0:T(8,128)S(1)}, u32[]{:S(2)}) copy-start(f32[16,8,128]{2,1,0:T(8,128)S(1)} %all-to-all-done) | copy-start | bytes 196612
  21.1 23.1 %all-to-all-start.1 = ((bf16[32,32,128]{2,1,0:T(8,128)(2,1)}), bf16[32,32,128]{2,1,0:T(8,128)(2,1)S(1)}, u32[]{:S(2)}, u32[]{:S(2)}) async-start(bf16[32,32,128]{2,1,0:T(8,128)(2,1)} %broadcast_in_dim.29), calls=%async_computation.1 | async-start | bytes 524288 | tf_op jit(solution)/shard_map/all_to_all | solution.py:450
  44.1 0.8 copy-start.2
  45.0 75.3 %copy-start.3 = (f32[32,128]{1,0:T(8,128)S(1)}, f32[32,128]{1,0:T(8,128)}, u32[]{:S(2)}) copy-start(f32[32,128]{1,0:T(8,128)} %start_ref.1) | copy-start | bytes 49156
  45.0 96.7 %copy-start.4 = (f32[3,32]{1,0:T(4,128)S(1)}, f32[3,32]{1,0:T(4,128)}, u32[]{:S(2)}) copy-start(f32[3,32]{1,0:T(4,128)} %param.8) | copy-start | bytes 1156
  103.2 17.1 %all-to-all-start.4 = ((f32[16,32,128]{2,1,0:T(8,128)}), f32[16,32,128]{2,1,0:T(8,128)S(1)}, u32[]{:S(2)}, u32[]{:S(2)}) async-start(f32[16,32,128]{2,1,0:T(8,128)} %apply.1), calls=%async_computation.4 | async-start | bytes 524288 | tf_op jit(solution)/shard_map/all_to_all | solution.py:461
  121.1 15.4 %all-to-all-start.5 = ((f32[32,8,128]{2,1,0:T(8,128)}), f32[32,8,128]{2,1,0:T(8,128)S(1)}, u32[]{:S(2)}, u32[]{:S(2)}) async-start(f32[32,8,128]{2,1,0:T(8,128)} %get-tuple-element.21), calls=%async_computation.5 | async-start | bytes 262144 | tf_op jit(solution)/shard_map/all_to_all | solution.py:469
  124.9 9.8 %collective-permute-start = (f32[104,128]{1,0:T(8,128)S(1)}, f32[104,128]{1,0:T(8,128)S(1)}, u32[]{:S(2)}, u32[]{:S(2)}) collective-permute-start(f32[104,128]{1,0:T(8,128)S(1)} %get-tuple-element.22.field_ref), channel_id=1, source_target_pairs={{0,1},{1,2},{2,3},{3,4},{4,5},{5,6},{6,7},{7,8},{8,9},{9,10},{10,1... | collective-permute-start | bytes 159752 | tf_op jit(solution)/shard_map/ppermute | solution.py:470
  127.0 9.5 %collective-permute-start.1 = (f32[104,128]{1,0:T(8,128)S(1)}, f32[104,128]{1,0:T(8,128)S(1)}, u32[]{:S(2)}, u32[]{:S(2)}) collective-permute-start(f32[104,128]{1,0:T(8,128)S(1)} %get-tuple-element.22.field_ref), channel_id=1, source_target_pairs={{1,0},{2,1},{3,2},{4,3},{5,4},{6,5},{7,6},{8,7},{9,8},{10,9},{11,1... | collective-permute-start | bytes 159752 | tf_op jit(solution)/shard_map/ppermute | solution.py:471
  137.1 12.6 %all-to-all-start.6 = ((f32[16,8,128]{2,1,0:T(8,128)}), f32[16,8,128]{2,1,0:T(8,128)S(1)}, u32[]{:S(2)}, u32[]{:S(2)}) async-start(f32[16,8,128]{2,1,0:T(8,128)} %regroup.1), calls=%async_computation.6 | async-start | bytes 131072 | tf_op jit(solution)/shard_map/all_to_all | solution.py:473

commit v5 on v4

--- a/solution.py
+++ b/solution.py
@@ -17,15 +17,12 @@
 EPS = 1e-06
 LANES = 128
 STEP = 256
+SIDES = 2
+CORES = 2
 BLOCK = 512
 VMEM_BYTES = 58 << 20
 FINISH_BYTES = 50 << 20
 SMALL_BYTES = 4 << 20
-
-
-def spread(block, axis, count):
-    copies = jnp.broadcast_to(block[None], (count,) + block.shape)
-    return lax.all_to_all(copies, axis, 0, 0, tiled=True)
 
 
 def three(value):
@@ -35,40 +32,51 @@
     return high, middle, rest - middle
 
 
-def factor_kernel(center_ref, normal_ref, area_ref, factor_ref):
-    width = center_ref.shape[1]
-    blank = jnp.zeros((4, width), jnp.float32)
-    area = area_ref[...]
-    place = jnp.concatenate([center_ref[...], area, blank], axis=0)
-    scaled = normal_ref[...] * (area * INV_FOUR_PI)
-    level = -jnp.sum(scaled * center_ref[...], axis=0, keepdims=True)
-    high, middle, low = three(jnp.concatenate([scaled, level, blank], axis=0))
-    at_level = lax.broadcasted_iota(jnp.int32, high.shape, 0) == 3
-    bare = jnp.where(at_level, 0.0, high)
-    bare_middle = jnp.where(at_level, 0.0, middle)
+def note_kernel(at_ref, *refs):
+    note_ref = refs[-1]
+    halves = []
+    for center_ref, normal_ref, area_ref in zip(refs[0:2], refs[2:4], refs[4:6]):
+        center, area = center_ref[...], area_ref[...]
+        scaled = normal_ref[...] * (area * INV_FOUR_PI)
+        level = -jnp.sum(scaled * center, axis=0, keepdims=True)
+        halves.append(jnp.concatenate([center, area, scaled, level], axis=0))
+    note = jnp.concatenate(halves, axis=1)
+    for device in range(note_ref.shape[0]):
+        note_ref[device] = note
+
+
+def notes_of(starts, centers, normals, areas, devices):
+    def specs(rows):
+        return [
+            pl.BlockSpec((rows, LANES), lambda i, at, which=which: (0, at[which]))
+            for which in (0, 1)
+        ]
+
+    return pl.pallas_call(
+        note_kernel,
+        grid_spec=pltpu.PrefetchScalarGridSpec(
+            num_scalar_prefetch=1,
+            grid=(1,),
+            in_specs=specs(3) + specs(3) + specs(1),
+            out_specs=pl.BlockSpec((devices, 8, 2 * LANES), lambda i, at: (0, 0, 0)),
+        ),
+        out_shape=jax.ShapeDtypeStruct((devices, 8, 2 * LANES), jnp.float32),
+        compiler_params=pltpu.CompilerParams(vmem_limit_bytes=VMEM_BYTES),
+        name="notes",
+    )(starts, centers, centers, normals, normals, areas, areas)
+
+
+def source_factors(note_ref):
+    notes = jnp.concatenate([note_ref[i] for i in range(note_ref.shape[0])], axis=1)
+    row = lax.broadcasted_iota(jnp.int32, notes.shape, 0)
+    place = jnp.where(row < 4, notes, 0.0)
+    high, middle, low = three(jnp.where(row < 4, pltpu.roll(notes, 4, 0), 0.0))
+    bare = jnp.where(row == 3, 0.0, high)
+    bare_middle = jnp.where(row == 3, 0.0, middle)
     none = jnp.zeros_like(high)
     rows = [high, bare, middle, bare, bare_middle, low, none, none]
     rows += list(three(place)) + [none] * 5
-    factor_ref[...] = jnp.concatenate(rows, axis=0).T.astype(jnp.bfloat16)
-
-
-def source_factors(centers, normals, areas, block=1024):
-    count = centers.shape[1]
-    return pl.pallas_call(
-        factor_kernel,
-        grid=(count // block,),
-        in_specs=[
-            pl.BlockSpec((3, block), lambda i: (0, i)),
-            pl.BlockSpec((3, block), lambda i: (0, i)),
-            pl.BlockSpec((1, block), lambda i: (0, i)),
-        ],
-        out_specs=pl.BlockSpec((block, LANES), lambda i: (i, 0)),
-        out_shape=jax.ShapeDtypeStruct((count, LANES), jnp.bfloat16),
-        cost_estimate=pl.CostEstimate(
-            flops=count * 400, bytes_accessed=count * 320, transcendentals=0
-        ),
-        name="factors",
-    )(centers, normals, areas[None, :])
+    return jnp.concatenate(rows, axis=0).T.astype(jnp.bfloat16)
 
 
 def target_factors(targets):
@@ -116,18 +124,19 @@
         wide_ref[row] = wide[:, row * LANES : (row + 1) * LANES]
 
 
-def build_kernel(factor_ref, target_ref, tile_ref, wide_ref, pair_ref, spread_ref):
+def build_kernel(note_ref, target_ref, tile_ref, wide_ref, pair_ref, spread_ref, factor_ref):
     @pl.when(pl.program_id(0) == 0)
     def _():
         prepare(target_ref, pair_ref, spread_ref)
 
+    factor_ref[...] = source_factors(note_ref)
     spread_params(factor_ref, spread_ref, wide_ref)
     for column in range(0, tile_ref.shape[1], STEP):
         fill(factor_ref, target_ref, wide_ref, pair_ref, column, [tile_ref])
 
 
 def finish_kernel(
-    factor_ref,
+    note_ref,
     target_ref,
     moved_ref,
     old_ref,
@@ -136,6 +145,7 @@
     wide_ref,
     pair_ref,
     spread_ref,
+    factor_ref,
     even_ref,
     odd_ref,
 ):
@@ -160,6 +170,7 @@
             product_ref[(column + lane) // LANES] += value[:, lane : lane + LANES]
 
     def whole(now_ref, before_ref):
+        factor_ref[...] = source_factors(note_ref)
         spread_params(factor_ref, spread_ref, wide_ref)
         for column in range(0, width, STEP):
             value = dot(step, old_ref, column)
@@ -193,14 +204,14 @@
             add_to(column, dot(blocks + step - 1, even_ref, column))
 
 
-def build(factors, targets):
-    count = factors.shape[0]
+def build(notes, targets):
+    count = notes.shape[0] * notes.shape[2]
     width = targets.shape[1]
     return pl.pallas_call(
         build_kernel,
         grid=(count // BLOCK // 2,),
         in_specs=[
-            pl.BlockSpec((BLOCK, LANES), lambda i: (i, 0)),
+            pl.BlockSpec((BLOCK // 256, 8, 256), lambda i: (i, 0, 0)),
             pl.BlockSpec((8, width), lambda i: (0, 0)),
         ],
         out_specs=pl.BlockSpec((BLOCK, width), lambda i: (i, 0)),
@@ -209,16 +220,17 @@
             pltpu.VMEM((4, BLOCK, LANES), jnp.float32),
             pltpu.VMEM((48, width), jnp.bfloat16),
             pltpu.VMEM((32, 4 * LANES), jnp.bfloat16),
+            pltpu.VMEM((BLOCK, LANES), jnp.bfloat16),
         ],
         compiler_params=pltpu.CompilerParams(vmem_limit_bytes=VMEM_BYTES),
         cost_estimate=pl.CostEstimate(
             flops=count * width * 50, bytes_accessed=count * width, transcendentals=count * width // 2
         ),
         name="build",
-    )(factors, targets)
-
-
-def finish_build(factors, targets, moved, tile):
+    )(notes, targets)
+
+
+def finish_build(notes, targets, moved, tile):
     count, width = tile.shape
     blocks = count // BLOCK // 2
     onsets = moved.shape[1]
@@ -226,7 +238,9 @@
         finish_kernel,
         grid=(blocks + 1,),
         in_specs=[
-            pl.BlockSpec((BLOCK, LANES), lambda i: (blocks + jnp.minimum(i, blocks - 1), 0)),
+            pl.BlockSpec(
+                (BLOCK // 256, 8, 256), lambda i: (blocks + jnp.minimum(i, blocks - 1), 0, 0)
+            ),
             pl.BlockSpec((8, width), lambda i: (0, 0)),
             pl.BlockSpec(moved.shape, lambda i: (0, 0, 0)),
             pl.BlockSpec((BLOCK, width), lambda i: (jnp.minimum(i, blocks - 1), 0)),
@@ -243,13 +257,14 @@
             pltpu.VMEM((4, BLOCK, LANES), jnp.float32),
             pltpu.VMEM((48, width), jnp.bfloat16),
             pltpu.VMEM((32, 4 * LANES), jnp.bfloat16),
+            pltpu.VMEM((BLOCK, LANES), jnp.bfloat16),
             pltpu.VMEM((BLOCK, width), jnp.bfloat16),
             pltpu.VMEM((BLOCK, width), jnp.bfloat16),
         ],
         input_output_aliases={3: 0},
         compiler_params=pltpu.CompilerParams(vmem_limit_bytes=FINISH_BYTES),
         name="finish",
-    )(factors, targets, moved, tile)
+    )(notes, targets, moved, tile)
 
 
 def apply_kernel(moved_ref, tile_ref, product_ref):
@@ -433,44 +448,71 @@
     col_count = lax.axis_size("col")
     row_index = lax.axis_index("row")
     col_index = lax.axis_index("col")
-    own = start.shape[1]
-    count = start.shape[0]
+    count, own = start.shape
     own_first = col_index * own
     own_areas = lax.dynamic_slice_in_dim(areas, own_first, own, 0)
     own_normals = lax.dynamic_slice_in_dim(normals, own_first, own, 1)
     own_centers = lax.dynamic_slice_in_dim(centers, own_first, own, 1)
 
-    mark = jnp.concatenate([jnp.ones((1, own)), jnp.zeros((4, own))], axis=0)
-    note = jnp.concatenate([own_centers, mark.astype(jnp.float32)], axis=0)
-    notes = spread(note, "row", row_count)
-    shown = jnp.broadcast_to(start.astype(jnp.bfloat16)[None], (col_count, count, own))
-    factors = source_factors(centers, normals, areas)
-    notes, shown, factors = lax.optimization_barrier((notes, shown, factors))
-    targets = jnp.transpose(notes, (1, 0, 2)).reshape(8, row_count * own)
-    moved = lax.all_to_all(shown, "col", 0, 0, tiled=True)
-
-    tile = build(factors, targets)
-    tile, partial = finish_build(factors, targets, moved, tile)
-
+    levels = col_count // (SIDES * CORES)
+    z_index = col_index // (SIDES * CORES)
+    y_index = col_index // CORES % SIDES
+    core_index = col_index % CORES
+    place = [
+        [[(z * SIDES + y) * CORES + core for core in range(CORES)] for y in range(SIDES)]
+        for z in range(levels)
+    ]
+    across = [
+        [place[z][y][core] for z in range(levels) for core in range(CORES)] for y in range(SIDES)
+    ]
+    along = [
+        [row * col_count + place[z][y][core] for row in range(row_count) for y in range(SIDES)]
+        for z in range(levels)
+        for core in range(CORES)
+    ]
+
+    def exchange_targets(value):
+        return lax.all_to_all(value, "col", 0, 0, tiled=True, axis_index_groups=across)
+
+    def exchange_sources(value):
+        return lax.all_to_all(
+            value, ("row", "col"), 0, 0, tiled=True, axis_index_groups=along
+        )
+
+    low = z_index * (SIDES * CORES) + core_index
+    starts = jnp.stack([low, low + CORES]).astype(jnp.int32)
+    notes = notes_of(starts, centers, normals, areas[None, :], row_count)
+    notes = lax.all_to_all(notes, "row", 0, 0, tiled=True)
+    shown = jnp.broadcast_to(
+        start.astype(jnp.bfloat16)[None], (row_count * SIDES, count, own)
+    )
+    targets = lax.dynamic_index_in_dim(
+        centers.reshape(3, levels, SIDES, CORES * own), y_index, 2, False
+    ).reshape(3, levels * CORES * own)
+    mark = jnp.ones((1, targets.shape[1]), jnp.float32)
+    targets = jnp.concatenate([targets, mark, jnp.zeros((4, targets.shape[1]))], axis=0)
     right = -jnp.sum(onset[:, :, None] * own_normals[:, None, :], axis=0)
     base = right - 0.5 * start
-    parts = lax.all_to_all(partial, "row", 0, 0, tiled=True)
-    residual, sent = residual_of(parts, base, col_count)
-    gathered = lax.all_to_all(sent, "col", 0, 0, tiled=True)
-    partial = apply(gathered, tile)
-    parts = lax.all_to_all(partial, "row", 0, 0, tiled=True)
+    notes, shown, targets, base = lax.optimization_barrier((notes, shown, targets, base))
+    moved = exchange_sources(shown)
+
+    tile = build(notes, targets)
+    tile, partial = finish_build(notes, targets, moved, tile)
+    residual, sent = residual_of(exchange_targets(partial), base, row_count * SIDES)
+    partial = apply(exchange_sources(sent), tile)
+    parts = exchange_targets(partial)
     here = jnp.pad(own_centers, ((0, 5), (0, 0)))
-    fields, sent = sums_of(parts, start, residual, here, own_areas[None, :], col_count)
+    fields, sent = sums_of(parts, start, residual, here, own_areas[None, :], levels * CORES)
 
     flat = row_index * col_count + col_index
     devices = row_count * col_count
     forward = [(i, i + 1) for i in range(devices - 1)]
     backward = [(i + 1, i) for i in range(devices - 1)]
-    parts = lax.all_to_all(sent, "col", 0, 0, tiled=True)
+    parts = exchange_targets(sent)
     before = lax.ppermute(fields, ("row", "col"), forward)
     after = lax.ppermute(fields, ("row", "col"), backward)
     parts, before, after = lax.optimization_barrier((parts, before, after))
-    parts = lax.all_to_all(regroup(parts, row_count), "row", 0, 0, tiled=True)
+    parts = exchange_sources(regroup(parts, row_count * SIDES))
     ends = jnp.stack([flat == 0, flat == devices - 1]).astype(jnp.int32)
     return last(parts, fields, before, after, onset.T, ends, count)
 

time: 153 us -> 156 us (1.020)
  starting transfers between devices: 44.8 us -> 38.4 us
  blocking collectives: 36.4 us -> 42.6 us
    all_to_all x5, starting transfers between devices: 35.1 us -> 28.6 us  [the longest x2 11.5 us: exchange_sources(): lax.all_to_all(value, ('row', 'col'), 0, 0, tiled=True, axis_index_groups...]
    all_to_all x2, blocking collectives: 36.4 us -> 42.6 us  [the longest x1 21.4 us: exchange_targets(): lax.all_to_all(value, 'col', 0, 0, tiled=True, axis_index_groups=across)]
  transfers between devices with their start and end apart: 7 -> 7, of which waited for: 5 -> 4; matrix products, arithmetic and copies ran while one was open for 2% -> 4% of each run, Pallas kernels for 9% -> 8%
where the time goes in v5:
time: 156 us; the launch traced here: 153 us
  blocking collectives  42.6 us (27%)
  Pallas kernels  38.9 us (25%)
  starting transfers between devices  38.4 us (25%)
  waiting for transfers between devices  24.6 us (16%)
  local copies, waits for them, and re-layouts  4.98 us (3%)
  other arithmetic  2.95 us (2%)
    all_to_all x1, blocking collectives, exchange_targets(): lax.all_to_all(value, 'col', 0, 0, tiled=True, axis_index_groups=across)  21.4 us
    all_to_all x1, blocking collectives, exchange_sources(): lax.all_to_all(value, ('row', 'col'), 0, 0, tiled=True, axis_index_groups...  21.2 us
    pallas_call x1, Pallas kernels, finish_build(): pl.pallas_call(finish_kernel, grid=(blocks + 1,), in_specs=[pl.BlockSpec(...  13.9 us
    pallas_call x1, Pallas kernels, build(): pl.pallas_call(build_kernel, grid=(count // BLOCK // 2,), in_specs=[pl.Bl...  11.6 us
    all_to_all x2, starting transfers between devices, exchange_sources(): lax.all_to_all(value, ('row', 'col'), 0, 0, tiled=True, axis_index_groups...  11.5 us
    all_to_all x1, starting transfers between devices, per_device(): notes = lax.all_to_all(notes, 'row', 0, 0, tiled=True)  10.1 us
    all_to_all x2, waiting for transfers between devices, exchange_targets(): lax.all_to_all(value, 'col', 0, 0, tiled=True, axis_index_groups=across)  9.55 us
    all_to_all x2, waiting for transfers between devices, exchange_sources(): lax.all_to_all(value, ('row', 'col'), 0, 0, tiled=True, axis_index_groups...  8.98 us
  transfers between devices with their start and end apart: 7, of which 4 were waited for; matrix products, arithmetic and copies ran while one was open for 4% of the time, Pallas kernels for 8%

profile of v5, /device:TPU:6, one launch (start us, length us, event | category | flops | bytes accessed | tf_op | source)
XLA Modules:
  0.0 153.2 jit_solution(9838148007667132667)
XLA Ops:
  0.7 0.6 pad_add_fusion.at_ref
  1.2 2.1 %notes.1 = f32[16,8,256]{2,1,0:T(8,128)} custom-call(s32[2]{0:T(128)} %pad_add_fusion.at_ref, f32[3,4096]{1,0:T(4,128)} %refs_1_.1, f32[3,4096]{1,0:T(4,128)} %refs_1_.1, f32[3,4096]{1,0:T(4,128)} %refs_3_.1, f32[3,4096]{1,0:T(4,128)} %refs_3_.1, f32[1,4096]{1,0:T(1,128)} %bitcast.18, f32[1,4096]{1,0:T(1,128)} %bitcast.19), custom_call_target="tpu_custom_call" | custom-call | tf_op jit(solution)/shard_map/notes/pallas_call | solution.py:55
  3.3 10.1 %all-to-all-start = ((f32[16,8,256]{2,1,0:T(8,128)}), f32[16,8,256]{2,1,0:T(8,128)S(1)}, u32[]{:S(2)}, u32[]{:S(2)}) async-start(f32[16,8,256]{2,1,0:T(8,128)} %notes.1), calls=%async_computation | async-start | bytes 262144 | tf_op jit(solution)/shard_map/all_to_all | solution.py:485
  13.4 0.9 reshape.14
  14.4 0.1 pad.9.clone
  14.5 0.7 constant_dynamic-slice_fusion.1
  15.2 0.7 maximum_maximum_fusion.target_ref
  15.9 0.8 multiply_reduce_fusion
  16.7 0.8 multiply_subtract_fusion
  17.5 4.3 %all-to-all-done.note_ref = f32[16,8,256]{2,1,0:T(8,128)S(1)} async-done(((f32[16,8,256]{2,1,0:T(8,128)}), f32[16,8,256]{2,1,0:T(8,128)S(1)}, u32[]{:S(2)}, u32[]{:S(2)}) %all-to-all-start) | async-done | bytes 131104 | tf_op jit(solution)/shard_map/all_to_all | solution.py:485
  21.8 0.7 broadcast_in_dim.21
  22.5 6.1 %all-to-all-start.1 = ((bf16[32,32,128]{2,1,0:T(8,128)(2,1)}), bf16[32,32,128]{2,1,0:T(8,128)(2,1)S(1)}, u32[]{:S(2)}, u32[]{:S(2)}) async-start(bf16[32,32,128]{2,1,0:T(8,128)(2,1)} %broadcast_in_dim.21), calls=%async_computation.1 | async-start | bytes 524288 | tf_op jit(solution)/shard_map/all_to_all | solution.py:478
  28.6 11.6 %build.1.old_ref = bf16[4096,2048]{1,0:T(8,128)(2,1)} custom-call(f32[16,8,256]{2,1,0:T(8,128)} %copy-done, f32[8,2048]{1,0:T(8,128)} %maximum_maximum_fusion.target_ref), custom_call_target="tpu_custom_call" | custom-call | flops 419430400 | bytes 8388608 | tf_op jit(solution)/shard_map/build/pallas_call | solution.py:210
  40.2 0.9 copy-done.1
  41.1 13.9 %finish.1 = (bf16[4096,2048]{1,0:T(8,128)(2,1)}, f32[16,32,128]{2,1,0:T(8,128)S(1)}) custom-call(f32[16,8,256]{2,1,0:T(8,128)S(1)} %copy-done.1, f32[8,2048]{1,0:T(8,128)S(1)} %copy-done.2, bf16[32,32,128]{2,1,0:T(8,128)(2,1)S(1)} %all-to-all-done.1.moved_ref, bf16[4096,2048]{1,0:T(8,128)(2,1)} %build.1.old_ref), custom_call_target="tpu_custom_call", output_to_operand_aliasing={{0}: (3, {})} | custom-call | tf_op jit(solution)/shard_map/finish/pallas_call | solution.py:237
  55.0 21.4 %all_to_all.35.part_ref = f32[16,32,128]{2,1,0:T(8,128)S(1)} all-to-all(f32[16,32,128]{2,1,0:T(8,128)S(1)} %get-tuple-element.18), channel_id=1, replica_groups={{0,1,4,5,8,9,12,13,16,17,20,21,24,25,28,29},{2,3,6,7,10,11,14,15,18,19,..., dimensions={0} | all-to-all | bytes 524288 | tf_op jit(solution)/shard_map/all_to_all | solution.py:475
  76.5 21.2 %all_to_all.36.moved_ref = bf16[32,32,128]{2,1,0:T(8,128)(2,1)} all-to-all(bf16[32,32,128]{2,1,0:T(8,128)(2,1)S(1)} %get-tuple-element.20), channel_id=1, replica_groups={{0,2,32,34,64,66,96,98,128,130,160,162,192,194,224,226,256,258,288,290,..., dimensions={0} | all-to-all | bytes 524288 | tf_op jit(solution)/shard_map/all_to_all | solution.py:478
  97.6 8.4 %apply.1 = f32[16,32,128]{2,1,0:T(8,128)} custom-call(bf16[32,32,128]{2,1,0:T(8,128)(2,1)} %all_to_all.36.moved_ref, bf16[4096,2048]{1,0:T(8,128)(2,1)} %get-tuple-element.21.tile_ref), custom_call_target="tpu_custom_call" | custom-call | tf_op jit(solution)/shard_map/apply/pallas_call | solution.py:290
  106.0 3.5 %all-to-all-start.4 = ((f32[16,32,128]{2,1,0:T(8,128)}), f32[16,32,128]{2,1,0:T(8,128)S(1)}, u32[]{:S(2)}, u32[]{:S(2)}) async-start(f32[16,32,128]{2,1,0:T(8,128)} %apply.1), calls=%async_computation.4 | async-start | bytes 524288 | tf_op jit(solution)/shard_map/all_to_all | solution.py:475
  109.5 0.7 constant_dynamic-slice_fusion
  110.2 0.8 dynamic-slice_bitcast_fusion.area_ref
  111.0 9.5 %all-to-all-done.4.part_ref = f32[16,32,128]{2,1,0:T(8,128)S(1)} async-done(((f32[16,32,128]{2,1,0:T(8,128)}), f32[16,32,128]{2,1,0:T(8,128)S(1)}, u32[]{:S(2)}, u32[]{:S(2)}) %all-to-all-start.4) | async-done | bytes 262176 | tf_op jit(solution)/shard_map/all_to_all | solution.py:475
  120.5 0.8 sums.1
  121.3 3.5 %all-to-all-start.5 = ((f32[16,8,128]{2,1,0:T(8,128)}), f32[16,8,128]{2,1,0:T(8,128)S(1)}, u32[]{:S(2)}, u32[]{:S(2)}) async-start(f32[16,8,128]{2,1,0:T(8,128)} %get-tuple-element.23), calls=%async_computation.5 | async-start | bytes 131072 | tf_op jit(solution)/shard_map/all_to_all | solution.py:475
  124.8 2.9 %collective-permute-start = (f32[104,128]{1,0:T(8,128)S(1)}, f32[104,128]{1,0:T(8,128)S(1)}, u32[]{:S(2)}, u32[]{:S(2)}) collective-permute-start(f32[104,128]{1,0:T(8,128)S(1)} %get-tuple-element.24.field_ref), channel_id=1, source_target_pairs={{0,1},{1,2},{2,3},{3,4},{4,5},{5,6},{6,7},{7,8},{8,9},{9,10},{10,1... | collective-permute-start | bytes 159752 | tf_op jit(solution)/shard_map/ppermute | solution.py:512
  127.8 6.9 %collective-permute-start.1 = (f32[104,128]{1,0:T(8,128)S(1)}, f32[104,128]{1,0:T(8,128)S(1)}, u32[]{:S(2)}, u32[]{:S(2)}) collective-permute-start(f32[104,128]{1,0:T(8,128)S(1)} %get-tuple-element.24.field_ref), channel_id=1, source_target_pairs={{1,0},{2,1},{3,2},{4,3},{5,4},{6,5},{7,6},{8,7},{9,8},{10,9},{11,1... | collective-permute-start | bytes 159752 | tf_op jit(solution)/shard_map/ppermute | solution.py:513
  134.6 1.8 %collective-permute-done.1.after_ref = f32[104,128]{1,0:T(8,128)S(1)} collective-permute-done((f32[104,128]{1,0:T(8,128)S(1)}, f32[104,128]{1,0:T(8,128)S(1)}, u32[]{:S(2)}, u32[]{:S(2)}) %collective-permute-start.1) | collective-permute-done | bytes 53280 | tf_op jit(solution)/shard_map/ppermute | solution.py:513
  136.4 0.7 regroup.1
  137.1 5.5 %all-to-all-start.6 = ((f32[32,8,128]{2,1,0:T(8,128)}), f32[32,8,128]{2,1,0:T(8,128)S(1)}, u32[]{:S(2)}, u32[]{:S(2)}) async-start(f32[32,8,128]{2,1,0:T(8,128)} %regroup.1), calls=%async_computation.6 | async-start | bytes 262144 | tf_op jit(solution)/shard_map/all_to_all | solution.py:478
  142.6 0.1 copy.11
  142.7 9.0 %all-to-all-done.6.part_ref = f32[32,8,128]{2,1,0:T(8,128)S(1)} async-done(((f32[32,8,128]{2,1,0:T(8,128)}), f32[32,8,128]{2,1,0:T(8,128)S(1)}, u32[]{:S(2)}, u32[]{:S(2)}) %all-to-all-start.6) | async-done | bytes 131104 | tf_op jit(solution)/shard_map/all_to_all | solution.py:478
  151.7 1.4 last.1
  (20 shorter events, 0.3 us)
Async XLA Ops:
  3.3 18.4 %all-to-all-start = ((f32[16,8,256]{2,1,0:T(8,128)}), f32[16,8,256]{2,1,0:T(8,128)S(1)}, u32[]{:S(2)}, u32[]{:S(2)}) async-start(f32[16,8,256]{2,1,0:T(8,128)} %notes.1), calls=%async_computation | async-start | bytes 262144 | tf_op jit(solution)/shard_map/all_to_all | solution.py:485
  15.9 24.3 %copy-start.2 = (f32[8,2048]{1,0:T(8,128)S(1)}, f32[8,2048]{1,0:T(8,128)}, u32[]{:S(2)}) copy-start(f32[8,2048]{1,0:T(8,128)} %maximum_maximum_fusion.target_ref) | copy-start | bytes 196612
  21.8 6.8 %copy-start = (f32[16,8,256]{2,1,0:T(8,128)}, f32[16,8,256]{2,1,0:T(8,128)S(1)}, u32[]{:S(2)}) copy-start(f32[16,8,256]{2,1,0:T(8,128)S(1)} %all-to-all-done.note_ref) | copy-start | bytes 393220
  22.5 17.7 %all-to-all-start.1 = ((bf16[32,32,128]{2,1,0:T(8,128)(2,1)}), bf16[32,32,128]{2,1,0:T(8,128)(2,1)S(1)}, u32[]{:S(2)}, u32[]{:S(2)}) async-start(bf16[32,32,128]{2,1,0:T(8,128)(2,1)} %broadcast_in_dim.21), calls=%async_computation.1 | async-start | bytes 524288 | tf_op jit(solution)/shard_map/all_to_all | solution.py:478
  40.2 0.9 copy-start.1
  41.1 79.4 %copy-start.3 = (f32[32,128]{1,0:T(8,128)S(1)}, f32[32,128]{1,0:T(8,128)}, u32[]{:S(2)}) copy-start(f32[32,128]{1,0:T(8,128)} %start_ref.1) | copy-start | bytes 49156
  41.1 101.4 %copy-start.4 = (f32[3,32]{1,0:T(4,128)S(1)}, f32[3,32]{1,0:T(4,128)}, u32[]{:S(2)}) copy-start(f32[3,32]{1,0:T(4,128)} %param.8) | copy-start | bytes 1156
  106.0 14.5 %all-to-all-start.4 = ((f32[16,32,128]{2,1,0:T(8,128)}), f32[16,32,128]{2,1,0:T(8,128)S(1)}, u32[]{:S(2)}, u32[]{:S(2)}) async-start(f32[16,32,128]{2,1,0:T(8,128)} %apply.1), calls=%async_computation.4 | async-start | bytes 524288 | tf_op jit(solution)/shard_map/all_to_all | solution.py:475
  121.3 15.1 %all-to-all-start.5 = ((f32[16,8,128]{2,1,0:T(8,128)}), f32[16,8,128]{2,1,0:T(8,128)S(1)}, u32[]{:S(2)}, u32[]{:S(2)}) async-start(f32[16,8,128]{2,1,0:T(8,128)} %get-tuple-element.23), calls=%async_computation.5 | async-start | bytes 131072 | tf_op jit(solution)/shard_map/all_to_all | solution.py:475
  124.8 9.8 %collective-permute-start = (f32[104,128]{1,0:T(8,128)S(1)}, f32[104,128]{1,0:T(8,128)S(1)}, u32[]{:S(2)}, u32[]{:S(2)}) collective-permute-start(f32[104,128]{1,0:T(8,128)S(1)} %get-tuple-element.24.field_ref), channel_id=1, source_target_pairs={{0,1},{1,2},{2,3},{3,4},{4,5},{5,6},{6,7},{7,8},{8,9},{9,10},{10,1... | collective-permute-start | bytes 159752 | tf_op jit(solution)/shard_map/ppermute | solution.py:512
  127.8 8.6 %collective-permute-start.1 = (f32[104,128]{1,0:T(8,128)S(1)}, f32[104,128]{1,0:T(8,128)S(1)}, u32[]{:S(2)}, u32[]{:S(2)}) collective-permute-start(f32[104,128]{1,0:T(8,128)S(1)} %get-tuple-element.24.field_ref), channel_id=1, source_target_pairs={{1,0},{2,1},{3,2},{4,3},{5,4},{6,5},{7,6},{8,7},{9,8},{10,9},{11,1... | collective-permute-start | bytes 159752 | tf_op jit(solution)/shard_map/ppermute | solution.py:513
  137.1 14.6 %all-to-all-start.6 = ((f32[32,8,128]{2,1,0:T(8,128)}), f32[32,8,128]{2,1,0:T(8,128)S(1)}, u32[]{:S(2)}, u32[]{:S(2)}) async-start(f32[32,8,128]{2,1,0:T(8,128)} %regroup.1), calls=%async_computation.6 | async-start | bytes 262144 | tf_op jit(solution)/shard_map/all_to_all | solution.py:478

commit v6 on v4

--- a/solution.py
+++ b/solution.py
@@ -35,7 +35,13 @@
     return high, middle, rest - middle
 
 
-def factor_kernel(center_ref, normal_ref, area_ref, factor_ref):
+def factor_kernel(center_ref, normal_ref, area_ref, start_ref, factor_ref, shown_ref):
+    @pl.when(pl.program_id(0) == 0)
+    def _():
+        shown = start_ref[...].astype(jnp.bfloat16)
+        for device in range(shown_ref.shape[0]):
+            shown_ref[device] = shown
+
     width = center_ref.shape[1]
     blank = jnp.zeros((4, width), jnp.float32)
     area = area_ref[...]
@@ -52,7 +58,7 @@
     factor_ref[...] = jnp.concatenate(rows, axis=0).T.astype(jnp.bfloat16)
 
 
-def source_factors(centers, normals, areas, block=1024):
+def source_factors(centers, normals, areas, start, devices, block=1024):
     count = centers.shape[1]
     return pl.pallas_call(
         factor_kernel,
@@ -61,14 +67,21 @@
             pl.BlockSpec((3, block), lambda i: (0, i)),
             pl.BlockSpec((3, block), lambda i: (0, i)),
             pl.BlockSpec((1, block), lambda i: (0, i)),
-        ],
-        out_specs=pl.BlockSpec((block, LANES), lambda i: (i, 0)),
-        out_shape=jax.ShapeDtypeStruct((count, LANES), jnp.bfloat16),
+            pl.BlockSpec(start.shape, lambda i: (0, 0)),
+        ],
+        out_specs=[
+            pl.BlockSpec((block, LANES), lambda i: (i, 0)),
+            pl.BlockSpec((devices,) + start.shape, lambda i: (0, 0, 0)),
+        ],
+        out_shape=[
+            jax.ShapeDtypeStruct((count, LANES), jnp.bfloat16),
+            jax.ShapeDtypeStruct((devices,) + start.shape, jnp.bfloat16),
+        ],
         cost_estimate=pl.CostEstimate(
-            flops=count * 400, bytes_accessed=count * 320, transcendentals=0
+            flops=count * 400, bytes_accessed=count * 400, transcendentals=0
         ),
         name="factors",
-    )(centers, normals, areas[None, :])
+    )(centers, normals, areas[None, :], start)
 
 
 def target_factors(targets):
@@ -443,17 +456,16 @@
     mark = jnp.concatenate([jnp.ones((1, own)), jnp.zeros((4, own))], axis=0)
     note = jnp.concatenate([own_centers, mark.astype(jnp.float32)], axis=0)
     notes = spread(note, "row", row_count)
-    shown = jnp.broadcast_to(start.astype(jnp.bfloat16)[None], (col_count, count, own))
-    factors = source_factors(centers, normals, areas)
-    notes, shown, factors = lax.optimization_barrier((notes, shown, factors))
+    factors, shown = source_factors(centers, normals, areas, start, col_count)
+    right = -jnp.sum(onset[:, :, None] * own_normals[:, None, :], axis=0)
+    base = right - 0.5 * start
+    notes, shown, factors, base = lax.optimization_barrier((notes, shown, factors, base))
     targets = jnp.transpose(notes, (1, 0, 2)).reshape(8, row_count * own)
     moved = lax.all_to_all(shown, "col", 0, 0, tiled=True)
 
     tile = build(factors, targets)
     tile, partial = finish_build(factors, targets, moved, tile)
 
-    right = -jnp.sum(onset[:, :, None] * own_normals[:, None, :], axis=0)
-    base = right - 0.5 * start
     parts = lax.all_to_all(partial, "row", 0, 0, tiled=True)
     residual, sent = residual_of(parts, base, col_count)
     gathered = lax.all_to_all(sent, "col", 0, 0, tiled=True)
@@ -468,8 +480,8 @@
     backward = [(i + 1, i) for i in range(devices - 1)]
     parts = lax.all_to_all(sent, "col", 0, 0, tiled=True)
     before = lax.ppermute(fields, ("row", "col"), forward)
-    after = lax.ppermute(fields, ("row", "col"), backward)
-    parts, before, after = lax.optimization_barrier((parts, before, after))
+    parts, before, later = lax.optimization_barrier((parts, before, fields))
+    after = lax.ppermute(later, ("row", "col"), backward)
     parts = lax.all_to_all(regroup(parts, row_count), "row", 0, 0, tiled=True)
     ends = jnp.stack([flat == 0, flat == devices - 1]).astype(jnp.int32)
     return last(parts, fields, before, after, onset.T, ends, count)

time: 153 us -> 152 us (level)
  starting transfers between devices: 44.8 us -> 42.7 us
  waiting for transfers between devices: 24.7 us -> 26.4 us
    ppermute x1, waiting for transfers between devices: 0.01 us -> 7.59 us  [per_device(): before = lax.ppermute(fields, ('row', 'col'), forward)]
    all_to_all x1, waiting for transfers between devices: 7.88 us -> 1.93 us  [per_device(): parts = lax.all_to_all(regroup(parts, row_count), 'row', 0, 0, tiled=True)]
    ppermute x1, starting transfers between devices: 7.71 us -> 4.3 us  [per_device(): after = lax.ppermute(later, ('row', 'col'), backward)]
  transfers between devices with their start and end apart: 7 -> 7, of which waited for: 5 -> 7; matrix products, arithmetic and copies ran while one was open for 2% -> 2% of each run, Pallas kernels for 9% -> 9%
where the time goes in v6:
time: 152 us; the launch traced here: 150 us
  starting transfers between devices  42.7 us (28%)
  Pallas kernels  38.8 us (26%)
  blocking collectives  36.4 us (24%)
  waiting for transfers between devices  26.4 us (17%)
  local copies, waits for them, and re-layouts  3.17 us (2%)
  other arithmetic  1.72 us (1%)
    all_to_all x1, blocking collectives, per_device(): gathered = lax.all_to_all(sent, 'col', 0, 0, tiled=True)  19.4 us
    all_to_all x1, blocking collectives, per_device(): parts = lax.all_to_all(partial, 'row', 0, 0, tiled=True)  17 us
    pallas_call x1, Pallas kernels, finish_build(): pl.pallas_call(finish_kernel, grid=(blocks + 1,), in_specs=[pl.BlockSpec(...  13.4 us
    all_to_all x1, starting transfers between devices, per_device(): moved = lax.all_to_all(shown, 'col', 0, 0, tiled=True)  10.8 us
    pallas_call x1, Pallas kernels, build(): pl.pallas_call(build_kernel, grid=(count // BLOCK // 2,), in_specs=[pl.Bl...  10.8 us
    all_to_all x1, waiting for transfers between devices, per_device(): parts = lax.all_to_all(partial, 'row', 0, 0, tiled=True)  10.5 us
    all_to_all x1, starting transfers between devices, spread(): return lax.all_to_all(copies, axis, 0, 0, tiled=True)  10.1 us
    pallas_call x1, Pallas kernels, apply(): pl.pallas_call(apply_kernel, grid=(count // depth,), in_specs=[pl.BlockSp...  8.37 us
  transfers between devices with their start and end apart: 7, of which 7 were waited for; matrix products, arithmetic and copies ran while one was open for 2% of the time, Pallas kernels for 9%

profile of v6, /device:TPU:6, one launch (start us, length us, event | category | flops | bytes accessed | tf_op | source)
XLA Modules:
  0.0 149.8 jit_solution(2295497909837075961)
XLA Ops:
  0.6 0.1 pad.9.clone
  0.8 0.7 constant_dynamic-slice_fusion
  1.6 0.6 broadcast_in_dim.22
  2.2 10.1 %all-to-all-start = ((f32[16,8,128]{2,1,0:T(8,128)}), f32[16,8,128]{2,1,0:T(8,128)S(1)}, u32[]{:S(2)}, u32[]{:S(2)}) async-start(f32[16,8,128]{2,1,0:T(8,128)} %broadcast_in_dim.22), calls=%async_computation | async-start | bytes 131072 | tf_op jit(solution)/shard_map/all_to_all | solution.py:28
  12.2 0.8 multiply_reduce_fusion
  13.0 3.3 %factors.1 = (bf16[4096,128]{1,0:T(8,128)(2,1)}, bf16[32,32,128]{2,1,0:T(8,128)(2,1)}) custom-call(f32[3,4096]{1,0:T(4,128)} %center_ref.1, f32[3,4096]{1,0:T(4,128)} %normal_ref.1, f32[1,4096]{1,0:T(1,128)} %bitcast.13, f32[32,128]{1,0:T(8,128)} %start_ref.3), custom_call_target="tpu_custom_call" | custom-call | flops 1638400 | bytes 1638400 | tf_op jit(solution)/shard_map/factors/pallas_call | solution.py:63
  16.3 0.8 multiply_subtract_fusion.base_ref
  17.1 3.2 %all-to-all-done = f32[16,8,128]{2,1,0:T(8,128)S(1)} async-done(((f32[16,8,128]{2,1,0:T(8,128)}), f32[16,8,128]{2,1,0:T(8,128)S(1)}, u32[]{:S(2)}, u32[]{:S(2)}) %all-to-all-start) | async-done | bytes 65568 | tf_op jit(solution)/shard_map/all_to_all | solution.py:28
  20.3 10.8 %all-to-all-start.1 = ((bf16[32,32,128]{2,1,0:T(8,128)(2,1)}), bf16[32,32,128]{2,1,0:T(8,128)(2,1)S(1)}, u32[]{:S(2)}, u32[]{:S(2)}) async-start(bf16[32,32,128]{2,1,0:T(8,128)(2,1)} %get-tuple-element.21), calls=%async_computation.1 | async-start | bytes 524288 | tf_op jit(solution)/shard_map/all_to_all | solution.py:464
  31.2 10.8 %build.1.old_ref = bf16[4096,2048]{1,0:T(8,128)(2,1)} custom-call(bf16[4096,128]{1,0:T(8,128)(2,1)} %get-tuple-element.19.factor_ref, f32[8,2048]{1,0:T(8,128)} %bitcast.10), custom_call_target="tpu_custom_call" | custom-call | flops 419430400 | bytes 8388608 | tf_op jit(solution)/shard_map/build/pallas_call | solution.py:212
  42.0 1.4 all-to-all-done.1.moved_ref
  43.4 0.8 copy-done.2
  44.2 13.4 %finish.1 = (bf16[4096,2048]{1,0:T(8,128)(2,1)}, f32[16,32,128]{2,1,0:T(8,128)S(1)}) custom-call(bf16[4096,128]{1,0:T(8,128)(2,1)S(1)} %copy-done, f32[8,2048]{1,0:T(8,128)S(1)} %bitcast.11, bf16[32,32,128]{2,1,0:T(8,128)(2,1)S(1)} %all-to-all-done.1.moved_ref, bf16[4096,2048]{1,0:T(8,128)(2,1)} %build.1.old_ref), custom_call_target="tpu_custom_call", output_to_operand_aliasing={{0}: (3, {})} | custom-call | tf_op jit(solution)/shard_map/finish/pallas_call | solution.py:238
  57.6 17.0 %all_to_all.35.part_ref = f32[16,32,128]{2,1,0:T(8,128)S(1)} all-to-all(f32[16,32,128]{2,1,0:T(8,128)S(1)} %get-tuple-element.22), channel_id=1, replica_groups=mesh['row'=16,'col'=32] {'row'}, dimensions={0} | all-to-all | bytes 524288 | tf_op jit(solution)/shard_map/all_to_all | solution.py:469
  74.7 19.4 %all_to_all.36.moved_ref = bf16[32,32,128]{2,1,0:T(8,128)(2,1)} all-to-all(bf16[32,32,128]{2,1,0:T(8,128)(2,1)S(1)} %get-tuple-element.24), channel_id=1, replica_groups=mesh['row'=16,'col'=32] {'col'}, dimensions={0} | all-to-all | bytes 524288 | tf_op jit(solution)/shard_map/all_to_all | solution.py:471
  94.1 8.4 %apply.1 = f32[16,32,128]{2,1,0:T(8,128)} custom-call(bf16[32,32,128]{2,1,0:T(8,128)(2,1)} %all_to_all.36.moved_ref, bf16[4096,2048]{1,0:T(8,128)(2,1)} %get-tuple-element.25.tile_ref), custom_call_target="tpu_custom_call" | custom-call | tf_op jit(solution)/shard_map/apply/pallas_call | solution.py:288
  102.5 5.8 %all-to-all-start.4 = ((f32[16,32,128]{2,1,0:T(8,128)}), f32[16,32,128]{2,1,0:T(8,128)S(1)}, u32[]{:S(2)}, u32[]{:S(2)}) async-start(f32[16,32,128]{2,1,0:T(8,128)} %apply.1), calls=%async_computation.4 | async-start | bytes 524288 | tf_op jit(solution)/shard_map/all_to_all | solution.py:473
  108.3 0.8 dynamic-slice_bitcast_fusion.area_ref
  109.0 10.5 %all-to-all-done.4.part_ref = f32[16,32,128]{2,1,0:T(8,128)S(1)} async-done(((f32[16,32,128]{2,1,0:T(8,128)}), f32[16,32,128]{2,1,0:T(8,128)S(1)}, u32[]{:S(2)}, u32[]{:S(2)}) %all-to-all-start.4) | async-done | bytes 262176 | tf_op jit(solution)/shard_map/all_to_all | solution.py:473
  119.5 0.8 sums.1
  120.3 3.8 %all-to-all-start.5 = ((f32[32,8,128]{2,1,0:T(8,128)}), f32[32,8,128]{2,1,0:T(8,128)S(1)}, u32[]{:S(2)}, u32[]{:S(2)}) async-start(f32[32,8,128]{2,1,0:T(8,128)} %get-tuple-element.27), calls=%async_computation.5 | async-start | bytes 262144 | tf_op jit(solution)/shard_map/all_to_all | solution.py:481
  124.2 2.1 %collective-permute-start = (f32[104,128]{1,0:T(8,128)S(1)}, f32[104,128]{1,0:T(8,128)S(1)}, u32[]{:S(2)}, u32[]{:S(2)}) collective-permute-start(f32[104,128]{1,0:T(8,128)S(1)} %get-tuple-element.31.field_ref), channel_id=1, source_target_pairs={{0,1},{1,2},{2,3},{3,4},{4,5},{5,6},{6,7},{7,8},{8,9},{9,10},{10,1... | collective-permute-start | bytes 159752 | tf_op jit(solution)/shard_map/ppermute | solution.py:482
  126.3 7.6 %collective-permute-done.before_ref = f32[104,128]{1,0:T(8,128)S(1)} collective-permute-done((f32[104,128]{1,0:T(8,128)S(1)}, f32[104,128]{1,0:T(8,128)S(1)}, u32[]{:S(2)}, u32[]{:S(2)}) %collective-permute-start) | collective-permute-done | bytes 53280 | tf_op jit(solution)/shard_map/ppermute | solution.py:482
  133.8 0.1 all-to-all-done.5.part_ref
  134.0 0.6 regroup.1
  134.6 5.8 %all-to-all-start.6 = ((f32[16,8,128]{2,1,0:T(8,128)}), f32[16,8,128]{2,1,0:T(8,128)S(1)}, u32[]{:S(2)}, u32[]{:S(2)}) async-start(f32[16,8,128]{2,1,0:T(8,128)} %regroup.1), calls=%async_computation.6 | async-start | bytes 131072 | tf_op jit(solution)/shard_map/all_to_all | solution.py:485
  140.4 4.3 %collective-permute-start.1 = (f32[104,128]{1,0:T(8,128)S(1)}, f32[104,128]{1,0:T(8,128)S(1)}, u32[]{:S(2)}, u32[]{:S(2)}) collective-permute-start(f32[104,128]{1,0:T(8,128)S(1)} %get-tuple-element.31.field_ref), channel_id=1, source_target_pairs={{1,0},{2,1},{3,2},{4,3},{5,4},{6,5},{7,6},{8,7},{9,8},{10,9},{11,1... | collective-permute-start | bytes 159752 | tf_op jit(solution)/shard_map/ppermute | solution.py:484
  144.7 0.1 add_convert_fusion.end_ref
  144.8 0.1 copy.9
  144.9 1.6 %collective-permute-done.1.after_ref = f32[104,128]{1,0:T(8,128)S(1)} collective-permute-done((f32[104,128]{1,0:T(8,128)S(1)}, f32[104,128]{1,0:T(8,128)S(1)}, u32[]{:S(2)}, u32[]{:S(2)}) %collective-permute-start.1) | collective-permute-done | bytes 53280 | tf_op jit(solution)/shard_map/ppermute | solution.py:484
  146.5 1.9 %all-to-all-done.6.part_ref = f32[16,8,128]{2,1,0:T(8,128)S(1)} async-done(((f32[16,8,128]{2,1,0:T(8,128)}), f32[16,8,128]{2,1,0:T(8,128)S(1)}, u32[]{:S(2)}, u32[]{:S(2)}) %all-to-all-start.6) | async-done | bytes 65568 | tf_op jit(solution)/shard_map/all_to_all | solution.py:485
  148.4 1.4 last.1
  (13 shorter events, 0.2 us)
Async XLA Ops:
  2.2 18.1 %all-to-all-start = ((f32[16,8,128]{2,1,0:T(8,128)}), f32[16,8,128]{2,1,0:T(8,128)S(1)}, u32[]{:S(2)}, u32[]{:S(2)}) async-start(f32[16,8,128]{2,1,0:T(8,128)} %broadcast_in_dim.22), calls=%async_computation | async-start | bytes 131072 | tf_op jit(solution)/shard_map/all_to_all | solution.py:28
  16.3 27.1 %copy-start = (bf16[4096,128]{1,0:T(8,128)(2,1)S(1)}, bf16[4096,128]{1,0:T(8,128)(2,1)}, u32[]{:S(2)}) copy-start(bf16[4096,128]{1,0:T(8,128)(2,1)} %get-tuple-element.19.factor_ref) | copy-start | bytes 3145732
  20.3 10.9 %copy-start.1 = (f32[16,8,128]{2,1,0:T(8,128)}, f32[16,8,128]{2,1,0:T(8,128)S(1)}, u32[]{:S(2)}) copy-start(f32[16,8,128]{2,1,0:T(8,128)S(1)} %all-to-all-done) | copy-start | bytes 196612
  20.3 23.1 %all-to-all-start.1 = ((bf16[32,32,128]{2,1,0:T(8,128)(2,1)}), bf16[32,32,128]{2,1,0:T(8,128)(2,1)S(1)}, u32[]{:S(2)}, u32[]{:S(2)}) async-start(bf16[32,32,128]{2,1,0:T(8,128)(2,1)} %get-tuple-element.21), calls=%async_computation.1 | async-start | bytes 524288 | tf_op jit(solution)/shard_map/all_to_all | solution.py:464
  43.4 0.8 copy-start.2
  44.2 75.3 %copy-start.3 = (f32[32,128]{1,0:T(8,128)S(1)}, f32[32,128]{1,0:T(8,128)}, u32[]{:S(2)}) copy-start(f32[32,128]{1,0:T(8,128)} %start_ref.3) | copy-start | bytes 49156
  44.2 100.6 %copy-start.4 = (f32[3,32]{1,0:T(4,128)S(1)}, f32[3,32]{1,0:T(4,128)}, u32[]{:S(2)}) copy-start(f32[3,32]{1,0:T(4,128)} %param.8) | copy-start | bytes 1156
  102.5 17.1 %all-to-all-start.4 = ((f32[16,32,128]{2,1,0:T(8,128)}), f32[16,32,128]{2,1,0:T(8,128)S(1)}, u32[]{:S(2)}, u32[]{:S(2)}) async-start(f32[16,32,128]{2,1,0:T(8,128)} %apply.1), calls=%async_computation.4 | async-start | bytes 524288 | tf_op jit(solution)/shard_map/all_to_all | solution.py:473
  120.3 13.6 %all-to-all-start.5 = ((f32[32,8,128]{2,1,0:T(8,128)}), f32[32,8,128]{2,1,0:T(8,128)S(1)}, u32[]{:S(2)}, u32[]{:S(2)}) async-start(f32[32,8,128]{2,1,0:T(8,128)} %get-tuple-element.27), calls=%async_computation.5 | async-start | bytes 262144 | tf_op jit(solution)/shard_map/all_to_all | solution.py:481
  124.2 9.7 %collective-permute-start = (f32[104,128]{1,0:T(8,128)S(1)}, f32[104,128]{1,0:T(8,128)S(1)}, u32[]{:S(2)}, u32[]{:S(2)}) collective-permute-start(f32[104,128]{1,0:T(8,128)S(1)} %get-tuple-element.31.field_ref), channel_id=1, source_target_pairs={{0,1},{1,2},{2,3},{3,4},{4,5},{5,6},{6,7},{7,8},{8,9},{9,10},{10,1... | collective-permute-start | bytes 159752 | tf_op jit(solution)/shard_map/ppermute | solution.py:482
  134.6 13.8 %all-to-all-start.6 = ((f32[16,8,128]{2,1,0:T(8,128)}), f32[16,8,128]{2,1,0:T(8,128)S(1)}, u32[]{:S(2)}, u32[]{:S(2)}) async-start(f32[16,8,128]{2,1,0:T(8,128)} %regroup.1), calls=%async_computation.6 | async-start | bytes 131072 | tf_op jit(solution)/shard_map/all_to_all | solution.py:485
  140.4 6.1 %collective-permute-start.1 = (f32[104,128]{1,0:T(8,128)S(1)}, f32[104,128]{1,0:T(8,128)S(1)}, u32[]{:S(2)}, u32[]{:S(2)}) collective-permute-start(f32[104,128]{1,0:T(8,128)S(1)} %get-tuple-element.31.field_ref), channel_id=1, source_target_pairs={{1,0},{2,1},{3,2},{4,3},{5,4},{6,5},{7,6},{8,7},{9,8},{10,9},{11,1... | collective-permute-start | bytes 159752 | tf_op jit(solution)/shard_map/ppermute | solution.py:484

commit v7 on v6

--- a/solution.py
+++ b/solution.py
@@ -85,6 +85,7 @@
 
 
 def target_factors(targets):
+    targets = jnp.concatenate([targets, jnp.zeros_like(targets)], axis=0)
     high = targets.astype(jnp.bfloat16).astype(jnp.float32)
     rest = targets - high
     middle = rest.astype(jnp.bfloat16).astype(jnp.float32)
@@ -214,7 +215,7 @@
         grid=(count // BLOCK // 2,),
         in_specs=[
             pl.BlockSpec((BLOCK, LANES), lambda i: (i, 0)),
-            pl.BlockSpec((8, width), lambda i: (0, 0)),
+            pl.BlockSpec((4, width), lambda i: (0, 0)),
         ],
         out_specs=pl.BlockSpec((BLOCK, width), lambda i: (i, 0)),
         out_shape=pltpu.HBM((count, width), jnp.bfloat16),
@@ -240,7 +241,7 @@
         grid=(blocks + 1,),
         in_specs=[
             pl.BlockSpec((BLOCK, LANES), lambda i: (blocks + jnp.minimum(i, blocks - 1), 0)),
-            pl.BlockSpec((8, width), lambda i: (0, 0)),
+            pl.BlockSpec((4, width), lambda i: (0, 0)),
             pl.BlockSpec(moved.shape, lambda i: (0, 0, 0)),
             pl.BlockSpec((BLOCK, width), lambda i: (jnp.minimum(i, blocks - 1), 0)),
         ],
@@ -333,9 +334,8 @@
     weighted = area * residual
     terms = [weighted * residual, weighted * change, area * change * change, area]
     total = jnp.sum(jnp.concatenate(terms, axis=0).T, axis=0, keepdims=True)
-    sent = jnp.broadcast_to(total, sent_ref.shape[1:])
     for device in range(sent_ref.shape[0]):
-        sent_ref[device] = sent
+        sent_ref[device] = jnp.broadcast_to(total, sent_ref.shape[1:])
 
 
 def sums_of(parts, start, residual, centers, areas, devices):
@@ -346,7 +346,7 @@
         out_specs=[WHOLE] * 2,
         out_shape=[
             jax.ShapeDtypeStruct((3 * count + 8, own), jnp.float32),
-            jax.ShapeDtypeStruct((devices, 8, 4 * count), jnp.float32),
+            jax.ShapeDtypeStruct((devices, 2, 4 * count), jnp.float32),
         ],
         compiler_params=pltpu.CompilerParams(vmem_limit_bytes=SMALL_BYTES),
         name="sums",
@@ -354,7 +354,7 @@
 
 
 def regroup_kernel(part_ref, sent_ref):
-    sent = jnp.sum(part_ref[...], axis=0)
+    sent = jnp.broadcast_to(jnp.sum(part_ref[...], axis=0)[0:1, :], sent_ref.shape[1:])
     for device in range(sent_ref.shape[0]):
         sent_ref[device] = sent
 
@@ -364,7 +364,7 @@
         regroup_kernel,
         in_specs=[WHOLE],
         out_specs=WHOLE,
-        out_shape=jax.ShapeDtypeStruct((devices,) + parts.shape[1:], jnp.float32),
+        out_shape=jax.ShapeDtypeStruct((devices, 8, parts.shape[2]), jnp.float32),
         compiler_params=pltpu.CompilerParams(vmem_limit_bytes=SMALL_BYTES),
         name="regroup",
     )(parts)
@@ -453,14 +453,13 @@
     own_normals = lax.dynamic_slice_in_dim(normals, own_first, own, 1)
     own_centers = lax.dynamic_slice_in_dim(centers, own_first, own, 1)
 
-    mark = jnp.concatenate([jnp.ones((1, own)), jnp.zeros((4, own))], axis=0)
-    note = jnp.concatenate([own_centers, mark.astype(jnp.float32)], axis=0)
+    note = jnp.concatenate([own_centers, jnp.ones((1, own), jnp.float32)], axis=0)
     notes = spread(note, "row", row_count)
     factors, shown = source_factors(centers, normals, areas, start, col_count)
     right = -jnp.sum(onset[:, :, None] * own_normals[:, None, :], axis=0)
     base = right - 0.5 * start
     notes, shown, factors, base = lax.optimization_barrier((notes, shown, factors, base))
-    targets = jnp.transpose(notes, (1, 0, 2)).reshape(8, row_count * own)
+    targets = jnp.transpose(notes, (1, 0, 2)).reshape(4, row_count * own)
     moved = lax.all_to_all(shown, "col", 0, 0, tiled=True)
 
     tile = build(factors, targets)
@@ -480,9 +479,9 @@
     backward = [(i + 1, i) for i in range(devices - 1)]
     parts = lax.all_to_all(sent, "col", 0, 0, tiled=True)
     before = lax.ppermute(fields, ("row", "col"), forward)
-    parts, before, later = lax.optimization_barrier((parts, before, fields))
+    sent, before, later = lax.optimization_barrier((regroup(parts, row_count), before, fields))
     after = lax.ppermute(later, ("row", "col"), backward)
-    parts = lax.all_to_all(regroup(parts, row_count), "row", 0, 0, tiled=True)
+    parts = lax.all_to_all(sent, "row", 0, 0, tiled=True)
     ends = jnp.stack([flat == 0, flat == devices - 1]).astype(jnp.int32)
     return last(parts, fields, before, after, onset.T, ends, count)
 

time: 152 us -> 151 us (level)
    ppermute x1, waiting for transfers between devices: 7.59 us -> 0.73 us  [per_device(): before = lax.ppermute(fields, ('row', 'col'), forward)]
    all_to_all x1, waiting for transfers between devices: 0.12 us -> 6.19 us  [per_device(): parts = lax.all_to_all(sent, 'col', 0, 0, tiled=True)]
  transfers between devices with their start and end apart: 7 -> 7, of which waited for: 7 -> 7; matrix products, arithmetic and copies ran while one was open for 2% -> 2% of each run, Pallas kernels for 9% -> 10%
where the time goes in v7:
time: 151 us; the launch traced here: 148 us
  starting transfers between devices  42.1 us (28%)
  Pallas kernels  38.7 us (26%)
  blocking collectives  36.5 us (24%)
  waiting for transfers between devices  25.4 us (17%)
  local copies, waits for them, and re-layouts  2.96 us (2%)
  other arithmetic  1.56 us (1%)
    all_to_all x1, blocking collectives, per_device(): gathered = lax.all_to_all(sent, 'col', 0, 0, tiled=True)  19.4 us
    all_to_all x1, blocking collectives, per_device(): parts = lax.all_to_all(partial, 'row', 0, 0, tiled=True)  17.1 us
    pallas_call x1, Pallas kernels, finish_build(): pl.pallas_call(finish_kernel, grid=(blocks + 1,), in_specs=[pl.BlockSpec(...  13.4 us
    pallas_call x1, Pallas kernels, build(): pl.pallas_call(build_kernel, grid=(count // BLOCK // 2,), in_specs=[pl.Bl...  10.8 us
    all_to_all x1, starting transfers between devices, per_device(): moved = lax.all_to_all(shown, 'col', 0, 0, tiled=True)  10.8 us
    all_to_all x1, waiting for transfers between devices, per_device(): parts = lax.all_to_all(partial, 'row', 0, 0, tiled=True)  10.5 us
    all_to_all x1, starting transfers between devices, spread(): return lax.all_to_all(copies, axis, 0, 0, tiled=True)  10.1 us
    pallas_call x1, Pallas kernels, apply(): pl.pallas_call(apply_kernel, grid=(count // depth,), in_specs=[pl.BlockSp...  8.37 us
  transfers between devices with their start and end apart: 7, of which 7 were waited for; matrix products, arithmetic and copies ran while one was open for 2% of the time, Pallas kernels for 10%

profile of v7, /device:TPU:6, one launch (start us, length us, event | category | flops | bytes accessed | tf_op | source)
XLA Modules:
  0.0 148.0 jit_solution(13254235970207518995)
XLA Ops:
  0.6 0.7 constant_dynamic-slice_fusion
  1.3 0.6 broadcast_in_dim.6
  2.0 10.1 %all-to-all-start = ((f32[16,4,128]{2,1,0:T(4,128)}), f32[16,4,128]{2,1,0:T(4,128)S(1)}, u32[]{:S(2)}, u32[]{:S(2)}) async-start(f32[16,4,128]{2,1,0:T(4,128)} %broadcast_in_dim.6), calls=%async_computation | async-start | bytes 65536 | tf_op jit(solution)/shard_map/all_to_all | solution.py:28
  12.0 0.8 multiply_reduce_fusion
  12.8 0.7 multiply_subtract_fusion.base_ref
  13.5 3.3 %factors.1 = (bf16[4096,128]{1,0:T(8,128)(2,1)}, bf16[32,32,128]{2,1,0:T(8,128)(2,1)}) custom-call(f32[3,4096]{1,0:T(4,128)} %center_ref.1, f32[3,4096]{1,0:T(4,128)} %normal_ref.1, f32[1,4096]{1,0:T(1,128)} %bitcast.12, f32[32,128]{1,0:T(8,128)} %start_ref.3), custom_call_target="tpu_custom_call" | custom-call | flops 1638400 | bytes 1638400 | tf_op jit(solution)/shard_map/factors/pallas_call | solution.py:63
  16.8 3.3 %all-to-all-done = f32[16,4,128]{2,1,0:T(4,128)S(1)} async-done(((f32[16,4,128]{2,1,0:T(4,128)}), f32[16,4,128]{2,1,0:T(4,128)S(1)}, u32[]{:S(2)}, u32[]{:S(2)}) %all-to-all-start) | async-done | bytes 32800 | tf_op jit(solution)/shard_map/all_to_all | solution.py:28
  20.1 10.8 %all-to-all-start.1 = ((bf16[32,32,128]{2,1,0:T(8,128)(2,1)}), bf16[32,32,128]{2,1,0:T(8,128)(2,1)S(1)}, u32[]{:S(2)}, u32[]{:S(2)}) async-start(bf16[32,32,128]{2,1,0:T(8,128)(2,1)} %get-tuple-element.21), calls=%async_computation.1 | async-start | bytes 524288 | tf_op jit(solution)/shard_map/all_to_all | solution.py:463
  30.9 10.8 %build.1.old_ref = bf16[4096,2048]{1,0:T(8,128)(2,1)} custom-call(bf16[4096,128]{1,0:T(8,128)(2,1)} %get-tuple-element.19.factor_ref, f32[4,2048]{1,0:T(4,128)} %bitcast.9), custom_call_target="tpu_custom_call" | custom-call | flops 419430400 | bytes 8388608 | tf_op jit(solution)/shard_map/build/pallas_call | solution.py:213
  41.7 1.4 all-to-all-done.1.moved_ref
  43.1 0.0 copy-done
  43.1 0.8 copy-done.2
  43.9 13.4 %finish.1 = (bf16[4096,2048]{1,0:T(8,128)(2,1)}, f32[16,32,128]{2,1,0:T(8,128)S(1)}) custom-call(bf16[4096,128]{1,0:T(8,128)(2,1)S(1)} %copy-done, f32[4,2048]{1,0:T(4,128)S(1)} %bitcast.10, bf16[32,32,128]{2,1,0:T(8,128)(2,1)S(1)} %all-to-all-done.1.moved_ref, bf16[4096,2048]{1,0:T(8,128)(2,1)} %build.1.old_ref), custom_call_target="tpu_custom_call", output_to_operand_aliasing={{0}: (3, {})} | custom-call | tf_op jit(solution)/shard_map/finish/pallas_call | solution.py:239
  57.3 17.1 %all_to_all.35.part_ref = f32[16,32,128]{2,1,0:T(8,128)S(1)} all-to-all(f32[16,32,128]{2,1,0:T(8,128)S(1)} %get-tuple-element.22), channel_id=1, replica_groups=mesh['row'=16,'col'=32] {'row'}, dimensions={0} | all-to-all | bytes 524288 | tf_op jit(solution)/shard_map/all_to_all | solution.py:468
  74.4 19.4 %all_to_all.36.moved_ref = bf16[32,32,128]{2,1,0:T(8,128)(2,1)} all-to-all(bf16[32,32,128]{2,1,0:T(8,128)(2,1)S(1)} %get-tuple-element.24), channel_id=1, replica_groups=mesh['row'=16,'col'=32] {'col'}, dimensions={0} | all-to-all | bytes 524288 | tf_op jit(solution)/shard_map/all_to_all | solution.py:470
  93.8 8.4 %apply.1 = f32[16,32,128]{2,1,0:T(8,128)} custom-call(bf16[32,32,128]{2,1,0:T(8,128)(2,1)} %all_to_all.36.moved_ref, bf16[4096,2048]{1,0:T(8,128)(2,1)} %get-tuple-element.25.tile_ref), custom_call_target="tpu_custom_call" | custom-call | tf_op jit(solution)/shard_map/apply/pallas_call | solution.py:289
  102.2 5.8 %all-to-all-start.4 = ((f32[16,32,128]{2,1,0:T(8,128)}), f32[16,32,128]{2,1,0:T(8,128)S(1)}, u32[]{:S(2)}, u32[]{:S(2)}) async-start(f32[16,32,128]{2,1,0:T(8,128)} %apply.1), calls=%async_computation.4 | async-start | bytes 524288 | tf_op jit(solution)/shard_map/all_to_all | solution.py:472
  108.0 0.8 dynamic-slice_bitcast_fusion.area_ref
  108.7 10.5 %all-to-all-done.4.part_ref = f32[16,32,128]{2,1,0:T(8,128)S(1)} async-done(((f32[16,32,128]{2,1,0:T(8,128)}), f32[16,32,128]{2,1,0:T(8,128)S(1)}, u32[]{:S(2)}, u32[]{:S(2)}) %all-to-all-start.4) | async-done | bytes 262176 | tf_op jit(solution)/shard_map/all_to_all | solution.py:472
  119.3 0.7 sums.1
  120.0 3.8 %all-to-all-start.5 = ((f32[32,2,128]{2,1,0:T(2,128)}), f32[32,2,128]{2,1,0:T(2,128)S(1)}, u32[]{:S(2)}, u32[]{:S(2)}) async-start(f32[32,2,128]{2,1,0:T(2,128)} %get-tuple-element.27), calls=%async_computation.5 | async-start | bytes 65536 | tf_op jit(solution)/shard_map/all_to_all | solution.py:480
  123.9 2.1 %collective-permute-start = (f32[104,128]{1,0:T(8,128)S(1)}, f32[104,128]{1,0:T(8,128)S(1)}, u32[]{:S(2)}, u32[]{:S(2)}) collective-permute-start(f32[104,128]{1,0:T(8,128)S(1)} %get-tuple-element.31.field_ref), channel_id=1, source_target_pairs={{0,1},{1,2},{2,3},{3,4},{4,5},{5,6},{6,7},{7,8},{8,9},{9,10},{10,1... | collective-permute-start | bytes 159752 | tf_op jit(solution)/shard_map/ppermute | solution.py:481
  125.9 6.2 %all-to-all-done.5.part_ref = f32[32,2,128]{2,1,0:T(2,128)S(1)} async-done(((f32[32,2,128]{2,1,0:T(2,128)}), f32[32,2,128]{2,1,0:T(2,128)S(1)}, u32[]{:S(2)}, u32[]{:S(2)}) %all-to-all-start.5) | async-done | bytes 32800 | tf_op jit(solution)/shard_map/all_to_all | solution.py:480
  132.1 0.7 regroup.1
  132.8 0.7 collective-permute-done.before_ref
  133.5 5.0 %all-to-all-start.6 = ((f32[16,8,128]{2,1,0:T(8,128)}), f32[16,8,128]{2,1,0:T(8,128)S(1)}, u32[]{:S(2)}, u32[]{:S(2)}) async-start(f32[16,8,128]{2,1,0:T(8,128)} %regroup.1), calls=%async_computation.6 | async-start | bytes 131072 | tf_op jit(solution)/shard_map/all_to_all | solution.py:484
  138.6 4.5 %collective-permute-start.1 = (f32[104,128]{1,0:T(8,128)S(1)}, f32[104,128]{1,0:T(8,128)S(1)}, u32[]{:S(2)}, u32[]{:S(2)}) collective-permute-start(f32[104,128]{1,0:T(8,128)S(1)} %get-tuple-element.31.field_ref), channel_id=1, source_target_pairs={{1,0},{2,1},{3,2},{4,3},{5,4},{6,5},{7,6},{8,7},{9,8},{10,9},{11,1... | collective-permute-start | bytes 159752 | tf_op jit(solution)/shard_map/ppermute | solution.py:483
  143.1 0.1 add_convert_fusion.end_ref
  143.2 0.1 copy.10
  143.3 1.6 %collective-permute-done.1.after_ref = f32[104,128]{1,0:T(8,128)S(1)} collective-permute-done((f32[104,128]{1,0:T(8,128)S(1)}, f32[104,128]{1,0:T(8,128)S(1)}, u32[]{:S(2)}, u32[]{:S(2)}) %collective-permute-start.1) | collective-permute-done | bytes 53280 | tf_op jit(solution)/shard_map/ppermute | solution.py:483
  144.9 1.7 %all-to-all-done.6.part_ref = f32[16,8,128]{2,1,0:T(8,128)S(1)} async-done(((f32[16,8,128]{2,1,0:T(8,128)}), f32[16,8,128]{2,1,0:T(8,128)S(1)}, u32[]{:S(2)}, u32[]{:S(2)}) %all-to-all-start.6) | async-done | bytes 65568 | tf_op jit(solution)/shard_map/all_to_all | solution.py:484
  146.6 1.4 last.1
  (11 shorter events, 0.1 us)
Async XLA Ops:
  2.0 18.1 %all-to-all-start = ((f32[16,4,128]{2,1,0:T(4,128)}), f32[16,4,128]{2,1,0:T(4,128)S(1)}, u32[]{:S(2)}, u32[]{:S(2)}) async-start(f32[16,4,128]{2,1,0:T(4,128)} %broadcast_in_dim.6), calls=%async_computation | async-start | bytes 65536 | tf_op jit(solution)/shard_map/all_to_all | solution.py:28
  16.8 26.3 %copy-start = (bf16[4096,128]{1,0:T(8,128)(2,1)S(1)}, bf16[4096,128]{1,0:T(8,128)(2,1)}, u32[]{:S(2)}) copy-start(bf16[4096,128]{1,0:T(8,128)(2,1)} %get-tuple-element.19.factor_ref) | copy-start | bytes 3145732
  20.1 10.8 %copy-start.1 = (f32[16,4,128]{2,1,0:T(4,128)}, f32[16,4,128]{2,1,0:T(4,128)S(1)}, u32[]{:S(2)}) copy-start(f32[16,4,128]{2,1,0:T(4,128)S(1)} %all-to-all-done) | copy-start | bytes 98308
  20.1 23.0 %all-to-all-start.1 = ((bf16[32,32,128]{2,1,0:T(8,128)(2,1)}), bf16[32,32,128]{2,1,0:T(8,128)(2,1)S(1)}, u32[]{:S(2)}, u32[]{:S(2)}) async-start(bf16[32,32,128]{2,1,0:T(8,128)(2,1)} %get-tuple-element.21), calls=%async_computation.1 | async-start | bytes 524288 | tf_op jit(solution)/shard_map/all_to_all | solution.py:463
  43.1 0.8 copy-start.2
  43.9 75.4 %copy-start.3 = (f32[32,128]{1,0:T(8,128)S(1)}, f32[32,128]{1,0:T(8,128)}, u32[]{:S(2)}) copy-start(f32[32,128]{1,0:T(8,128)} %start_ref.3) | copy-start | bytes 49156
  43.9 99.3 %copy-start.4 = (f32[3,32]{1,0:T(4,128)S(1)}, f32[3,32]{1,0:T(4,128)}, u32[]{:S(2)}) copy-start(f32[3,32]{1,0:T(4,128)} %param.8) | copy-start | bytes 1156
  102.2 17.1 %all-to-all-start.4 = ((f32[16,32,128]{2,1,0:T(8,128)}), f32[16,32,128]{2,1,0:T(8,128)S(1)}, u32[]{:S(2)}, u32[]{:S(2)}) async-start(f32[16,32,128]{2,1,0:T(8,128)} %apply.1), calls=%async_computation.4 | async-start | bytes 524288 | tf_op jit(solution)/shard_map/all_to_all | solution.py:472
  120.0 12.1 %all-to-all-start.5 = ((f32[32,2,128]{2,1,0:T(2,128)}), f32[32,2,128]{2,1,0:T(2,128)S(1)}, u32[]{:S(2)}, u32[]{:S(2)}) async-start(f32[32,2,128]{2,1,0:T(2,128)} %get-tuple-element.27), calls=%async_computation.5 | async-start | bytes 65536 | tf_op jit(solution)/shard_map/all_to_all | solution.py:480
  123.9 9.7 %collective-permute-start = (f32[104,128]{1,0:T(8,128)S(1)}, f32[104,128]{1,0:T(8,128)S(1)}, u32[]{:S(2)}, u32[]{:S(2)}) collective-permute-start(f32[104,128]{1,0:T(8,128)S(1)} %get-tuple-element.31.field_ref), channel_id=1, source_target_pairs={{0,1},{1,2},{2,3},{3,4},{4,5},{5,6},{6,7},{7,8},{8,9},{9,10},{10,1... | collective-permute-start | bytes 159752 | tf_op jit(solution)/shard_map/ppermute | solution.py:481
  133.5 13.0 %all-to-all-start.6 = ((f32[16,8,128]{2,1,0:T(8,128)}), f32[16,8,128]{2,1,0:T(8,128)S(1)}, u32[]{:S(2)}, u32[]{:S(2)}) async-start(f32[16,8,128]{2,1,0:T(8,128)} %regroup.1), calls=%async_computation.6 | async-start | bytes 131072 | tf_op jit(solution)/shard_map/all_to_all | solution.py:484
  138.6 6.3 %collective-permute-start.1 = (f32[104,128]{1,0:T(8,128)S(1)}, f32[104,128]{1,0:T(8,128)S(1)}, u32[]{:S(2)}, u32[]{:S(2)}) collective-permute-start(f32[104,128]{1,0:T(8,128)S(1)} %get-tuple-element.31.field_ref), channel_id=1, source_target_pairs={{1,0},{2,1},{3,2},{4,3},{5,4},{6,5},{7,6},{8,7},{9,8},{10,9},{11,1... | collective-permute-start | bytes 159752 | tf_op jit(solution)/shard_map/ppermute | solution.py:483

commit v8 on v7

--- a/solution.py
+++ b/solution.py
@@ -462,6 +462,7 @@
     targets = jnp.transpose(notes, (1, 0, 2)).reshape(4, row_count * own)
     moved = lax.all_to_all(shown, "col", 0, 0, tiled=True)
 
+    targets = pltpu.with_memory_space_constraint(targets, pltpu.HBM)
     tile = build(factors, targets)
     tile, partial = finish_build(factors, targets, moved, tile)
 

time: 151 us -> 150 us (level)
  no operation moved by 1% of the time
where the time goes in v8:
time: 150 us; the launch traced here: 147 us
  starting transfers between devices  42.1 us (28%)
  Pallas kernels  38.8 us (26%)
  blocking collectives  36.6 us (24%)
  waiting for transfers between devices  25.4 us (17%)
  local copies, waits for them, and re-layouts  2.21 us (1%)
  other arithmetic  1.56 us (1%)
    all_to_all x1, blocking collectives, per_device(): gathered = lax.all_to_all(sent, 'col', 0, 0, tiled=True)  19.5 us
    all_to_all x1, blocking collectives, per_device(): parts = lax.all_to_all(partial, 'row', 0, 0, tiled=True)  17.1 us
    pallas_call x1, Pallas kernels, finish_build(): pl.pallas_call(finish_kernel, grid=(blocks + 1,), in_specs=[pl.BlockSpec(...  13.4 us
    pallas_call x1, Pallas kernels, build(): pl.pallas_call(build_kernel, grid=(count // BLOCK // 2,), in_specs=[pl.Bl...  10.8 us
    all_to_all x1, starting transfers between devices, per_device(): moved = lax.all_to_all(shown, 'col', 0, 0, tiled=True)  10.8 us
    all_to_all x1, waiting for transfers between devices, per_device(): parts = lax.all_to_all(partial, 'row', 0, 0, tiled=True)  10.5 us
    all_to_all x1, starting transfers between devices, spread(): return lax.all_to_all(copies, axis, 0, 0, tiled=True)  10.1 us
    pallas_call x1, Pallas kernels, apply(): pl.pallas_call(apply_kernel, grid=(count // depth,), in_specs=[pl.BlockSp...  8.36 us
  transfers between devices with their start and end apart: 7, of which 7 were waited for; matrix products, arithmetic and copies ran while one was open for 2% of the time, Pallas kernels for 10%

profile of v8, /device:TPU:6, one launch (start us, length us, event | category | flops | bytes accessed | tf_op | source)
XLA Modules:
  0.0 147.3 jit_solution(13130237033486407289)
XLA Ops:
  0.6 0.7 constant_dynamic-slice_fusion
  1.3 0.6 broadcast_in_dim.6
  2.0 10.1 %all-to-all-start = ((f32[16,4,128]{2,1,0:T(4,128)}), f32[16,4,128]{2,1,0:T(4,128)S(1)}, u32[]{:S(2)}, u32[]{:S(2)}) async-start(f32[16,4,128]{2,1,0:T(4,128)} %broadcast_in_dim.6), calls=%async_computation | async-start | bytes 65536 | tf_op jit(solution)/shard_map/all_to_all | solution.py:28
  12.0 0.8 multiply_reduce_fusion
  12.8 0.7 multiply_subtract_fusion.base_ref
  13.5 3.3 %factors.1 = (bf16[4096,128]{1,0:T(8,128)(2,1)}, bf16[32,32,128]{2,1,0:T(8,128)(2,1)}) custom-call(f32[3,4096]{1,0:T(4,128)} %center_ref.1, f32[3,4096]{1,0:T(4,128)} %normal_ref.1, f32[1,4096]{1,0:T(1,128)} %bitcast.12, f32[32,128]{1,0:T(8,128)} %start_ref.3), custom_call_target="tpu_custom_call" | custom-call | flops 1638400 | bytes 1638400 | tf_op jit(solution)/shard_map/factors/pallas_call | solution.py:63
  16.8 3.3 %all-to-all-done = f32[16,4,128]{2,1,0:T(4,128)S(1)} async-done(((f32[16,4,128]{2,1,0:T(4,128)}), f32[16,4,128]{2,1,0:T(4,128)S(1)}, u32[]{:S(2)}, u32[]{:S(2)}) %all-to-all-start) | async-done | bytes 32800 | tf_op jit(solution)/shard_map/all_to_all | solution.py:28
  20.1 10.8 %all-to-all-start.1 = ((bf16[32,32,128]{2,1,0:T(8,128)(2,1)}), bf16[32,32,128]{2,1,0:T(8,128)(2,1)S(1)}, u32[]{:S(2)}, u32[]{:S(2)}) async-start(bf16[32,32,128]{2,1,0:T(8,128)(2,1)} %get-tuple-element.21), calls=%async_computation.1 | async-start | bytes 524288 | tf_op jit(solution)/shard_map/all_to_all | solution.py:463
  30.9 0.0 copy-done.2
  30.9 10.8 %build.1.old_ref = bf16[4096,2048]{1,0:T(8,128)(2,1)} custom-call(bf16[4096,128]{1,0:T(8,128)(2,1)} %get-tuple-element.19.factor_ref, f32[4,2048]{1,0:T(4,128)} %bitcast.10), custom_call_target="tpu_custom_call" | custom-call | flops 419430400 | bytes 8388608 | tf_op jit(solution)/shard_map/build/pallas_call | solution.py:213
  41.7 1.3 all-to-all-done.1.moved_ref
  43.1 0.0 copy-done
  43.1 13.4 %finish.1 = (bf16[4096,2048]{1,0:T(8,128)(2,1)}, f32[16,32,128]{2,1,0:T(8,128)S(1)}) custom-call(bf16[4096,128]{1,0:T(8,128)(2,1)S(1)} %copy-done, f32[4,2048]{1,0:T(4,128)} %bitcast.11, bf16[32,32,128]{2,1,0:T(8,128)(2,1)S(1)} %all-to-all-done.1.moved_ref, bf16[4096,2048]{1,0:T(8,128)(2,1)} %build.1.old_ref), custom_call_target="tpu_custom_call", output_to_operand_aliasing={{0}: (3, {})} | custom-call | tf_op jit(solution)/shard_map/finish/pallas_call | solution.py:239
  56.5 17.1 %all_to_all.35.part_ref = f32[16,32,128]{2,1,0:T(8,128)S(1)} all-to-all(f32[16,32,128]{2,1,0:T(8,128)S(1)} %get-tuple-element.22), channel_id=1, replica_groups=mesh['row'=16,'col'=32] {'row'}, dimensions={0} | all-to-all | bytes 524288 | tf_op jit(solution)/shard_map/all_to_all | solution.py:469
  73.7 19.5 %all_to_all.36.moved_ref = bf16[32,32,128]{2,1,0:T(8,128)(2,1)} all-to-all(bf16[32,32,128]{2,1,0:T(8,128)(2,1)S(1)} %get-tuple-element.24), channel_id=1, replica_groups=mesh['row'=16,'col'=32] {'col'}, dimensions={0} | all-to-all | bytes 524288 | tf_op jit(solution)/shard_map/all_to_all | solution.py:471
  93.2 8.4 %apply.1 = f32[16,32,128]{2,1,0:T(8,128)} custom-call(bf16[32,32,128]{2,1,0:T(8,128)(2,1)} %all_to_all.36.moved_ref, bf16[4096,2048]{1,0:T(8,128)(2,1)} %get-tuple-element.25.tile_ref), custom_call_target="tpu_custom_call" | custom-call | tf_op jit(solution)/shard_map/apply/pallas_call | solution.py:289
  101.5 5.8 %all-to-all-start.4 = ((f32[16,32,128]{2,1,0:T(8,128)}), f32[16,32,128]{2,1,0:T(8,128)S(1)}, u32[]{:S(2)}, u32[]{:S(2)}) async-start(f32[16,32,128]{2,1,0:T(8,128)} %apply.1), calls=%async_computation.4 | async-start | bytes 524288 | tf_op jit(solution)/shard_map/all_to_all | solution.py:473
  107.3 0.8 dynamic-slice_bitcast_fusion.area_ref
  108.1 10.5 %all-to-all-done.4.part_ref = f32[16,32,128]{2,1,0:T(8,128)S(1)} async-done(((f32[16,32,128]{2,1,0:T(8,128)}), f32[16,32,128]{2,1,0:T(8,128)S(1)}, u32[]{:S(2)}, u32[]{:S(2)}) %all-to-all-start.4) | async-done | bytes 262176 | tf_op jit(solution)/shard_map/all_to_all | solution.py:473
  118.6 0.7 sums.1
  119.3 3.8 %all-to-all-start.5 = ((f32[32,2,128]{2,1,0:T(2,128)}), f32[32,2,128]{2,1,0:T(2,128)S(1)}, u32[]{:S(2)}, u32[]{:S(2)}) async-start(f32[32,2,128]{2,1,0:T(2,128)} %get-tuple-element.27), calls=%async_computation.5 | async-start | bytes 65536 | tf_op jit(solution)/shard_map/all_to_all | solution.py:481
  123.2 2.1 %collective-permute-start = (f32[104,128]{1,0:T(8,128)S(1)}, f32[104,128]{1,0:T(8,128)S(1)}, u32[]{:S(2)}, u32[]{:S(2)}) collective-permute-start(f32[104,128]{1,0:T(8,128)S(1)} %get-tuple-element.31.field_ref), channel_id=1, source_target_pairs={{0,1},{1,2},{2,3},{3,4},{4,5},{5,6},{6,7},{7,8},{8,9},{9,10},{10,1... | collective-permute-start | bytes 159752 | tf_op jit(solution)/shard_map/ppermute | solution.py:482
  125.3 6.2 %all-to-all-done.5.part_ref = f32[32,2,128]{2,1,0:T(2,128)S(1)} async-done(((f32[32,2,128]{2,1,0:T(2,128)}), f32[32,2,128]{2,1,0:T(2,128)S(1)}, u32[]{:S(2)}, u32[]{:S(2)}) %all-to-all-start.5) | async-done | bytes 32800 | tf_op jit(solution)/shard_map/all_to_all | solution.py:481
  131.5 0.7 regroup.1
  132.1 0.7 collective-permute-done.before_ref
  132.9 5.0 %all-to-all-start.6 = ((f32[16,8,128]{2,1,0:T(8,128)}), f32[16,8,128]{2,1,0:T(8,128)S(1)}, u32[]{:S(2)}, u32[]{:S(2)}) async-start(f32[16,8,128]{2,1,0:T(8,128)} %regroup.1), calls=%async_computation.6 | async-start | bytes 131072 | tf_op jit(solution)/shard_map/all_to_all | solution.py:485
  137.9 4.5 %collective-permute-start.1 = (f32[104,128]{1,0:T(8,128)S(1)}, f32[104,128]{1,0:T(8,128)S(1)}, u32[]{:S(2)}, u32[]{:S(2)}) collective-permute-start(f32[104,128]{1,0:T(8,128)S(1)} %get-tuple-element.31.field_ref), channel_id=1, source_target_pairs={{1,0},{2,1},{3,2},{4,3},{5,4},{6,5},{7,6},{8,7},{9,8},{10,9},{11,1... | collective-permute-start | bytes 159752 | tf_op jit(solution)/shard_map/ppermute | solution.py:484
  142.4 0.1 add_convert_fusion.end_ref
  142.5 0.1 copy.10
  142.6 1.6 %collective-permute-done.1.after_ref = f32[104,128]{1,0:T(8,128)S(1)} collective-permute-done((f32[104,128]{1,0:T(8,128)S(1)}, f32[104,128]{1,0:T(8,128)S(1)}, u32[]{:S(2)}, u32[]{:S(2)}) %collective-permute-start.1) | collective-permute-done | bytes 53280 | tf_op jit(solution)/shard_map/ppermute | solution.py:484
  144.2 1.7 %all-to-all-done.6.part_ref = f32[16,8,128]{2,1,0:T(8,128)S(1)} async-done(((f32[16,8,128]{2,1,0:T(8,128)}), f32[16,8,128]{2,1,0:T(8,128)S(1)}, u32[]{:S(2)}, u32[]{:S(2)}) %all-to-all-start.6) | async-done | bytes 65568 | tf_op jit(solution)/shard_map/all_to_all | solution.py:485
  145.9 1.4 last.1
  (9 shorter events, 0.1 us)
Async XLA Ops:
  2.0 18.1 %all-to-all-start = ((f32[16,4,128]{2,1,0:T(4,128)}), f32[16,4,128]{2,1,0:T(4,128)S(1)}, u32[]{:S(2)}, u32[]{:S(2)}) async-start(f32[16,4,128]{2,1,0:T(4,128)} %broadcast_in_dim.6), calls=%async_computation | async-start | bytes 65536 | tf_op jit(solution)/shard_map/all_to_all | solution.py:28
  16.8 26.3 %copy-start = (bf16[4096,128]{1,0:T(8,128)(2,1)S(1)}, bf16[4096,128]{1,0:T(8,128)(2,1)}, u32[]{:S(2)}) copy-start(bf16[4096,128]{1,0:T(8,128)(2,1)} %get-tuple-element.19.factor_ref) | copy-start | bytes 3145732
  20.1 10.8 %copy-start.2 = (f32[16,4,128]{2,1,0:T(4,128)}, f32[16,4,128]{2,1,0:T(4,128)S(1)}, u32[]{:S(2)}) copy-start(f32[16,4,128]{2,1,0:T(4,128)S(1)} %all-to-all-done) | copy-start | bytes 98308
  20.1 23.0 %all-to-all-start.1 = ((bf16[32,32,128]{2,1,0:T(8,128)(2,1)}), bf16[32,32,128]{2,1,0:T(8,128)(2,1)S(1)}, u32[]{:S(2)}, u32[]{:S(2)}) async-start(bf16[32,32,128]{2,1,0:T(8,128)(2,1)} %get-tuple-element.21), calls=%async_computation.1 | async-start | bytes 524288 | tf_op jit(solution)/shard_map/all_to_all | solution.py:463
  41.7 76.8 %copy-start.1 = (f32[32,128]{1,0:T(8,128)S(1)}, f32[32,128]{1,0:T(8,128)}, u32[]{:S(2)}) copy-start(f32[32,128]{1,0:T(8,128)} %start_ref.3) | copy-start | bytes 49156
  41.7 100.8 %copy-start.3 = (f32[3,32]{1,0:T(4,128)S(1)}, f32[3,32]{1,0:T(4,128)}, u32[]{:S(2)}) copy-start(f32[3,32]{1,0:T(4,128)} %param.8) | copy-start | bytes 1156
  101.5 17.1 %all-to-all-start.4 = ((f32[16,32,128]{2,1,0:T(8,128)}), f32[16,32,128]{2,1,0:T(8,128)S(1)}, u32[]{:S(2)}, u32[]{:S(2)}) async-start(f32[16,32,128]{2,1,0:T(8,128)} %apply.1), calls=%async_computation.4 | async-start | bytes 524288 | tf_op jit(solution)/shard_map/all_to_all | solution.py:473
  119.3 12.1 %all-to-all-start.5 = ((f32[32,2,128]{2,1,0:T(2,128)}), f32[32,2,128]{2,1,0:T(2,128)S(1)}, u32[]{:S(2)}, u32[]{:S(2)}) async-start(f32[32,2,128]{2,1,0:T(2,128)} %get-tuple-element.27), calls=%async_computation.5 | async-start | bytes 65536 | tf_op jit(solution)/shard_map/all_to_all | solution.py:481
  123.2 9.7 %collective-permute-start = (f32[104,128]{1,0:T(8,128)S(1)}, f32[104,128]{1,0:T(8,128)S(1)}, u32[]{:S(2)}, u32[]{:S(2)}) collective-permute-start(f32[104,128]{1,0:T(8,128)S(1)} %get-tuple-element.31.field_ref), channel_id=1, source_target_pairs={{0,1},{1,2},{2,3},{3,4},{4,5},{5,6},{6,7},{7,8},{8,9},{9,10},{10,1... | collective-permute-start | bytes 159752 | tf_op jit(solution)/shard_map/ppermute | solution.py:482
  132.9 13.1 %all-to-all-start.6 = ((f32[16,8,128]{2,1,0:T(8,128)}), f32[16,8,128]{2,1,0:T(8,128)S(1)}, u32[]{:S(2)}, u32[]{:S(2)}) async-start(f32[16,8,128]{2,1,0:T(8,128)} %regroup.1), calls=%async_computation.6 | async-start | bytes 131072 | tf_op jit(solution)/shard_map/all_to_all | solution.py:485
  137.9 6.3 %collective-permute-start.1 = (f32[104,128]{1,0:T(8,128)S(1)}, f32[104,128]{1,0:T(8,128)S(1)}, u32[]{:S(2)}, u32[]{:S(2)}) collective-permute-start(f32[104,128]{1,0:T(8,128)S(1)} %get-tuple-element.31.field_ref), channel_id=1, source_target_pairs={{1,0},{2,1},{3,2},{4,3},{5,4},{6,5},{7,6},{8,7},{9,8},{10,9},{11,1... | collective-permute-start | bytes 159752 | tf_op jit(solution)/shard_map/ppermute | solution.py:484

commit v9 on v8

--- a/solution.py
+++ b/solution.py
@@ -283,7 +283,7 @@
             product_ref[chunk] += product[:, chunk * LANES : (chunk + 1) * LANES]
 
 
-def apply(moved, tile, depth=1024):
+def apply(moved, tile, depth=2048):
     count, width = tile.shape
     onsets = moved.shape[1]
     return pl.pallas_call(

time: 150 us -> 150 us (level)
  no operation moved by 1% of the time
where the time goes in v9:
time: 150 us; the launch traced here: 147 us
  starting transfers between devices  42.1 us (28%)
  Pallas kernels  38.6 us (26%)
  blocking collectives  36.6 us (24%)
  waiting for transfers between devices  25.4 us (17%)
  local copies, waits for them, and re-layouts  2.21 us (1%)
  other arithmetic  1.56 us (1%)
    all_to_all x1, blocking collectives, per_device(): gathered = lax.all_to_all(sent, 'col', 0, 0, tiled=True)  19.5 us
    all_to_all x1, blocking collectives, per_device(): parts = lax.all_to_all(partial, 'row', 0, 0, tiled=True)  17.1 us
    pallas_call x1, Pallas kernels, finish_build(): pl.pallas_call(finish_kernel, grid=(blocks + 1,), in_specs=[pl.BlockSpec(...  13.4 us
    pallas_call x1, Pallas kernels, build(): pl.pallas_call(build_kernel, grid=(count // BLOCK // 2,), in_specs=[pl.Bl...  10.8 us
    all_to_all x1, starting transfers between devices, per_device(): moved = lax.all_to_all(shown, 'col', 0, 0, tiled=True)  10.8 us
    all_to_all x1, waiting for transfers between devices, per_device(): parts = lax.all_to_all(partial, 'row', 0, 0, tiled=True)  10.5 us
    all_to_all x1, starting transfers between devices, spread(): return lax.all_to_all(copies, axis, 0, 0, tiled=True)  10.1 us
    pallas_call x1, Pallas kernels, apply(): pl.pallas_call(apply_kernel, grid=(count // depth,), in_specs=[pl.BlockSp...  8.14 us
  transfers between devices with their start and end apart: 7, of which 7 were waited for; matrix products, arithmetic and copies ran while one was open for 2% of the time, Pallas kernels for 10%

profile of v9, /device:TPU:6, one launch (start us, length us, event | category | flops | bytes accessed | tf_op | source)
XLA Modules:
  0.0 147.1 jit_solution(2613820265928572297)
XLA Ops:
  0.6 0.7 constant_dynamic-slice_fusion
  1.3 0.6 broadcast_in_dim.6
  2.0 10.1 %all-to-all-start = ((f32[16,4,128]{2,1,0:T(4,128)}), f32[16,4,128]{2,1,0:T(4,128)S(1)}, u32[]{:S(2)}, u32[]{:S(2)}) async-start(f32[16,4,128]{2,1,0:T(4,128)} %broadcast_in_dim.6), calls=%async_computation | async-start | bytes 65536 | tf_op jit(solution)/shard_map/all_to_all | solution.py:28
  12.0 0.8 multiply_reduce_fusion
  12.8 0.7 multiply_subtract_fusion.base_ref
  13.5 3.3 %factors.1 = (bf16[4096,128]{1,0:T(8,128)(2,1)}, bf16[32,32,128]{2,1,0:T(8,128)(2,1)}) custom-call(f32[3,4096]{1,0:T(4,128)} %center_ref.1, f32[3,4096]{1,0:T(4,128)} %normal_ref.1, f32[1,4096]{1,0:T(1,128)} %bitcast.12, f32[32,128]{1,0:T(8,128)} %start_ref.3), custom_call_target="tpu_custom_call" | custom-call | flops 1638400 | bytes 1638400 | tf_op jit(solution)/shard_map/factors/pallas_call | solution.py:63
  16.8 3.3 %all-to-all-done = f32[16,4,128]{2,1,0:T(4,128)S(1)} async-done(((f32[16,4,128]{2,1,0:T(4,128)}), f32[16,4,128]{2,1,0:T(4,128)S(1)}, u32[]{:S(2)}, u32[]{:S(2)}) %all-to-all-start) | async-done | bytes 32800 | tf_op jit(solution)/shard_map/all_to_all | solution.py:28
  20.1 10.8 %all-to-all-start.1 = ((bf16[32,32,128]{2,1,0:T(8,128)(2,1)}), bf16[32,32,128]{2,1,0:T(8,128)(2,1)S(1)}, u32[]{:S(2)}, u32[]{:S(2)}) async-start(bf16[32,32,128]{2,1,0:T(8,128)(2,1)} %get-tuple-element.21), calls=%async_computation.1 | async-start | bytes 524288 | tf_op jit(solution)/shard_map/all_to_all | solution.py:463
  30.9 10.8 %build.1.old_ref = bf16[4096,2048]{1,0:T(8,128)(2,1)} custom-call(bf16[4096,128]{1,0:T(8,128)(2,1)} %get-tuple-element.19.factor_ref, f32[4,2048]{1,0:T(4,128)} %bitcast.10), custom_call_target="tpu_custom_call" | custom-call | flops 419430400 | bytes 8388608 | tf_op jit(solution)/shard_map/build/pallas_call | solution.py:213
  41.7 1.3 all-to-all-done.1.moved_ref
  43.1 0.0 copy-done
  43.1 13.4 %finish.1 = (bf16[4096,2048]{1,0:T(8,128)(2,1)}, f32[16,32,128]{2,1,0:T(8,128)S(1)}) custom-call(bf16[4096,128]{1,0:T(8,128)(2,1)S(1)} %copy-done, f32[4,2048]{1,0:T(4,128)} %bitcast.11, bf16[32,32,128]{2,1,0:T(8,128)(2,1)S(1)} %all-to-all-done.1.moved_ref, bf16[4096,2048]{1,0:T(8,128)(2,1)} %build.1.old_ref), custom_call_target="tpu_custom_call", output_to_operand_aliasing={{0}: (3, {})} | custom-call | tf_op jit(solution)/shard_map/finish/pallas_call | solution.py:239
  56.5 17.1 %all_to_all.35.part_ref = f32[16,32,128]{2,1,0:T(8,128)S(1)} all-to-all(f32[16,32,128]{2,1,0:T(8,128)S(1)} %get-tuple-element.22), channel_id=1, replica_groups=mesh['row'=16,'col'=32] {'row'}, dimensions={0} | all-to-all | bytes 524288 | tf_op jit(solution)/shard_map/all_to_all | solution.py:469
  73.7 19.5 %all_to_all.36.moved_ref = bf16[32,32,128]{2,1,0:T(8,128)(2,1)} all-to-all(bf16[32,32,128]{2,1,0:T(8,128)(2,1)S(1)} %get-tuple-element.24), channel_id=1, replica_groups=mesh['row'=16,'col'=32] {'col'}, dimensions={0} | all-to-all | bytes 524288 | tf_op jit(solution)/shard_map/all_to_all | solution.py:471
  93.2 8.1 %apply.1 = f32[16,32,128]{2,1,0:T(8,128)} custom-call(bf16[32,32,128]{2,1,0:T(8,128)(2,1)} %all_to_all.36.moved_ref, bf16[4096,2048]{1,0:T(8,128)(2,1)} %get-tuple-element.25.tile_ref), custom_call_target="tpu_custom_call" | custom-call | tf_op jit(solution)/shard_map/apply/pallas_call | solution.py:289
  101.3 5.8 %all-to-all-start.4 = ((f32[16,32,128]{2,1,0:T(8,128)}), f32[16,32,128]{2,1,0:T(8,128)S(1)}, u32[]{:S(2)}, u32[]{:S(2)}) async-start(f32[16,32,128]{2,1,0:T(8,128)} %apply.1), calls=%async_computation.4 | async-start | bytes 524288 | tf_op jit(solution)/shard_map/all_to_all | solution.py:473
  107.1 0.8 dynamic-slice_bitcast_fusion.area_ref
  107.8 10.5 %all-to-all-done.4.part_ref = f32[16,32,128]{2,1,0:T(8,128)S(1)} async-done(((f32[16,32,128]{2,1,0:T(8,128)}), f32[16,32,128]{2,1,0:T(8,128)S(1)}, u32[]{:S(2)}, u32[]{:S(2)}) %all-to-all-start.4) | async-done | bytes 262176 | tf_op jit(solution)/shard_map/all_to_all | solution.py:473
  118.4 0.7 sums.1
  119.1 3.8 %all-to-all-start.5 = ((f32[32,2,128]{2,1,0:T(2,128)}), f32[32,2,128]{2,1,0:T(2,128)S(1)}, u32[]{:S(2)}, u32[]{:S(2)}) async-start(f32[32,2,128]{2,1,0:T(2,128)} %get-tuple-element.27), calls=%async_computation.5 | async-start | bytes 65536 | tf_op jit(solution)/shard_map/all_to_all | solution.py:481
  123.0 2.1 %collective-permute-start = (f32[104,128]{1,0:T(8,128)S(1)}, f32[104,128]{1,0:T(8,128)S(1)}, u32[]{:S(2)}, u32[]{:S(2)}) collective-permute-start(f32[104,128]{1,0:T(8,128)S(1)} %get-tuple-element.31.field_ref), channel_id=1, source_target_pairs={{0,1},{1,2},{2,3},{3,4},{4,5},{5,6},{6,7},{7,8},{8,9},{9,10},{10,1... | collective-permute-start | bytes 159752 | tf_op jit(solution)/shard_map/ppermute | solution.py:482
  125.0 6.2 %all-to-all-done.5.part_ref = f32[32,2,128]{2,1,0:T(2,128)S(1)} async-done(((f32[32,2,128]{2,1,0:T(2,128)}), f32[32,2,128]{2,1,0:T(2,128)S(1)}, u32[]{:S(2)}, u32[]{:S(2)}) %all-to-all-start.5) | async-done | bytes 32800 | tf_op jit(solution)/shard_map/all_to_all | solution.py:481
  131.2 0.7 regroup.1
  131.9 0.7 collective-permute-done.before_ref
  132.6 5.0 %all-to-all-start.6 = ((f32[16,8,128]{2,1,0:T(8,128)}), f32[16,8,128]{2,1,0:T(8,128)S(1)}, u32[]{:S(2)}, u32[]{:S(2)}) async-start(f32[16,8,128]{2,1,0:T(8,128)} %regroup.1), calls=%async_computation.6 | async-start | bytes 131072 | tf_op jit(solution)/shard_map/all_to_all | solution.py:485
  137.7 4.5 %collective-permute-start.1 = (f32[104,128]{1,0:T(8,128)S(1)}, f32[104,128]{1,0:T(8,128)S(1)}, u32[]{:S(2)}, u32[]{:S(2)}) collective-permute-start(f32[104,128]{1,0:T(8,128)S(1)} %get-tuple-element.31.field_ref), channel_id=1, source_target_pairs={{1,0},{2,1},{3,2},{4,3},{5,4},{6,5},{7,6},{8,7},{9,8},{10,9},{11,1... | collective-permute-start | bytes 159752 | tf_op jit(solution)/shard_map/ppermute | solution.py:484
  142.2 0.1 add_convert_fusion.end_ref
  142.3 0.0 copy-done.3
  142.3 0.1 copy.10
  142.4 1.6 %collective-permute-done.1.after_ref = f32[104,128]{1,0:T(8,128)S(1)} collective-permute-done((f32[104,128]{1,0:T(8,128)S(1)}, f32[104,128]{1,0:T(8,128)S(1)}, u32[]{:S(2)}, u32[]{:S(2)}) %collective-permute-start.1) | collective-permute-done | bytes 53280 | tf_op jit(solution)/shard_map/ppermute | solution.py:484
  144.0 1.7 %all-to-all-done.6.part_ref = f32[16,8,128]{2,1,0:T(8,128)S(1)} async-done(((f32[16,8,128]{2,1,0:T(8,128)}), f32[16,8,128]{2,1,0:T(8,128)S(1)}, u32[]{:S(2)}, u32[]{:S(2)}) %all-to-all-start.6) | async-done | bytes 65568 | tf_op jit(solution)/shard_map/all_to_all | solution.py:485
  145.7 1.4 last.1
  (9 shorter events, 0.1 us)
Async XLA Ops:
  2.0 18.1 %all-to-all-start = ((f32[16,4,128]{2,1,0:T(4,128)}), f32[16,4,128]{2,1,0:T(4,128)S(1)}, u32[]{:S(2)}, u32[]{:S(2)}) async-start(f32[16,4,128]{2,1,0:T(4,128)} %broadcast_in_dim.6), calls=%async_computation | async-start | bytes 65536 | tf_op jit(solution)/shard_map/all_to_all | solution.py:28
  16.8 26.3 %copy-start = (bf16[4096,128]{1,0:T(8,128)(2,1)S(1)}, bf16[4096,128]{1,0:T(8,128)(2,1)}, u32[]{:S(2)}) copy-start(bf16[4096,128]{1,0:T(8,128)(2,1)} %get-tuple-element.19.factor_ref) | copy-start | bytes 3145732
  20.1 10.8 %copy-start.2 = (f32[16,4,128]{2,1,0:T(4,128)}, f32[16,4,128]{2,1,0:T(4,128)S(1)}, u32[]{:S(2)}) copy-start(f32[16,4,128]{2,1,0:T(4,128)S(1)} %all-to-all-done) | copy-start | bytes 98308
  20.1 23.0 %all-to-all-start.1 = ((bf16[32,32,128]{2,1,0:T(8,128)(2,1)}), bf16[32,32,128]{2,1,0:T(8,128)(2,1)S(1)}, u32[]{:S(2)}, u32[]{:S(2)}) async-start(bf16[32,32,128]{2,1,0:T(8,128)(2,1)} %get-tuple-element.21), calls=%async_computation.1 | async-start | bytes 524288 | tf_op jit(solution)/shard_map/all_to_all | solution.py:463
  41.7 76.6 %copy-start.1 = (f32[32,128]{1,0:T(8,128)S(1)}, f32[32,128]{1,0:T(8,128)}, u32[]{:S(2)}) copy-start(f32[32,128]{1,0:T(8,128)} %start_ref.3) | copy-start | bytes 49156
  41.7 100.5 %copy-start.3 = (f32[3,32]{1,0:T(4,128)S(1)}, f32[3,32]{1,0:T(4,128)}, u32[]{:S(2)}) copy-start(f32[3,32]{1,0:T(4,128)} %param.8) | copy-start | bytes 1156
  101.3 17.1 %all-to-all-start.4 = ((f32[16,32,128]{2,1,0:T(8,128)}), f32[16,32,128]{2,1,0:T(8,128)S(1)}, u32[]{:S(2)}, u32[]{:S(2)}) async-start(f32[16,32,128]{2,1,0:T(8,128)} %apply.1), calls=%async_computation.4 | async-start | bytes 524288 | tf_op jit(solution)/shard_map/all_to_all | solution.py:473
  119.1 12.1 %all-to-all-start.5 = ((f32[32,2,128]{2,1,0:T(2,128)}), f32[32,2,128]{2,1,0:T(2,128)S(1)}, u32[]{:S(2)}, u32[]{:S(2)}) async-start(f32[32,2,128]{2,1,0:T(2,128)} %get-tuple-element.27), calls=%async_computation.5 | async-start | bytes 65536 | tf_op jit(solution)/shard_map/all_to_all | solution.py:481
  123.0 9.7 %collective-permute-start = (f32[104,128]{1,0:T(8,128)S(1)}, f32[104,128]{1,0:T(8,128)S(1)}, u32[]{:S(2)}, u32[]{:S(2)}) collective-permute-start(f32[104,128]{1,0:T(8,128)S(1)} %get-tuple-element.31.field_ref), channel_id=1, source_target_pairs={{0,1},{1,2},{2,3},{3,4},{4,5},{5,6},{6,7},{7,8},{8,9},{9,10},{10,1... | collective-permute-start | bytes 159752 | tf_op jit(solution)/shard_map/ppermute | solution.py:482
  132.6 13.1 %all-to-all-start.6 = ((f32[16,8,128]{2,1,0:T(8,128)}), f32[16,8,128]{2,1,0:T(8,128)S(1)}, u32[]{:S(2)}, u32[]{:S(2)}) async-start(f32[16,8,128]{2,1,0:T(8,128)} %regroup.1), calls=%async_computation.6 | async-start | bytes 131072 | tf_op jit(solution)/shard_map/all_to_all | solution.py:485
  137.7 6.3 %collective-permute-start.1 = (f32[104,128]{1,0:T(8,128)S(1)}, f32[104,128]{1,0:T(8,128)S(1)}, u32[]{:S(2)}, u32[]{:S(2)}) collective-permute-start(f32[104,128]{1,0:T(8,128)S(1)} %get-tuple-element.31.field_ref), channel_id=1, source_target_pairs={{1,0},{2,1},{3,2},{4,3},{5,4},{6,5},{7,6},{8,7},{9,8},{10,9},{11,1... | collective-permute-start | bytes 159752 | tf_op jit(solution)/shard_map/ppermute | solution.py:484
